TPU v7x, 32 devices: a whole 2x2x4 slice. The times are simulated.
32 devices in a mesh: batch: 4 (over y, core), wide: 8 (over z, x).
Axes of the slice: x: 2, y: 2, z: 4, core: 2. Of those that a mesh axis runs over, the one named last changes fastest.
Arguments:
- inputs: bfloat16 [32, 512, 768], P(('batch', 'wide')), may hold values from -6 to 6
- lengths: int32 [32], P(('batch', 'wide')), may hold values from 1 to 512, 6553 in all
- cotangent: bfloat16 [32, 512, 768], P(('batch', 'wide')), may hold values from -6 to 6
- w_qkv: bfloat16 [768, 2304], P(('batch', 'wide')), may hold values from -0.21875 to 0.21875
- w_out: bfloat16 [768, 768], P(('batch', 'wide')), may hold values from -3.5 to 3.5
- conv_taps: bfloat16 [2304, 3], P(('batch', 'wide')), may hold values from -3.5 to 3.5
- gain_one: bfloat16 [768], P(('batch', 'wide')), may hold values from 0.099609375 to 1.8984375
- gain_two: bfloat16 [768], P(('batch', 'wide')), may hold values from 0.099609375 to 1.8984375
- w_in: bfloat16 [768, 3072], P(None, 'wide'), may hold values from -0.21875 to 0.21875
- w_fc2: bfloat16 [3072, 768], P('wide'), may hold values from -0.109375 to 0.109375
Outputs:
- output: bfloat16 [32, 512, 768], P(('batch', 'wide'))
- grad_inputs: bfloat16 [32, 512, 768], P(('batch', 'wide'))
- grad_w_qkv: float32 [768, 2304], P(('batch', 'wide'))
- grad_w_out: float32 [768, 768], P(('batch', 'wide'))
- grad_conv_taps: float32 [2304, 3], P(('batch', 'wide'))
- grad_gain_one: float32 [768], P(('batch', 'wide'))
- grad_gain_two: float32 [768], P(('batch', 'wide'))
- grad_w_in: float32 [768, 3072], P('batch', 'wide')
- grad_w_fc2: float32 [3072, 768], P('wide', 'batch')
Inputs may be any that keep to these rules, and one draw needn't show every extreme that they name: lengths[s] is the number of real tokens of sequence s; the longest has exactly 512.
All inputs are finite; a program needn't handle non-finite values. No bound on the sum of `lengths` on one device may be relied on, other than what follows from the above.
Results may differ from a plain program's by a relative error of at most 0.017.
Values may be sent and summed in bfloat16 or wider, within the bound.
No kernel may reach another device: no remote copies, remote signals or barrier semaphores. Data moves between devices by JAX's collectives and lax.ppermute only.
A program may use at most 256 MiB of HBM per device.

v0:
```python
import functools
import jax
import jax.numpy as jnp
from jax import lax
from jax.experimental import pallas as pl
from jax.experimental.pallas import tpu as pltpu
from jax.sharding import PartitionSpec as P

HEADS = 12
HD = 64


epsilon = 1e-05


def contract_first(left, right):
    return lax.dot_general(
        left, right, (((0,), (0,)), ((), ())), preferred_element_type=jnp.float32
    )


def contract_last(left, right):
    return lax.dot_general(
        left, right, (((1,), (1,)), ((), ())), preferred_element_type=jnp.float32
    )


def norm_parts(values_in):
    centered = values_in - jnp.mean(values_in, axis=-1, keepdims=True)
    inv_std = lax.rsqrt(jnp.mean(centered * centered, axis=-1, keepdims=True) + epsilon)
    return (centered * inv_std, inv_std)


def norm_back(grad_normed, gain_vec, normed_hat, inv_std):
    grad_hat = grad_normed * gain_vec
    mean_first = jnp.mean(grad_hat, axis=-1, keepdims=True)
    mean_second = jnp.mean(grad_hat * normed_hat, axis=-1, keepdims=True)
    grad_value = inv_std * (grad_hat - mean_first - normed_hat * mean_second)
    return (grad_value, jnp.sum(grad_normed * normed_hat, axis=0))


def shift_down(signal, steps):
    filler = jnp.zeros((steps, signal.shape[1]), signal.dtype)
    return jnp.concatenate([filler, signal[:-steps]], axis=0)


def shift_up(signal, steps):
    filler = jnp.zeros((steps, signal.shape[1]), signal.dtype)
    return jnp.concatenate([signal[steps:], filler], axis=0)


def scores_block(query_block, keys, start_row, seq_live):
    rows_block = query_block.shape[0]
    scores = (
        jnp.einsum("qhd,khd->hqk", query_block, keys, preferred_element_type=jnp.float32) * 0.125
    )
    query_pos = start_row + jnp.arange(rows_block)
    key_pos = jnp.arange(keys.shape[0])
    allowed = (key_pos[None, :] <= query_pos[:, None]) & (key_pos[None, :] < seq_live)
    return (scores, allowed[None])


def shards(inputs, lengths, cotangent, w_qkv, w_out, conv_taps, gain_one, gain_two, w_in, w_fc2):
    full_qkv, full_out, full_taps, full_gain_one, full_gain_two = (
        lax.all_gather(w_qkv, ("batch", "wide"), axis=0, tiled=True),
        lax.all_gather(w_out, ("batch", "wide"), axis=0, tiled=True),
        lax.all_gather(conv_taps, ("batch", "wide"), axis=0, tiled=True),
        lax.all_gather(gain_one, ("batch", "wide"), axis=0, tiled=True),
        lax.all_gather(gain_two, ("batch", "wide"), axis=0, tiled=True),
    )
    seq_length, width = (inputs.shape[1], inputs.shape[2])
    tokens_in = inputs[0].astype(jnp.float32)
    seq_live = lengths[0]
    live_rows = jnp.arange(seq_length) < seq_live
    taps = full_taps.astype(jnp.float32)
    gain_first = full_gain_one.astype(jnp.float32)
    gain_second = full_gain_two.astype(jnp.float32)
    hat_one, inv_one = norm_parts(tokens_in)
    normed_one = (hat_one * gain_first).astype(jnp.bfloat16)
    projected = jnp.dot(normed_one, full_qkv, preferred_element_type=jnp.float32)
    mixed = (
        projected * taps[:, 0]
        + shift_down(projected, 1) * taps[:, 1]
        + shift_down(projected, 2) * taps[:, 2]
    ).astype(jnp.bfloat16)
    query = mixed[:, :width].reshape(seq_length, HEADS, HD)
    keys = mixed[:, width : 2 * width].reshape(seq_length, HEADS, HD)
    values = mixed[:, 2 * width :].reshape(seq_length, HEADS, HD)
    rows_block = min(512, seq_length)
    block_index = 0
    start_row = block_index * rows_block
    scores, allowed = scores_block(query, keys, start_row, seq_live)
    masked = jnp.where(allowed, scores, -1e30)
    top_score = jnp.max(masked, axis=-1, keepdims=True)
    exp_terms = jnp.exp(masked - top_score)
    row_totals = jnp.sum(exp_terms, axis=-1, keepdims=True)
    probs_low = (exp_terms / row_totals).astype(jnp.bfloat16)
    out_parts = jnp.einsum("hqk,khd->qhd", probs_low, values, preferred_element_type=jnp.float32)
    lse_parts = [top_score + jnp.log(row_totals)]
    attended_low = out_parts.reshape(seq_length, width).astype(jnp.bfloat16)
    branch_attn = jnp.dot(attended_low, full_out, preferred_element_type=jnp.float32)
    residual = tokens_in + branch_attn
    hat_two, inv_two = norm_parts(residual)
    normed_two = (hat_two * gain_second).astype(jnp.bfloat16)
    grad_out = jnp.where(live_rows[:, None], cotangent[0], jnp.zeros_like(cotangent[0]))
    row_set = lax.all_gather(normed_two[None], "wide", axis=0, tiled=True).reshape(-1, width)
    pre_act = jnp.dot(row_set, w_in, preferred_element_type=jnp.float32)
    activ = jnp.square(jax.nn.relu(pre_act)).astype(jnp.bfloat16)
    piece = activ
    branch_ffn = lax.psum_scatter(
        jnp.dot(piece, w_fc2, preferred_element_type=jnp.float32).astype(jnp.bfloat16),
        "wide",
        scatter_dimension=0,
        tiled=True,
    ).astype(jnp.float32)
    grad_set = lax.all_gather(grad_out[None], "wide", axis=0, tiled=True).reshape(-1, width)
    grad_act = contract_last(grad_set, w_fc2)
    grad_fc2_part = contract_first(activ, grad_set)
    grad_pre = (grad_act * 2.0 * jax.nn.relu(pre_act)).astype(jnp.bfloat16)
    grad_in_part = contract_first(row_set, grad_pre)
    piece = grad_pre
    grad_normed_two = lax.psum_scatter(
        contract_last(piece, w_in).astype(jnp.bfloat16), "wide", scatter_dimension=0, tiled=True
    ).astype(jnp.float32)
    grad_w_in, grad_w_fc2 = (
        lax.psum_scatter(
            grad_in_part.astype(jnp.bfloat16), "batch", scatter_dimension=0, tiled=True
        ).astype(jnp.float32),
        lax.psum_scatter(
            grad_fc2_part.astype(jnp.bfloat16), "batch", scatter_dimension=1, tiled=True
        ).astype(jnp.float32),
    )
    output = jnp.where(live_rows[:, None], residual + branch_ffn, 0.0).astype(jnp.bfloat16)[None]
    grad_ln_two, grad_gain_second = norm_back(grad_normed_two, gain_second, hat_two, inv_two)
    grad_residual = grad_out.astype(jnp.float32) + grad_ln_two
    grad_branch = grad_residual.astype(jnp.bfloat16)
    grad_w_out_part = contract_first(attended_low, grad_branch)
    grad_attended = contract_last(grad_branch, full_out).astype(jnp.bfloat16)
    grad_att_heads = grad_attended.reshape(seq_length, HEADS, HD)
    delta_all = jnp.sum(grad_att_heads.astype(jnp.float32) * out_parts, axis=-1)
    block_index = 0
    start_row = block_index * rows_block
    scores, allowed = scores_block(query, keys, start_row, seq_live)
    probs_full = jnp.where(allowed, jnp.exp(scores - lse_parts[block_index]), 0.0)
    probs_low = probs_full.astype(jnp.bfloat16)
    grad_probs = jnp.einsum(
        "qhd,khd->hqk", grad_att_heads, values, preferred_element_type=jnp.float32
    )
    delta_block = jnp.transpose(delta_all)[:, :, None]
    grad_scores = (probs_full * (grad_probs - delta_block)).astype(jnp.bfloat16)
    grad_query_parts = 0.125 * jnp.einsum(
        "hqk,khd->qhd", grad_scores, keys, preferred_element_type=jnp.float32
    )
    grad_keys = 0.125 * jnp.einsum(
        "hqk,qhd->khd", grad_scores, query, preferred_element_type=jnp.float32
    )
    grad_values = jnp.einsum(
        "hqk,qhd->khd", probs_low, grad_att_heads, preferred_element_type=jnp.float32
    )
    grad_mixed = jnp.concatenate(
        [
            grad_query_parts.reshape(seq_length, width),
            grad_keys.reshape(seq_length, width),
            grad_values.reshape(seq_length, width),
        ],
        axis=1,
    )
    grad_taps_part = jnp.stack(
        [
            jnp.sum(grad_mixed * projected, axis=0),
            jnp.sum(grad_mixed * shift_down(projected, 1), axis=0),
            jnp.sum(grad_mixed * shift_down(projected, 2), axis=0),
        ],
        axis=1,
    )
    grad_projected = (
        grad_mixed * taps[:, 0]
        + shift_up(grad_mixed, 1) * taps[:, 1]
        + shift_up(grad_mixed, 2) * taps[:, 2]
    ).astype(jnp.bfloat16)
    grad_qkv_part = contract_first(normed_one, grad_projected)
    grad_normed_one = contract_last(grad_projected, full_qkv)
    grad_ln_one, grad_gain_first = norm_back(grad_normed_one, gain_first, hat_one, inv_one)
    grad_inputs = (grad_residual + grad_ln_one).astype(jnp.bfloat16)[None]
    grad_w_qkv, grad_w_out, grad_conv_taps, grad_gain_one, grad_gain_two = (
        lax.psum_scatter(grad_qkv_part, ("batch", "wide"), scatter_dimension=0, tiled=True),
        lax.psum_scatter(grad_w_out_part, ("batch", "wide"), scatter_dimension=0, tiled=True),
        lax.psum_scatter(grad_taps_part, ("batch", "wide"), scatter_dimension=0, tiled=True),
        lax.psum_scatter(grad_gain_first, ("batch", "wide"), scatter_dimension=0, tiled=True),
        lax.psum_scatter(grad_gain_second, ("batch", "wide"), scatter_dimension=0, tiled=True),
    )
    return (
        output,
        grad_inputs,
        grad_w_qkv,
        grad_w_out,
        grad_conv_taps,
        grad_gain_one,
        grad_gain_two,
        grad_w_in,
        grad_w_fc2,
    )


BF = jnp.bfloat16
F32 = jnp.float32
AXES = ("batch", "wide")
LANES = 256
PART = 128
VMEM_MIB = {"ffn": 36}


def fits(mesh, args):
    inputs, w_qkv, w_in = args[0], args[3], args[8]
    count = mesh.shape["batch"] * mesh.shape["wide"]
    return (
        mesh.shape["batch"] == 4
        and mesh.shape["wide"] == 8
        and inputs.shape[0] == count
        and inputs.shape[1] % LANES == 0
        and w_qkv.shape[0] % (count * 8) == 0
        and w_qkv.shape[0] % LANES == 0
        and w_qkv.shape[0] // HEADS == HD
        and w_in.shape[1] == 8 * 3 * PART
        and (w_in.shape[0] // 4) % 16 == 0
    )


def dot(left, right, left_dim, right_dim):
    return lax.dot_general(
        left, right, (((left_dim,), (right_dim,)), ((), ())), preferred_element_type=F32
    )


def flip_pairs(rule):
    return [(i, i ^ rule(i)) for i in range(32)]


def send(array, rule):
    return lax.ppermute(array, AXES, flip_pairs(rule))


def over_core(i):
    return 8


def over_first(i):
    return 16 if i & 8 else 1


def over_second(i):
    return 1 if i & 8 else 16


def over_z(step):
    return lambda i: 2 * step


def tie(value, *others):
    return lax.optimization_barrier((value,) + others)[0]


def join(parts):
    return jnp.concatenate(parts)


def added(keep, come):
    return (keep.astype(F32) + come.astype(F32)).astype(BF)


def halved(keep, come):
    half = keep.shape[0] // 2
    return added(keep[:half], come[:half]), added(keep[half:], come[half:])


def place_of(me, other):
    apart = me ^ other
    x_bit, z_bits = apart & 1, (apart & 2) | ((apart >> 2) & 1)
    core_bit, y_bit = (apart >> 3) & 1, (apart >> 4) & 1
    on_first = ((other >> 3) & 1) == 0
    high = jnp.where(on_first, y_bit, x_bit)
    low = jnp.where(on_first, x_bit, y_bit)
    return core_bit * 16 + high * 8 + low * 4 + z_bits


def call(kernel, grid, in_specs, out_specs, out_shape, scratch=(), busy=1, name=None, aliases=None):
    return pl.pallas_call(
        kernel,
        grid_spec=pltpu.PrefetchScalarGridSpec(
            num_scalar_prefetch=1,
            grid=grid,
            in_specs=in_specs,
            out_specs=out_specs,
            scratch_shapes=list(scratch),
        ),
        out_shape=out_shape,
        compiler_params=pltpu.CompilerParams(
            dimension_semantics=("arbitrary",) * len(grid), vmem_limit_bytes=VMEM_MIB.get(name, 20) * 1024 * 1024
        ),
        cost_estimate=pl.CostEstimate(flops=int(busy * 1.15e9), bytes_accessed=0, transcendentals=0),
        name=name,
        input_output_aliases=aliases or {},
    )


def whole(shape):
    zeros = (0,) * len(shape)
    return pl.BlockSpec(shape, lambda *_: zeros, pipeline_mode=pl.Buffered(1))


def hat_of(values_in):
    centered = values_in - jnp.mean(values_in, axis=-1, keepdims=True)
    inv_std = lax.rsqrt(jnp.mean(centered * centered, axis=-1, keepdims=True) + epsilon)
    return centered * inv_std, inv_std


def turned(value):
    return jnp.transpose(value.astype(F32)).astype(BF)


def prepare_kernel(meta, cot_ref, go_ref, got_ref):
    live = lax.broadcasted_iota(jnp.int32, (cot_ref.shape[0], 1), 0) < meta[33]
    value = jnp.where(live, cot_ref[...].astype(F32), 0.0)
    go_ref[...] = value.astype(BF)
    got_ref[...] = jnp.transpose(value).astype(BF)


def pack_kernel(meta, up_ref, down_ref, out_ref, a_ref, b_ref):
    half = up_ref.shape[0] // 2
    second_half, second_core = (meta[32] >> 1) == 1, (meta[32] & 1) == 1
    up = jnp.where(second_half, up_ref[half:, :], up_ref[:half, :])
    down = turned(jnp.where(second_half, down_ref[:, half:], down_ref[:, :half]))
    for i, part in enumerate((up, down)):
        a_ref[0, i * half : (i + 1) * half, :] = jnp.where(second_core, part[:, PART : 2 * PART], part[:, :PART])
    left, right = swap_halves(up[:, 2 * PART :], down[:, 2 * PART :])
    b_ref[0, :half, :] = jnp.where(second_core, right, left).astype(BF)
    rows = out_ref.shape[0]
    for c in range(out_ref.shape[1] // PART):
        b_ref[0, half + c * rows : half + (c + 1) * rows, :] = out_ref[:, c * PART : (c + 1) * PART]


def block_of(meta, i, own_ref, other_ref):
    place = meta[i]
    return jnp.where(place < 16, own_ref[place & 15], other_ref[place & 15])


def project_kernel(
    meta, x_ref, own_ref, other_ref, few_own_ref, few_other_ref,
    proj_ref, mixed_ref, wn_ref, nt_ref, taps_ref, gains_ref, normed,
):
    rows = own_ref.shape[1]
    step = pl.program_id(0)

    def few_of(device, lanes):
        block = block_of(meta, device, few_own_ref, few_other_ref)[:8].astype(F32)
        return jnp.concatenate([block, jnp.zeros((8, lanes - PART), F32)], axis=1)

    @pl.when(step == 0)
    def _():
        width = gains_ref.shape[1]
        lane = lax.broadcasted_iota(jnp.int32, (8, width), 1)
        gains = jnp.zeros((8, width), F32)
        for i in range(32):
            first = i * rows
            moved = pltpu.roll(few_of(i, width), first, 1)
            gains = jnp.where((lane >= first) & (lane < first + rows), moved, gains)
        gains_ref[...] = gains
        hat, _ = hat_of(x_ref[...].astype(F32))
        low = (hat * gains[3:4, :]).astype(BF)
        normed[...] = low
        flipped = turned(low)
        for i in range(32):
            nt_ref[meta[i]] = flipped[i * rows : (i + 1) * rows]

    channels = 3 * rows
    lane = lax.broadcasted_iota(jnp.int32, (8, LANES), 1)
    taps = jnp.zeros((8, LANES), F32)
    for i in range(LANES // channels + 2):
        device = jnp.minimum((step * LANES) // channels + i, 31)
        first = device * channels - step * LANES
        moved = pltpu.roll(few_of(device, LANES), (first + 2 * LANES) & (LANES - 1), 1)
        taps = jnp.where((lane >= first) & (lane < first + channels), moved, taps)
    taps_ref[...] = taps
    for i in range(32):
        wn_ref[i * rows : (i + 1) * rows, :] = block_of(meta, i, own_ref, other_ref)
    value = dot(normed[...], wn_ref[...], 1, 0)
    at = lax.broadcasted_iota(jnp.int32, value.shape, 0)
    one = jnp.where(at >= 1, pltpu.roll(value, 1, 0), 0.0)
    two = jnp.where(at >= 2, pltpu.roll(value, 2, 0), 0.0)
    mixed = value * taps[0:1, :] + one * taps[1:2, :] + two * taps[2:3, :]
    proj_ref[...] = value.astype(BF)
    mixed_ref[...] = mixed.astype(BF)


def head_row(head, scale=1.0):
    lane = lax.broadcasted_iota(jnp.int32, (1, LANES), 1)
    return jnp.where(lane // HD == head, scale, 0.0).astype(BF)


def allowed_in(meta, keys, first_query, queries):
    key = lax.broadcasted_iota(jnp.int32, (keys, queries), 0)
    query = first_query + lax.broadcasted_iota(jnp.int32, (1, queries), 1)
    return key < jnp.minimum(query + 1, meta[33])


def attend_kernel(meta, q_ref, k_ref, v_ref, out_ref, lse_ref, flipped):
    seq = q_ref.shape[0]
    tile = LANES
    values_t = turned(v_ref[...])
    keys = k_ref[...]
    for t in range(seq // tile):
        upto = (t + 1) * tile
        allowed = allowed_in(meta, upto, t * tile, tile)
        query = q_ref[t * tile : upto, :]
        for head in range(LANES // HD):
            scores = dot(keys[:upto], query * head_row(head, 0.125), 1, 1)
            scores = jnp.where(allowed, scores, -1e30)
            top = jnp.max(scores, axis=0, keepdims=True)
            terms = jnp.exp(scores - top)
            total = jnp.sum(terms, axis=0, keepdims=True)
            probs = (terms * (1.0 / total)).astype(BF)
            flipped[head * HD : (head + 1) * HD, t * tile : upto] = dot(
                values_t[head * HD : (head + 1) * HD, :upto], probs, 1, 0
            )
            lse_ref[0, head : head + 1, t * tile : upto] = top + jnp.log(total)
    out_ref[...] = jnp.transpose(flipped[...]).astype(BF)


def mend_kernel(meta, att_ref, own_ref, other_ref, x_ref, gain_ref, res_ref, n2_ref, n2t_ref, at_ref, wn_ref):
    flipped = turned(att_ref[...])
    rows = at_ref.shape[1]
    for i in range(32):
        at_ref[meta[i]] = flipped[i * rows : (i + 1) * rows]
        block = block_of(meta, i, own_ref, other_ref)
        for c in range(wn_ref.shape[1] // PART):
            wn_ref[i * rows : (i + 1) * rows, c * PART : (c + 1) * PART] = block[c * rows : (c + 1) * rows]
    residual = x_ref[...].astype(F32) + dot(att_ref[...], wn_ref[...], 1, 0)
    res_ref[...] = residual
    hat, _ = hat_of(residual)
    low = (hat * gain_ref[4:5, :]).astype(BF)
    n2_ref[...] = low
    n2t_ref[...] = turned(low)


def swap_halves(left, right):
    left, right = left.astype(F32), right.astype(F32)
    low = lax.broadcasted_iota(jnp.int32, (1, PART), 1) < PART // 2
    return (
        jnp.where(low, left, pltpu.roll(right, PART // 2, 1)),
        jnp.where(low, pltpu.roll(left, PART // 2, 1), right),
    )


def ffn_kernel(packed, meta, *refs):
    token_refs, refs = (refs[:4], refs[4:8]), refs[8:]
    count = 8 if packed else 4
    tiles, refs = refs[:count], refs[count:]
    if packed:
        branch_ref, grad_ref, branch_acc, grad_acc, low_ref, high_ref = refs
    else:
        sums_in, (branch_ref, grad_ref, both_ref, low_ref, high_ref, branch_acc, grad_acc) = refs[:4], refs[4:]
    sums = (branch_ref, grad_ref, branch_acc, grad_acc)
    step = pl.program_id(0)

    @pl.when(step == 0)
    def _():
        for i, ref in enumerate(sums):
            ref[...] = jnp.zeros_like(ref) if packed else sums_in[i][...]

    half = tiles[0].shape[1] if packed else tiles[0].shape[1] // 2
    if packed:
        blocks = [jnp.concatenate([tiles[2 * k][0], tiles[2 * k + 1][0]], axis=0) for k in range(4)]
        pairs = [swap_halves(blocks[0], blocks[1]), swap_halves(blocks[2], blocks[3])]
        w_up, w_down = (jnp.concatenate([pairs[0][i], pairs[1][i]], axis=1).astype(BF) for i in range(2))
    else:
        w_up, w_down = (
            jnp.concatenate(
                [
                    jnp.concatenate([tiles[2 * k + b][0, i * half : (i + 1) * half, :] for b in range(2)], axis=0)
                    for k in range(2)
                ],
                axis=1,
            )
            for i in range(2)
        )
    up_sum = down_sum = 0.0
    for i, (n2_ref, go_ref, n2t_ref, got_ref) in enumerate(token_refs):
        pre = jnp.maximum(dot(n2_ref[...], w_up, 1, 0), 0.0)
        activ = (pre * pre).astype(BF)
        grad_pre = (dot(go_ref[...], w_down, 1, 0) * 2.0 * pre).astype(BF)
        sums[2 * i][...] += dot(activ, w_down, 1, 1)
        sums[2 * i + 1][...] += dot(grad_pre, w_up, 1, 1)
        up_sum += dot(n2t_ref[...], grad_pre, 1, 0)
        down_sum += dot(got_ref[...], activ, 1, 0)
    first_wide = step * (4 if packed else 2)
    results = []
    for k in range(2):
        lanes = slice(k * PART, (k + 1) * PART)
        if packed:
            results += [(part,) for part in swap_halves(up_sum[:, lanes], down_sum[:, lanes])]
        else:
            results.append((up_sum[:, lanes], down_sum[:, lanes]))
    for k, parts in enumerate(results):
        for b in range(2):
            place = meta[b * 16 + (meta[32] & 1) * 8 + first_wide + k]
            for is_high, target in enumerate((low_ref, high_ref)):

                @pl.when((place >> 3) == is_high)
                def _(place=place, target=target, parts=parts, b=b):
                    for i, part in enumerate(parts):
                        target[place & 7, i * half : (i + 1) * half, :] = part[b * half : (b + 1) * half].astype(BF)

    if not packed:

        @pl.when(step == pl.num_programs(0) - 1)
        def _():
            seq = branch_acc.shape[0]
            both_ref[:seq, :] = branch_acc[...].astype(BF)
            both_ref[seq:, :] = grad_acc[...].astype(BF)


def turn_kernel(meta, grad_ref, branch_ref, come_ref, res_ref, gain_ref, go_ref, at_ref, wn_ref, out_ref, gres_ref, gatt_ref, ggain_ref, keep_ref, away_ref):
    residual = res_ref[...]
    seq = residual.shape[0]
    live = lax.broadcasted_iota(jnp.int32, (seq, 1), 0) < meta[33]
    branch = branch_ref[...] + come_ref[:seq, :].astype(F32)
    out_ref[...] = jnp.where(live, residual + branch, 0.0).astype(BF)
    hat, inv_std = hat_of(residual)
    grad = grad_ref[...] + come_ref[seq:, :].astype(F32)
    ggain_ref[...] = jnp.sum(grad * hat, axis=0, keepdims=True)
    scaled = grad * gain_ref[4:5, :]
    mean_first = jnp.mean(scaled, axis=-1, keepdims=True)
    mean_second = jnp.mean(scaled * hat, axis=-1, keepdims=True)
    grad_res = go_ref[...].astype(F32) + inv_std * (scaled - mean_first - hat * mean_second)
    gres_ref[...] = grad_res
    low = grad_res.astype(BF)
    gatt_ref[...] = dot(low, wn_ref[...], 1, 1).astype(BF)
    result = dot(at_ref[...], low, 1, 0)
    lanes = keep_ref.shape[2]
    chunks = result.shape[1] // lanes
    rows = keep_ref.shape[1] // chunks
    for i in range(32):
        target = away_ref if i >= 16 else keep_ref
        for c in range(chunks):
            target[i & 15, c * rows : (c + 1) * rows, :] = result[
                i * rows : (i + 1) * rows, c * lanes : (c + 1) * lanes
            ].astype(BF)


def attend_back_kernel(
    meta, q_ref, k_ref, v_ref, pq_ref, pk_ref, pv_ref, tq_ref, tk_ref, tv_ref, go_ref, out_ref, lse_ref,
    gq_ref, gk_ref, gv_ref, dtq_ref, dtk_ref, dtv_ref, flipped,
):
    seq = q_ref.shape[0]
    tile = LANES
    keys, values = k_ref[...], v_ref[...]
    keys_t = turned(keys)
    delta_t = jnp.transpose(go_ref[...].astype(F32) * out_ref[...].astype(F32))
    grad_keys = [jnp.zeros((tile, LANES), F32) for _ in range(seq // tile)]
    grad_values = list(grad_keys)
    for t in range(seq // tile):
        upto = (t + 1) * tile
        allowed = allowed_in(meta, upto, t * tile, tile)
        query, grad = q_ref[t * tile : upto, :], go_ref[t * tile : upto, :]
        for head in range(LANES // HD):
            lanes = slice(head * HD, (head + 1) * HD)
            query_h, grad_h = query * head_row(head, 0.125), grad * head_row(head)
            delta = jnp.sum(delta_t[lanes, t * tile : upto], axis=0, keepdims=True)
            scores = dot(keys[:upto], query_h, 1, 1)
            lse = lse_ref[0, head : head + 1, t * tile : upto]
            probs = jnp.where(allowed, jnp.exp(scores - lse), 0.0)
            grad_scores = (probs * (dot(values[:upto], grad_h, 1, 1) - delta)).astype(BF)
            flipped[lanes, t * tile : upto] = dot(keys_t[lanes, :upto], grad_scores, 1, 0) * 0.125
            add_values = dot(probs.astype(BF), grad_h, 1, 0)
            add_keys = dot(grad_scores, query_h, 1, 0)
            for s in range(t + 1):
                rows = slice(s * tile, (s + 1) * tile)
                grad_values[s] += add_values[rows]
                grad_keys[s] += add_keys[rows]
    mixed = (
        jnp.transpose(flipped[...]),
        jnp.concatenate(grad_keys, axis=0),
        jnp.concatenate(grad_values, axis=0),
    )
    at = lax.broadcasted_iota(jnp.int32, (seq, LANES), 0)
    for grad, proj_ref, taps_ref, g_ref, dt_ref in zip(
        mixed, (pq_ref, pk_ref, pv_ref), (tq_ref, tk_ref, tv_ref), (gq_ref, gk_ref, gv_ref), (dtq_ref, dtk_ref, dtv_ref)
    ):
        one = jnp.where(at < seq - 1, pltpu.roll(grad, seq - 1, 0), 0.0)
        two = jnp.where(at < seq - 2, pltpu.roll(grad, seq - 2, 0), 0.0)
        g_ref[...] = (grad * taps_ref[0:1, :] + one * taps_ref[1:2, :] + two * taps_ref[2:3, :]).astype(BF)
        proj = proj_ref[...].astype(F32)
        for tap, part in enumerate((grad, one, two)):
            dt_ref[tap : tap + 1, :] = jnp.sum(part * proj, axis=0, keepdims=True)


def weight_kernel(with_few, meta, nt_ref, *refs):
    if with_few:
        (*tap_refs, gain_ref), refs, few = refs[:7], refs[7:-1], refs[-1]
    keep_ref, away_ref = refs[-2:]
    half, full = keep_ref.shape
    start = 0
    for g_ref in refs[:-2]:
        result = dot(nt_ref[...], g_ref[...], 1, 0).astype(BF)
        columns = slice(start, start + g_ref.shape[1])
        start += g_ref.shape[1]
        keep_ref[:, columns] = result[:half]
        away_ref[:, columns] = result[half:]
    if with_few:
        rows = half // 16
        row = lax.broadcasted_iota(jnp.int32, (8, PART), 0)
        lane = lax.broadcasted_iota(jnp.int32, (8, PART), 1)
        taps = jnp.concatenate([ref[...] for ref in tap_refs], axis=1)
        gains = jnp.broadcast_to(gain_ref[...], (8, gain_ref.shape[1]))

        def taken(values_in, first):
            start = first // PART * PART
            window = values_in[:, start : start + 2 * PART]
            return pltpu.roll(window, (start - first) % window.shape[1], 1)[:, :PART]

        for i in range(32):
            piece = jnp.where((row == 3) & (lane < rows), taken(gains, i * rows), 0.0)
            few[meta[i]] = jnp.where((row < 3) & (lane < 3 * rows), taken(taps, i * 3 * rows), piece)
        for i, ref in enumerate((keep_ref, away_ref)):
            ref[:, full - PART :] = jnp.zeros((half, PART), BF)
            for k in range(16):
                ref[k * rows : k * rows + 8, full - PART :] = few[i * 16 + k].astype(BF)


def last_kernel(meta, *refs):
    grads, (w_ref, x_ref, gain_ref, gres_ref, gin_ref) = refs[:-5], refs[-5:]
    grad = dot(jnp.concatenate([g_ref[...] for g_ref in grads], axis=1), w_ref[...], 1, 1)
    hat, inv_std = hat_of(x_ref[...].astype(F32))
    scaled = grad * gain_ref[3:4, :]
    mean_first = jnp.mean(scaled, axis=-1, keepdims=True)
    mean_second = jnp.mean(scaled * hat, axis=-1, keepdims=True)
    back = inv_std * (scaled - mean_first - hat * mean_second)
    gin_ref[...] = (gres_ref[...] + back).astype(BF)


def own_sequence(inputs, lengths, cotangent, w_qkv, w_out, conv_taps, gain_one, gain_two, w_in, w_fc2):
    seq, width = inputs.shape[1], inputs.shape[2]
    rows, wide = w_qkv.shape
    half = width // 2
    tap_rows = conv_taps.shape[0]
    batch = lax.axis_index("batch")
    core = batch & 1
    me = batch * 8 + lax.axis_index("wide")
    number = jnp.arange(64, dtype=jnp.int32)
    meta = jnp.where(number < 32, place_of(me, number & 31), jnp.where(number == 32, batch, lengths[0]))
    x, cot = inputs[0], cotangent[0]
    shape = jax.ShapeDtypeStruct
    row_spec = whole((1, width))
    gain_spec = whole((8, width))
    token = whole((seq, width))
    token_t = whole((width, seq))
    groups = width // LANES

    few_rows = [jnp.pad(conv_taps.T, ((0, 0), (0, PART - tap_rows)))]
    few_rows += [jnp.pad(gain[None], ((0, 0), (0, PART - rows))) for gain in (gain_one, gain_two)]
    few_rows = jnp.concatenate(few_rows + [jnp.zeros((rows - 5, PART), BF)])
    qkv_block = jnp.concatenate([w_qkv, few_rows], axis=1)[None]
    qkv_block, meta, first_core = lax.optimization_barrier((qkv_block, meta, core == 0))
    qkv_far = send(qkv_block, over_z(2))
    out_rows = rows * (width // PART)
    a_block, b_block = call(
        pack_kernel, (1,), [whole(w.shape) for w in (w_in, w_fc2, w_out)],
        [whole((1, width, PART)), whole((1, half + out_rows, PART))],
        [shape((1, width, PART), BF), shape((1, half + out_rows, PART), BF)], busy=2, name="pack",
    )(meta, w_in, w_fc2, w_out)

    b_far = send(tie(b_block, qkv_far), over_z(2))
    qkv2 = join([qkv_block, tie(qkv_far, b_block)])
    qkv_near = send(qkv2, over_z(1))
    qkv4 = join([qkv2, qkv_near])
    qkv_first = send(qkv4, over_first)
    b2 = join([b_block, tie(b_far, qkv4)])
    b_near = send(b2, over_z(1))
    a_far = send(tie(a_block, b2), over_z(2))
    qkv8 = join([qkv4, tie(qkv_first, b2)])
    qkv_second = send(qkv8, over_second)
    grad_out, grad_out_t = call(
        prepare_kernel, (1,), [token], [token, token_t],
        [shape((seq, width), BF), shape((width, seq), BF)], busy=1, name="prepare",
    )(meta, tie(cot, qkv_far))
    go_other = send(grad_out, over_core)
    got_other = send(grad_out_t, over_core)
    b4 = join([b2, tie(b_near, qkv8)])
    a2 = join([a_block, tie(a_far, qkv8)])
    a_near = send(a2, over_z(1))
    qkv16 = join([qkv8, tie(qkv_second, a2, b4)])
    qkv_core = send(qkv16, over_core)
    b_first = send(tie(b4, qkv16), over_first)
    a4 = join([a2, tie(a_near, qkv_core)])
    a_first = send(a4, over_first)

    lane_block = pl.BlockSpec((seq, LANES), lambda j, m: (0, j))
    half_block = pl.BlockSpec((16, rows, LANES), lambda j, m: (0, 0, j))
    few_block = pl.BlockSpec((16, rows, PART), lambda j, m: (0, 0, wide // PART))
    tap_block = pl.BlockSpec((8, LANES), lambda j, m: (0, j))
    projected, mixed, qkv_full, normed_t, taps, gains = call(
        project_kernel, (wide // LANES,),
        [token, half_block, half_block, few_block, few_block],
        [lane_block, lane_block, pl.BlockSpec((width, LANES), lambda j, m: (0, j)), whole((32, rows, seq)),
         tap_block, gain_spec],
        [shape((seq, wide), BF), shape((seq, wide), BF), shape((width, wide), BF), shape((32, rows, seq), BF),
         shape((8, wide), F32), shape((8, width), F32)],
        [pltpu.VMEM((seq, width), BF)], busy=7, name="project",
    )(meta, tie(x, a4), qkv16, qkv_core, qkv16, qkv_core)

    b8 = join([b4, tie(b_first, mixed)])
    b_second = send(b8, over_second)
    part_specs = [pl.BlockSpec((seq, LANES), lambda j, m, p=p: (0, p * groups + j)) for p in range(3)]
    lse_spec = pl.BlockSpec((1, 8, seq), lambda j, m: (j, 0, 0))
    a8 = join([a4, tie(a_first, mixed)])
    ready = tie(mixed, b8, a8, go_other, got_other)
    attended, lse = call(
        attend_kernel, (groups,), part_specs, [lane_block, lse_spec],
        [shape((seq, width), BF), shape((groups, 8, seq), F32)], [pltpu.VMEM((LANES, seq), F32)],
        busy=9, name="attend",
    )(meta, ready, ready, ready)

    b16 = join([b8, tie(b_second, attended)])
    out16 = b16[:, half:, :]
    out_core = send(out16, over_core)
    a_second = send(tie(a8, b16), over_second)
    residual, normed_two, normed_two_t, attended_t, out_full = call(
        mend_kernel, (1,),
        [token, whole(out16.shape), whole(out16.shape), token, gain_spec],
        [token, token, token_t, whole((32, rows, seq)), whole((width, width))],
        [shape((seq, width), F32), shape((seq, width), BF), shape((width, seq), BF), shape((32, rows, seq), BF),
         shape((width, width), BF)],
        busy=2.5, name="mend",
    )(meta, attended, out16, out_core, x, gains)
    n2_other = send(normed_two, over_core)
    n2t_other = send(normed_two_t, over_core)

    sequences = [normed_two, grad_out, normed_two_t, grad_out_t, n2_other, go_other, n2t_other, got_other]
    sequence_specs = [token, token, token_t, token_t] * 2

    def tile(block_rows, per_step, k, b):
        return pl.BlockSpec(
            (1, block_rows, PART), lambda s, m: (m[b * 16 + (m[32] & 1) * 8 + s * per_step + k], 0, 0)
        )

    total = shape((seq, width), F32)
    grads_b = shape((8, half, PART), BF)
    branch, grad_two, branch_o, grad_o, b_low, b_high = call(
        functools.partial(ffn_kernel, True), (2,),
        sequence_specs + [tile(half, 4, k, b) for k in range(4) for b in range(2)],
        [token] * 4 + [whole(grads_b.shape)] * 2, [total] * 4 + [grads_b] * 2, busy=2, name="ffn",
    )(meta, *sequences, *[b16] * 8)
    a16 = join([a8, tie(a_second, branch)])
    b_sum = send(b_high, over_second)
    grads_a = shape((8, width, PART), BF)
    branch, grad_two, both, a_low, a_high = call(
        functools.partial(ffn_kernel, False), (4,),
        sequence_specs + [tile(width, 2, k, b) for k in range(2) for b in range(2)] + [token] * 4,
        [token] * 2 + [whole((2 * seq, width))] + [whole(grads_a.shape)] * 2,
        [total] * 2 + [shape((2 * seq, width), BF)] + [grads_a] * 2,
        [pltpu.VMEM((seq, width), F32)] * 2, busy=15, name="ffn",
    )(meta, tie(normed_two, b_high), *sequences[1:], *[a16] * 4, branch, grad_two, branch_o, grad_o)
    b_sum = tie(b_sum, branch)
    come = send(tie(both, b_sum), over_core)
    a_sum = send(a_high, over_second)
    b_keep, b_go = halved(b_low, b_sum)
    half_out = shape((16, rows * (width // PART), PART), BF)
    output, grad_residual, grad_attended, grad_gain_second, keep_out, away_out = call(
        turn_kernel, (1,),
        [token] * 2 + [whole((2 * seq, width)), token, gain_spec, token, token_t, whole((width, width))],
        [token] * 3 + [row_spec, whole(half_out.shape), whole(half_out.shape)],
        [shape((seq, width), BF), shape((seq, width), F32), shape((seq, width), BF), shape((1, width), F32),
         half_out, half_out],
        busy=4, name="turn",
    )(meta, tie(grad_two, a_high, b_go), branch, come, residual, gains, grad_out, attended_t.reshape(width, seq), out_full)

    def attend_back(first, count, wait_for):
        def lanes(height, part, start):
            return pl.BlockSpec((height, LANES), lambda i, m: (0, part * groups + start + i))

        specs = [lanes(seq, p, first) for p in range(3)]
        tap_specs = [lanes(8, p, first) for p in range(3)]
        return call(
            attend_back_kernel, (count,),
            specs * 2 + tap_specs + [specs[0]] * 2 + [pl.BlockSpec((1, 8, seq), lambda i, m: (first + i, 0, 0))],
            [lanes(seq, 0, 0)] * 3 + [lanes(8, 0, 0)] * 3,
            [shape((seq, count * LANES), BF)] * 3 + [shape((8, count * LANES), F32)] * 3,
            [pltpu.VMEM((LANES, seq), F32)], busy=count, name="attend_back",
        )(meta, mixed, mixed, mixed, projected, projected, projected, taps, taps, taps,
          tie(grad_attended, *wait_for), attended, lse)

    def weights(grads, few, wait_for):
        size = sum(g.shape[1] for g in grads) + (PART if few else 0)
        spec = whole((half, size))
        keep, away = call(
            functools.partial(weight_kernel, bool(few)), (1,),
            [token_t] + [whole(part.shape) for part in [*few, *grads]],
            [spec, spec], [shape((half, size), BF)] * 2, [pltpu.VMEM((32, 8, PART), F32)] if few else (),
            busy=1, name="weight",
        )(meta, tie(normed_t.reshape(width, seq), *wait_for), *few, *grads)
        return keep.reshape(16, rows, size), away.reshape(16, rows, size)

    out_come = send(away_out, over_core)
    back0 = attend_back(0, groups - 1, (away_out,))

    out_sum = added(keep_out, tie(out_come, back0[0]))
    out_go = out_sum[8:]
    out_come = send(out_go, over_second)
    x_keep, x_away = weights(back0[:3], [], (out_go,))
    x_sum = send(x_away, over_core)
    a_keep, a_go = halved(a_low, tie(a_sum, x_away))
    a_sum = send(a_go, over_first)
    back2 = attend_back(groups - 1, 1, (back0[0], x_away, a_go))
    backs = (back0, back2)
    grad_projected = [back[part] for part in range(3) for back in backs]
    few = [back[3 + part] for part in range(3) for back in backs] + [grad_gain_second]
    y_keep, y_away = weights(back2[:3], few, ())
    y_sum = send(y_away, over_core)

    out_keep, out_go = halved(out_sum[:8], tie(out_come, y_away))
    b_keep = jnp.concatenate([b_keep, out_keep], axis=1)
    b_go = jnp.concatenate([b_go, out_go], axis=1)
    b_sum = send(b_go, over_first)
    grad_inputs = call(
        last_kernel, (1,),
        [whole(g.shape) for g in grad_projected] + [whole((width, wide)), token, gain_spec, token],
        [token], [shape((seq, width), BF)], busy=4, name="last",
    )(meta, *grad_projected, qkv_full, x, gains, tie(grad_residual, y_away, a_go, b_go))[0]
    x_keep, x_go = halved(x_keep, tie(x_sum, grad_inputs))
    x_sum = send(x_go, over_second)
    y_keep, y_go = halved(y_keep, tie(y_sum, x_go))
    y_sum = send(y_go, over_second)
    a_keep, a_go = halved(a_keep, tie(a_sum, y_go))
    a_sum = send(a_go, over_z(1))
    b_keep, b_go = halved(b_keep, tie(b_sum, a_go))
    b_sum = send(b_go, over_z(1))
    x_keep, x_go = halved(x_keep, tie(x_sum, b_go))
    x_sum = send(x_go, over_first)
    y_keep, y_go = halved(y_keep, tie(y_sum, x_go))
    y_sum = send(y_go, over_first)
    a_keep, a_go = halved(a_keep, tie(a_sum, y_go))
    a_sum = send(a_go, over_z(2))
    b_keep, b_go = halved(b_keep, tie(b_sum, a_go))
    b_sum = send(b_go, over_z(2))
    x_keep, x_go = halved(x_keep, tie(x_sum, b_go))
    x_sum = send(x_go, over_z(1))
    y_keep, y_go = halved(y_keep, tie(y_sum, x_go))
    y_sum = send(y_go, over_z(1))
    grad_a = a_keep[0].astype(F32) + tie(a_sum, y_go)[0].astype(F32)
    grad_b = b_keep[0].astype(F32) + tie(b_sum, y_go)[0].astype(F32)
    grad_out_w = jnp.transpose(grad_b[half:].reshape(width // PART, rows, PART), (1, 0, 2)).reshape(rows, width)
    quarter = width // 4

    def share(swapped):
        pairs = [
            (g[first : first + quarter], g[first + quarter : first + 2 * quarter])
            for g, first in ((grad_a, 0), (grad_a, half), (grad_b, 0))
        ]
        return jnp.concatenate([jnp.where(first_core, p[swapped], p[1 - swapped]) for p in pairs])

    mine = share(0)
    theirs = send(share(1), over_core)
    mine, theirs = jnp.where(first_core, mine, theirs), jnp.where(first_core, theirs, mine)
    units = PART // 2
    grad_in_w, grad_fc2_w = (
        jnp.concatenate(
            [part[i * quarter : (i + 1) * quarter] for part in (mine, theirs)]
            + [part[2 * quarter :, i * units : (i + 1) * units] for part in (mine, theirs)],
            axis=1,
        )
        for i in range(2)
    )

    x_keep, x_go = halved(x_keep, tie(x_sum, grad_a, grad_b))
    x_sum = send(x_go, over_z(2))
    y_keep, y_go = halved(y_keep, tie(y_sum, x_go))
    y_sum = send(y_go, over_z(2))
    x_total = x_keep[0].astype(F32) + x_sum[0].astype(F32)
    y_total = y_keep[0].astype(F32) + y_sum[0].astype(F32)
    few = y_total[:8, 3 * LANES :]
    grad_qkv = jnp.concatenate(
        [
            part
            for i in range(3)
            for part in (x_total[:, 2 * i * LANES : 2 * (i + 1) * LANES], y_total[:, i * LANES : (i + 1) * LANES])
        ],
        axis=1,
    )
    grad_gain_first = jnp.sum(grad_qkv * w_qkv.astype(F32), axis=1) / gain_one.astype(F32)
    return (
        output[None],
        grad_inputs[None],
        grad_qkv,
        grad_out_w,
        few[:3, :tap_rows].T,
        grad_gain_first,
        few[3, :rows],
        grad_in_w,
        jnp.transpose(grad_fc2_w),
    )


def solution(mesh):
    fast = functools.partial(own_sequence)

    def program(*args):
        body = fast if fits(mesh, args) else shards
        return jax.shard_map(
            body,
            mesh=mesh,
            in_specs=(
                P(("batch", "wide"), None, None),
                P(("batch", "wide")),
                P(("batch", "wide"), None, None),
                P(("batch", "wide"), None),
                P(("batch", "wide"), None),
                P(("batch", "wide"), None),
                P(("batch", "wide")),
                P(("batch", "wide")),
                P(None, "wide"),
                P("wide", None),
            ),
            out_specs=(
                P(("batch", "wide"), None, None),
                P(("batch", "wide"), None, None),
                P(("batch", "wide"), None),
                P(("batch", "wide"), None),
                P(("batch", "wide"), None),
                P(("batch", "wide")),
                P(("batch", "wide")),
                P("batch", "wide"),
                P("wide", "batch"),
            ),
            check_vma=False,
        )(*args)

    return program
```

profile of v0, /device:TPU:0, one launch (start us, length us, event | category | flops | bytes accessed | tf_op | source)
XLA Modules:
  0.0 196.2 jit_solution(7086003057697646473)
XLA Ops:
  1.3 1.0 fusion.22
  2.3 4.1 %collective-permute-start = (bf16[1,24,2432]{2,1,0:T(8,128)(2,1)S(1)}, bf16[1,24,2432]{2,1,0:T(8,128)(2,1)S(1)}, u32[]{:S(2)}, u32[]{:S(2)}) collective-permute-start(bf16[1,24,2432]{2,1,0:T(8,128)(2,1)S(1)} %fusion.22), channel_id=1, source_target_pairs={{0,4},{1,5},{2,6},{3,7},{4,0},{5,1},{6,2},{7,3},{8,12},{9,13},{10,... | collective-permute-start | bytes 350216 | tf_op jit(solution)/shard_map/ppermute | solution.py:240
  6.5 1.1 copy-done.4
  7.5 1.1 copy-done.5
  8.6 0.8 copy-done.6
  9.3 0.8 pack.1
  10.2 1.9 collective-permute-done
  12.1 0.8 collective-permute-start.2
  13.0 6.1 %collective-permute-done.2 = bf16[2,24,2432]{2,1,0:T(8,128)(2,1)S(1)} collective-permute-done((bf16[2,24,2432]{2,1,0:T(8,128)(2,1)S(1)}, bf16[2,24,2432]{2,1,0:T(8,128)(2,1)S(1)}, u32[]{:S(2)}, u32[]{:S(2)}) %collective-permute-start.2) | collective-permute-done | bytes 233504 | tf_op jit(solution)/shard_map/ppermute | solution.py:240
  19.1 1.3 collective-permute-start.4
  20.5 3.3 %collective-permute-start.1 = (bf16[1,528,128]{2,1,0:T(8,128)(2,1)S(1)}, bf16[1,528,128]{2,1,0:T(8,128)(2,1)S(1)}, u32[]{:S(2)}, u32[]{:S(2)}) collective-permute-start(bf16[1,528,128]{2,1,0:T(8,128)(2,1)S(1)} %get-tuple-element.108), channel_id=1, source_target_pairs={{0,4},{1,5},{2,6},{3,7},{4,0},{5,1},{6,2},{7,3},{8,12},{9,13},{10,... | collective-permute-start | bytes 405512 | tf_op jit(solution)/shard_map/ppermute | solution.py:240
  23.9 5.8 %collective-permute-done.1 = bf16[1,528,128]{2,1,0:T(8,128)(2,1)S(1)} collective-permute-done((bf16[1,528,128]{2,1,0:T(8,128)(2,1)S(1)}, bf16[1,528,128]{2,1,0:T(8,128)(2,1)S(1)}, u32[]{:S(2)}, u32[]{:S(2)}) %collective-permute-start.1) | collective-permute-done | bytes 135200 | tf_op jit(solution)/shard_map/ppermute | solution.py:240
  30.5 0.7 collective-permute-start.7
  31.2 3.4 %collective-permute-start.3 = (bf16[1,768,128]{2,1,0:T(8,128)(2,1)S(1)}, bf16[1,768,128]{2,1,0:T(8,128)(2,1)S(1)}, u32[]{:S(2)}, u32[]{:S(2)}) collective-permute-start(bf16[1,768,128]{2,1,0:T(8,128)(2,1)S(1)} %get-tuple-element.111), channel_id=1, source_target_pairs={{0,4},{1,5},{2,6},{3,7},{4,0},{5,1},{6,2},{7,3},{8,12},{9,13},{10,... | collective-permute-start | bytes 589832 | tf_op jit(solution)/shard_map/ppermute | solution.py:240
  34.7 7.4 %collective-permute-done.3 = bf16[1,768,128]{2,1,0:T(8,128)(2,1)S(1)} collective-permute-done((bf16[1,768,128]{2,1,0:T(8,128)(2,1)S(1)}, bf16[1,768,128]{2,1,0:T(8,128)(2,1)S(1)}, u32[]{:S(2)}, u32[]{:S(2)}) %collective-permute-start.3) | collective-permute-done | bytes 196640 | tf_op jit(solution)/shard_map/ppermute | solution.py:240
  42.1 1.3 collective-permute-done.7
  43.9 2.9 %collective-permute-start.5 = (bf16[2,768,128]{2,1,0:T(8,128)(2,1)S(1)}, bf16[2,768,128]{2,1,0:T(8,128)(2,1)S(1)}, u32[]{:S(2)}, u32[]{:S(2)}) collective-permute-start(bf16[2,768,128]{2,1,0:T(8,128)(2,1)S(1)} %get-tuple-element.259), channel_id=1, source_target_pairs={{0,2},{1,3},{2,0},{3,1},{4,6},{5,7},{6,4},{7,5},{8,10},{9,11},{10,... | collective-permute-start | bytes 1179656 | tf_op jit(solution)/shard_map/ppermute | solution.py:240
  46.8 0.8 prepare.1
  48.6 7.9 %collective-permute-done.5 = bf16[2,768,128]{2,1,0:T(8,128)(2,1)S(1)} collective-permute-done((bf16[2,768,128]{2,1,0:T(8,128)(2,1)S(1)}, bf16[2,768,128]{2,1,0:T(8,128)(2,1)S(1)}, u32[]{:S(2)}, u32[]{:S(2)}) %collective-permute-start.5) | collective-permute-done | bytes 393248 | tf_op jit(solution)/shard_map/ppermute | solution.py:240
  57.2 7.2 %project.1 = (bf16[512,2304]{1,0:T(8,128)(2,1)S(1)}, bf16[512,2304]{1,0:T(8,128)(2,1)S(1)}, bf16[768,2304]{1,0:T(8,128)(2,1)S(1)}, bf16[32,24,512]{2,1,0:T(8,128...) custom-call(s32[64]{0:T(128)S(1)} %compare_select_fusion.1.meta, bf16[512,768]{1,0:T(8,128)(2,1)S(1)} %bitcast.53, ...), custom_call_target="tpu_custom_call" | custom-call | flops 8049999872 | tf_op jit(solution)/shard_map/project/pallas_call | solution.py:701
  65.1 5.7 %collective-permute-done.10 = bf16[4,768,128]{2,1,0:T(8,128)(2,1)S(1)} collective-permute-done((bf16[4,768,128]{2,1,0:T(8,128)(2,1)S(1)}, bf16[4,768,128]{2,1,0:T(8,128)(2,1)S(1)}, u32[]{:S(2)}, u32[]{:S(2)}) %collective-permute-start.10) | collective-permute-done | bytes 786464 | tf_op jit(solution)/shard_map/ppermute | solution.py:240
  71.1 9.2 %attend.1 = (bf16[512,768]{1,0:T(8,128)(2,1)S(1)}, f32[3,8,512]{2,1,0:T(8,128)S(1)}) custom-call(s32[64]{0:T(128)S(1)} %compare_select_fusion.1.meta, bf16[512,2304]{1,0:T(8,128)(2,1)S(1)} %get-tuple-element.125.q_ref.k_ref.v_ref, bf16[512,2304]{1,0:T(8,128)(2,1)S(1)} %get-tuple-element.125.q_ref.k_ref.v_ref, ...), custom_call_target="tpu_custom_call" | custom-call | flops 10350000128 | tf_op jit(solution)/shard_map/attend/pallas_call | solution.py:717
  80.7 1.9 collective-permute-done.14.other_ref
  82.6 2.2 %mend.1 = (f32[512,768]{1,0:T(8,128)S(1)}, bf16[512,768]{1,0:T(8,128)(2,1)S(1)}, bf16[768,512]{1,0:T(8,128)(2,1)S(1)}, bf16[32,24,512]{2,1,0:T(8,128)(2,1)S(1)}, bf16[768,768]{1,0:T(8,128)(2,1)S(1)}) custom-call(s32[64]{0:T(128)S(1)} %compare_select_fusion.1.meta, bf16[512,768]{1,0:T(8,128)(2,1)S(1)} %get-tuple-element.126.att_ref.out_ref, ...), custom_call_target="tpu_custom_call" | custom-call | flops 2875000064 | tf_op jit(solution)/shard_map/mend/pallas_call | solution.py:727
  84.8 1.2 copy-done.9
  86.5 1.8 collective-permute-done.15.refs_4_
  88.3 1.1 collective-permute-done.16.refs_6_
  89.4 7.3 %ffn.2 = (f32[512,768]{1,0:T(8,128)S(1)}, f32[512,768]{1,0:T(8,128)S(1)}, f32[512,768]{1,0:T(8,128)S(1)}, f32[512,768]{1,0:T(8,128)S(1)}, bf16[8,384,128]{2,1,0:...) custom-call(s32[64]{0:T(128)S(1)} %compare_select_fusion.1.meta, bf16[512,768]{1,0:T(8,128)(2,1)S(1)} %get-tuple-element.132.refs_0_, ...), custom_call_target="tpu_custom_call" | custom-call | flops 2300000000 | tf_op jit(solution)/shard_map/ffn/pallas_call | solution.py:748
  96.9 4.2 %collective-permute-done.17 = bf16[8,768,128]{2,1,0:T(8,128)(2,1)S(1)} collective-permute-done((bf16[8,768,128]{2,1,0:T(8,128)(2,1)S(1)}, bf16[8,768,128]{2,1,0:T(8,128)(2,1)S(1)}, u32[]{:S(2)}, u32[]{:S(2)}) %collective-permute-start.17) | collective-permute-done | bytes 1572896 | tf_op jit(solution)/shard_map/ppermute | solution.py:240
  101.1 1.2 constant_dynamic-update-slice_fusion.35.refs_8_.refs_9_.refs_10_.refs_11_
  102.4 15.2 %ffn.3 = (f32[512,768]{1,0:T(8,128)S(1)}, f32[512,768]{1,0:T(8,128)S(1)}, bf16[1024,768]{1,0:T(8,128)(2,1)S(1)}, bf16[8,768,128]{2,1,0:T(8,128)(2,1)S(1)}, bf16[8,768,128]{2,1,0:T(8,128)(2,1)S(1)}) custom-call(s32[64]{0:T(128)S(1)} %compare_select_fusion.1.meta, bf16[512,768]{1,0:T(8,128)(2,1)S(1)} %get-tuple-element.132.refs_0_, ...), custom_call_target="tpu_custom_call" | custom-call | flops 17250000896 | tf_op jit(solution)/shard_map/ffn/pallas_call | solution.py:756
  118.0 3.1 %collective-permute-done.19.come_ref = bf16[1024,768]{1,0:T(8,128)(2,1)S(1)} collective-permute-done((bf16[1024,768]{1,0:T(8,128)(2,1)S(1)}, bf16[1024,768]{1,0:T(8,128)(2,1)S(1)}, u32[]{:S(2)}, u32[]{:S(2)}) %collective-permute-start.19) | collective-permute-done | bytes 1572896 | tf_op jit(solution)/shard_map/ppermute | solution.py:240
  121.1 4.0 %turn.1 = (bf16[512,768]{1,0:T(8,128)(2,1)}, f32[512,768]{1,0:T(8,128)S(1)}, bf16[512,768]{1,0:T(8,128)(2,1)S(1)}, f32[1,768]{1,0:T(1,128)S(1)}, bf16[16,144,128...) custom-call(s32[64]{0:T(128)S(1)} %compare_select_fusion.1.meta, f32[512,768]{1,0:T(8,128)S(1)} %get-tuple-element.144.grad_ref, ...), custom_call_target="tpu_custom_call" | custom-call | flops 4600000000 | tf_op jit(solution)/shard_map/turn/pallas_call | solution.py:768
  125.2 9.1 %attend_back.2 = (bf16[512,512]{1,0:T(8,128)(2,1)S(1)}, bf16[512,512]{1,0:T(8,128)(2,1)S(1)}, bf16[512,512]{1,0:T(8,128)(2,1)S(1)}, f32[8,512]{1,0:T(8,128)S(1)}...) custom-call(s32[64]{0:T(128)S(1)} %compare_select_fusion.1.meta, ...), custom_call_target="tpu_custom_call" | custom-call | flops 2300000000 | tf_op jit(solution)/shard_map/attend_back/pallas_call | solution.py:783
  134.6 1.9 weight.2
  136.5 1.7 collective-permute-done.21
  138.6 1.2 collective-permute-start.26
  139.8 4.4 %attend_back.3 = (bf16[512,256]{1,0:T(8,128)(2,1)S(1)}, bf16[512,256]{1,0:T(8,128)(2,1)S(1)}, bf16[512,256]{1,0:T(8,128)(2,1)S(1)}, f32[8,256]{1,0:T(8,128)S(1)}...) custom-call(s32[64]{0:T(128)S(1)} %compare_select_fusion.1.meta, ...), custom_call_target="tpu_custom_call" | custom-call | flops 1150000000 | tf_op jit(solution)/shard_map/attend_back/pallas_call | solution.py:783
  144.2 1.3 weight.3
  145.6 0.6 collective-permute-start.27
  146.5 1.0 collective-permute-start.25
  147.4 0.7 copy-done.8
  148.2 4.0 %last.1 = bf16[512,768]{1,0:T(8,128)(2,1)} custom-call(s32[64]{0:T(128)S(1)} %compare_select_fusion.1.meta, bf16[512,512]{1,0:T(8,128)(2,1)S(1)} %get-tuple-element.157.refs_0_, bf16[512,256]{1,0:T(8,128)(2,1)S(1)} %get-tuple-element.168.refs_7_.refs_1_, bf16[512,512]{1,0:T(8,128)(2,1)S(1)} %get-tuple-element.162.refs_1_.refs_2_, ...), custom_call_target="tpu_custom_call" | custom-call | flops 4600000000 | tf_op jit(solution)/shard_map/last/pallas_call | solution.py:824
  153.1 1.8 collective-permute-start.31
  155.0 1.8 collective-permute-start.30
  156.8 0.9 collective-permute-done.25
  157.9 2.3 %collective-permute-start.29 = (bf16[2,528,128]{2,1,0:T(8,128)(2,1)S(1)}, bf16[2,528,128]{2,1,0:T(8,128)(2,1)S(1)}, u32[]{:S(2)}, u32[]{:S(2)}) collective-permute-start(bf16[2,528,128]{2,1,0:T(8,128)(2,1)S(1)} %get-tuple-element.212), channel_id=1, source_target_pairs={{0,2},{1,3},{2,0},{3,1},{4,6},{5,7},{6,4},{7,5},{8,10},{9,11},{10,... | collective-permute-start | bytes 811016 | tf_op jit(solution)/shard_map/ppermute | solution.py:240
  160.3 2.1 %collective-permute-done.24 = bf16[8,24,1536]{2,1,0:T(8,128)(2,1)S(1)} collective-permute-done((bf16[8,24,1536]{2,1,0:T(8,128)(2,1)S(1)}, bf16[8,24,1536]{2,1,0:T(8,128)(2,1)S(1)}, u32[]{:S(2)}, u32[]{:S(2)}) %collective-permute-start.24) | collective-permute-done | bytes 589856 | tf_op jit(solution)/shard_map/ppermute | solution.py:240
  162.6 1.0 collective-permute-start.28
  163.5 3.0 %collective-permute-done.31 = bf16[8,24,896]{2,1,0:T(8,128)(2,1)S(1)} collective-permute-done((bf16[8,24,896]{2,1,0:T(8,128)(2,1)S(1)}, bf16[8,24,896]{2,1,0:T(8,128)(2,1)S(1)}, u32[]{:S(2)}, u32[]{:S(2)}) %collective-permute-start.31) | collective-permute-done | bytes 344096 | tf_op jit(solution)/shard_map/ppermute | solution.py:240
  166.6 0.8 collective-permute-start.34
  167.4 1.8 collective-permute-start.38
  169.2 4.0 %collective-permute-done.29 = bf16[2,528,128]{2,1,0:T(8,128)(2,1)S(1)} collective-permute-done((bf16[2,528,128]{2,1,0:T(8,128)(2,1)S(1)}, bf16[2,528,128]{2,1,0:T(8,128)(2,1)S(1)}, u32[]{:S(2)}, u32[]{:S(2)}) %collective-permute-start.29) | collective-permute-done | bytes 270368 | tf_op jit(solution)/shard_map/ppermute | solution.py:240
  173.5 1.8 collective-permute-start.32
  175.7 7.6 %collective-permute-done.38 = bf16[1,768,128]{2,1,0:T(8,128)(2,1)S(1)} collective-permute-done((bf16[1,768,128]{2,1,0:T(8,128)(2,1)S(1)}, bf16[1,768,128]{2,1,0:T(8,128)(2,1)S(1)}, u32[]{:S(2)}, u32[]{:S(2)}) %collective-permute-start.38) | collective-permute-done | bytes 196640 | tf_op jit(solution)/shard_map/ppermute | solution.py:240
  183.4 1.6 collective-permute-done.37
  185.2 2.1 %collective-permute-start.36 = (bf16[1,24,896]{2,1,0:T(8,128)(2,1)S(1)}, bf16[1,24,896]{2,1,0:T(8,128)(2,1)S(1)}, u32[]{:S(2)}, u32[]{:S(2)}) collective-permute-start(bf16[1,24,896]{2,1,0:T(8,128)(2,1)S(1)} %add_convert_fusion.25), channel_id=1, source_target_pairs={{0,4},{1,5},{2,6},{3,7},{4,0},{5,1},{6,2},{7,3},{8,12},{9,13},{10,... | collective-permute-start | bytes 129032 | tf_op jit(solution)/shard_map/ppermute | solution.py:240
  187.3 0.6 copy.23
  187.9 0.9 collective-permute-start.33
  188.9 1.3 collective-permute-done.36
  190.2 0.6 slice_bitcast_fusion
  191.3 2.3 %collective-permute-done.33 = bf16[1,24,1536]{2,1,0:T(8,128)(2,1)S(1)} collective-permute-done((bf16[1,24,1536]{2,1,0:T(8,128)(2,1)S(1)}, bf16[1,24,1536]{2,1,0:T(8,128)(2,1)S(1)}, u32[]{:S(2)}, u32[]{:S(2)}) %collective-permute-start.33) | collective-permute-done | bytes 73760 | tf_op jit(solution)/shard_map/ppermute | solution.py:240
  194.6 0.8 maximum_bitcast_fusion
  195.4 0.8 pad_maximum_fusion.3
  (125 shorter events, 10.6 us)
Async XLA Ops:
  2.3 9.8 %collective-permute-start = (bf16[1,24,2432]{2,1,0:T(8,128)(2,1)S(1)}, bf16[1,24,2432]{2,1,0:T(8,128)(2,1)S(1)}, u32[]{:S(2)}, u32[]{:S(2)}) collective-permute-start(bf16[1,24,2432]{2,1,0:T(8,128)(2,1)S(1)} %fusion.22), channel_id=1, source_target_pairs={{0,4},{1,5},{2,6},{3,7},{4,0},{5,1},{6,2},{7,3},{8,12},{9,13},{10,... | collective-permute-start | bytes 350216 | tf_op jit(solution)/shard_map/ppermute | solution.py:240
  6.4 1.1 copy-start.4
  7.5 1.1 copy-start.5
  8.6 0.8 copy-start.6
  12.1 6.9 %collective-permute-start.2 = (bf16[2,24,2432]{2,1,0:T(8,128)(2,1)S(1)}, bf16[2,24,2432]{2,1,0:T(8,128)(2,1)S(1)}, u32[]{:S(2)}, u32[]{:S(2)}) collective-permute-start(bf16[2,24,2432]{2,1,0:T(8,128)(2,1)S(1)} %pad_maximum_fusion.5), channel_id=1, source_target_pairs={{0,2},{1,3},{2,0},{3,1},{4,6},{5,7},{6,4},{7,5},{8,10},{9,11},{10,... | collective-permute-start | bytes 700424 | tf_op jit(solution)/shard_map/ppermute | solution.py:240
  19.1 10.6 %collective-permute-start.4 = (bf16[4,24,2432]{2,1,0:T(8,128)(2,1)S(1)}, bf16[4,24,2432]{2,1,0:T(8,128)(2,1)S(1)}, u32[]{:S(2)}, u32[]{:S(2)}) collective-permute-start(bf16[4,24,2432]{2,1,0:T(8,128)(2,1)S(1)} %get-tuple-element.255), channel_id=1, source_target_pairs={{0,1},{1,0},{2,3},{3,2},{4,5},{5,4},{6,7},{7,6},{8,24},{9,25},{10,... | collective-permute-start | bytes 1400840 | tf_op jit(solution)/shard_map/ppermute | solution.py:240
  20.5 9.2 %collective-permute-start.1 = (bf16[1,528,128]{2,1,0:T(8,128)(2,1)S(1)}, bf16[1,528,128]{2,1,0:T(8,128)(2,1)S(1)}, u32[]{:S(2)}, u32[]{:S(2)}) collective-permute-start(bf16[1,528,128]{2,1,0:T(8,128)(2,1)S(1)} %get-tuple-element.108), channel_id=1, source_target_pairs={{0,4},{1,5},{2,6},{3,7},{4,0},{5,1},{6,2},{7,3},{8,12},{9,13},{10,... | collective-permute-start | bytes 405512 | tf_op jit(solution)/shard_map/ppermute | solution.py:240
  29.9 13.8 %collective-permute-start.6 = (bf16[8,24,2432]{2,1,0:T(8,128)(2,1)S(1)}, bf16[8,24,2432]{2,1,0:T(8,128)(2,1)S(1)}, u32[]{:S(2)}, u32[]{:S(2)}) collective-permute-start(bf16[8,24,2432]{2,1,0:T(8,128)(2,1)S(1)} %get-tuple-element.230), channel_id=1, source_target_pairs={{0,16},{1,17},{2,18},{3,19},{4,20},{5,21},{6,22},{7,23},{8,9},{9,8... | collective-permute-start | bytes 2801672 | tf_op jit(solution)/shard_map/ppermute | solution.py:240
  30.5 12.9 %collective-permute-start.7 = (bf16[2,528,128]{2,1,0:T(8,128)(2,1)S(1)}, bf16[2,528,128]{2,1,0:T(8,128)(2,1)S(1)}, u32[]{:S(2)}, u32[]{:S(2)}) collective-permute-start(bf16[2,528,128]{2,1,0:T(8,128)(2,1)S(1)} %get-tuple-element.267), channel_id=1, source_target_pairs={{0,2},{1,3},{2,0},{3,1},{4,6},{5,7},{6,4},{7,5},{8,10},{9,11},{10,... | collective-permute-start | bytes 811016 | tf_op jit(solution)/shard_map/ppermute | solution.py:240
  31.2 10.9 %collective-permute-start.3 = (bf16[1,768,128]{2,1,0:T(8,128)(2,1)S(1)}, bf16[1,768,128]{2,1,0:T(8,128)(2,1)S(1)}, u32[]{:S(2)}, u32[]{:S(2)}) collective-permute-start(bf16[1,768,128]{2,1,0:T(8,128)(2,1)S(1)} %get-tuple-element.111), channel_id=1, source_target_pairs={{0,4},{1,5},{2,6},{3,7},{4,0},{5,1},{6,2},{7,3},{8,12},{9,13},{10,... | collective-permute-start | bytes 589832 | tf_op jit(solution)/shard_map/ppermute | solution.py:240
  43.5 3.3 %copy-start.2 = (bf16[1,512,768]{2,1,0:T(8,128)(2,1)S(1)}, bf16[1,512,768]{2,1,0:T(8,128)(2,1)}, u32[]{:S(2)}) copy-start(bf16[1,512,768]{2,1,0:T(8,128)(2,1)} %param.12) | copy-start | bytes 2359300
  43.8 12.7 %collective-permute-start.8 = (bf16[16,24,2432]{2,1,0:T(8,128)(2,1)S(1)}, bf16[16,24,2432]{2,1,0:T(8,128)(2,1)S(1)}, u32[]{:S(2)}, u32[]{:S(2)}) collective-permute-start(bf16[16,24,2432]{2,1,0:T(8,128)(2,1)S(1)} %constant_dynamic-update-slice_fusion.14.own_ref.few_own_ref), channel_id=1, source_target_pairs={{0,8},{1,9},{2,10},{3,11},{4,12},{5,13},{6,14},{7,15},{8,0},{9,1},... | collective-permute-start | bytes 5603336 | tf_op jit(solution)/shard_map/ppermute | solution.py:240
  43.9 12.6 %collective-permute-start.5 = (bf16[2,768,128]{2,1,0:T(8,128)(2,1)S(1)}, bf16[2,768,128]{2,1,0:T(8,128)(2,1)S(1)}, u32[]{:S(2)}, u32[]{:S(2)}) collective-permute-start(bf16[2,768,128]{2,1,0:T(8,128)(2,1)S(1)} %get-tuple-element.259), channel_id=1, source_target_pairs={{0,2},{1,3},{2,0},{3,1},{4,6},{5,7},{6,4},{7,5},{8,10},{9,11},{10,... | collective-permute-start | bytes 1179656 | tf_op jit(solution)/shard_map/ppermute | solution.py:240
  47.6 9.5 %copy-start.3 = (bf16[1,512,768]{2,1,0:T(8,128)(2,1)S(1)}, bf16[1,512,768]{2,1,0:T(8,128)(2,1)}, u32[]{:S(2)}) copy-start(bf16[1,512,768]{2,1,0:T(8,128)(2,1)} %param.10) | copy-start | bytes 2359300
  47.7 23.5 %collective-permute-start.12 = (bf16[768,512]{1,0:T(8,128)(2,1)S(1)}, bf16[768,512]{1,0:T(8,128)(2,1)S(1)}, u32[]{:S(2)}, u32[]{:S(2)}) collective-permute-start(bf16[768,512]{1,0:T(8,128)(2,1)S(1)} %get-tuple-element.124.refs_3_), channel_id=1, source_target_pairs={{0,8},{1,9},{2,10},{3,11},{4,12},{5,13},{6,14},{7,15},{8,0},{9,1},... | collective-permute-start | bytes 2359304 | tf_op jit(solution)/shard_map/ppermute | solution.py:240
  47.9 23.3 %collective-permute-start.11 = (bf16[512,768]{1,0:T(8,128)(2,1)S(1)}, bf16[512,768]{1,0:T(8,128)(2,1)S(1)}, u32[]{:S(2)}, u32[]{:S(2)}) collective-permute-start(bf16[512,768]{1,0:T(8,128)(2,1)S(1)} %get-tuple-element.123.refs_1_.go_ref), channel_id=1, source_target_pairs={{0,8},{1,9},{2,10},{3,11},{4,12},{5,13},{6,14},{7,15},{8,0},{9,1},... | collective-permute-start | bytes 2359304 | tf_op jit(solution)/shard_map/ppermute | solution.py:240
  48.2 16.1 %collective-permute-start.9 = (bf16[4,528,128]{2,1,0:T(8,128)(2,1)S(1)}, bf16[4,528,128]{2,1,0:T(8,128)(2,1)S(1)}, u32[]{:S(2)}, u32[]{:S(2)}) collective-permute-start(bf16[4,528,128]{2,1,0:T(8,128)(2,1)S(1)} %get-tuple-element.119), channel_id=1, source_target_pairs={{0,1},{1,0},{2,3},{3,2},{4,5},{5,4},{6,7},{7,6},{8,24},{9,25},{10,... | collective-permute-start | bytes 1622024 | tf_op jit(solution)/shard_map/ppermute | solution.py:240
  56.7 14.1 %collective-permute-start.10 = (bf16[4,768,128]{2,1,0:T(8,128)(2,1)S(1)}, bf16[4,768,128]{2,1,0:T(8,128)(2,1)S(1)}, u32[]{:S(2)}, u32[]{:S(2)}) collective-permute-start(bf16[4,768,128]{2,1,0:T(8,128)(2,1)S(1)} %get-tuple-element.237), channel_id=1, source_target_pairs={{0,1},{1,0},{2,3},{3,2},{4,5},{5,4},{6,7},{7,6},{8,24},{9,25},{10,... | collective-permute-start | bytes 2359304 | tf_op jit(solution)/shard_map/ppermute | solution.py:240
  64.4 6.7 %copy-start.7 = (bf16[768,2304]{1,0:T(8,128)(2,1)}, bf16[768,2304]{1,0:T(8,128)(2,1)S(1)}, u32[]{:S(2)}) copy-start(bf16[768,2304]{1,0:T(8,128)(2,1)S(1)} %get-tuple-element.171.refs_6_) | copy-start | bytes 10616836
  64.6 15.7 %collective-permute-start.13 = (bf16[8,528,128]{2,1,0:T(8,128)(2,1)S(1)}, bf16[8,528,128]{2,1,0:T(8,128)(2,1)S(1)}, u32[]{:S(2)}, u32[]{:S(2)}) collective-permute-start(bf16[8,528,128]{2,1,0:T(8,128)(2,1)S(1)} %get-tuple-element.228), channel_id=1, source_target_pairs={{0,16},{1,17},{2,18},{3,19},{4,20},{5,21},{6,22},{7,23},{8,9},{9,8... | collective-permute-start | bytes 3244040 | tf_op jit(solution)/shard_map/ppermute | solution.py:240
  71.1 9.2 %copy-start.13 = (bf16[16,768,128]{2,1,0:T(8,128)(2,1)}, bf16[16,768,128]{2,1,0:T(8,128)(2,1)S(1)}, u32[]{:S(2)}) copy-start(bf16[16,768,128]{2,1,0:T(8,128)(2,1)S(1)} %get-tuple-element.215) | copy-start | bytes 9437188
  80.5 2.1 %collective-permute-start.14 = (bf16[16,144,128]{2,1,0:T(8,128)(2,1)S(1)}, bf16[16,144,128]{2,1,0:T(8,128)(2,1)S(1)}, u32[]{:S(2)}, u32[]{:S(2)}) collective-permute-start(bf16[16,144,128]{2,1,0:T(8,128)(2,1)S(1)} %slice.363.own_ref), channel_id=1, source_target_pairs={{0,8},{1,9},{2,10},{3,11},{4,12},{5,13},{6,14},{7,15},{8,0},{9,1},... | collective-permute-start | bytes 1769480 | tf_op jit(solution)/shard_map/ppermute | solution.py:240
  80.6 20.5 %collective-permute-start.17 = (bf16[8,768,128]{2,1,0:T(8,128)(2,1)S(1)}, bf16[8,768,128]{2,1,0:T(8,128)(2,1)S(1)}, u32[]{:S(2)}, u32[]{:S(2)}) collective-permute-start(bf16[8,768,128]{2,1,0:T(8,128)(2,1)S(1)} %get-tuple-element.133), channel_id=1, source_target_pairs={{0,16},{1,17},{2,18},{3,19},{4,20},{5,21},{6,22},{7,23},{8,9},{9,8... | collective-permute-start | bytes 4718600 | tf_op jit(solution)/shard_map/ppermute | solution.py:240
  84.8 1.2 copy-start.9
  86.0 2.3 %collective-permute-start.15 = (bf16[512,768]{1,0:T(8,128)(2,1)S(1)}, bf16[512,768]{1,0:T(8,128)(2,1)S(1)}, u32[]{:S(2)}, u32[]{:S(2)}) collective-permute-start(bf16[512,768]{1,0:T(8,128)(2,1)S(1)} %get-tuple-element.132.refs_0_), channel_id=1, source_target_pairs={{0,8},{1,9},{2,10},{3,11},{4,12},{5,13},{6,14},{7,15},{8,0},{9,1},... | collective-permute-start | bytes 2359304 | tf_op jit(solution)/shard_map/ppermute | solution.py:240
  86.2 3.3 %collective-permute-start.16 = (bf16[768,512]{1,0:T(8,128)(2,1)S(1)}, bf16[768,512]{1,0:T(8,128)(2,1)S(1)}, u32[]{:S(2)}, u32[]{:S(2)}) collective-permute-start(bf16[768,512]{1,0:T(8,128)(2,1)S(1)} %get-tuple-element.130.refs_2_), channel_id=1, source_target_pairs={{0,8},{1,9},{2,10},{3,11},{4,12},{5,13},{6,14},{7,15},{8,0},{9,1},... | collective-permute-start | bytes 2359304 | tf_op jit(solution)/shard_map/ppermute | solution.py:240
  96.7 5.6 %copy-start = (f32[512,768]{1,0:T(8,128)}, f32[512,768]{1,0:T(8,128)S(1)}, u32[]{:S(2)}) copy-start(f32[512,768]{1,0:T(8,128)S(1)} %get-tuple-element.137.refs_14_) | copy-start | bytes 4718596
  96.7 5.6 %copy-start.1 = (f32[512,768]{1,0:T(8,128)}, f32[512,768]{1,0:T(8,128)S(1)}, u32[]{:S(2)}) copy-start(f32[512,768]{1,0:T(8,128)S(1)} %get-tuple-element.138.refs_15_) | copy-start | bytes 4718596
  96.7 20.9 %collective-permute-start.18 = (bf16[8,384,128]{2,1,0:T(8,128)(2,1)S(1)}, bf16[8,384,128]{2,1,0:T(8,128)(2,1)S(1)}, u32[]{:S(2)}, u32[]{:S(2)}) collective-permute-start(bf16[8,384,128]{2,1,0:T(8,128)(2,1)S(1)} %get-tuple-element.131), channel_id=1, source_target_pairs={{0,16},{1,17},{2,18},{3,19},{4,20},{5,21},{6,22},{7,23},{8,9},{9,8... | collective-permute-start | bytes 2359304 | tf_op jit(solution)/shard_map/ppermute | solution.py:240
  117.6 3.5 %copy-start.10 = (f32[512,768]{1,0:T(8,128)S(1)}, f32[512,768]{1,0:T(8,128)}, u32[]{:S(2)}) copy-start(f32[512,768]{1,0:T(8,128)} %copy-done.9) | copy-start | bytes 4718596
  117.6 3.5 %collective-permute-start.19 = (bf16[1024,768]{1,0:T(8,128)(2,1)S(1)}, bf16[1024,768]{1,0:T(8,128)(2,1)S(1)}, u32[]{:S(2)}, u32[]{:S(2)}) collective-permute-start(bf16[1024,768]{1,0:T(8,128)(2,1)S(1)} %get-tuple-element.146), channel_id=1, source_target_pairs={{0,8},{1,9},{2,10},{3,11},{4,12},{5,13},{6,14},{7,15},{8,0},{9,1},... | collective-permute-start | bytes 4718600 | tf_op jit(solution)/shard_map/ppermute | solution.py:240
  117.7 20.5 %collective-permute-start.21 = (bf16[8,768,128]{2,1,0:T(8,128)(2,1)S(1)}, bf16[8,768,128]{2,1,0:T(8,128)(2,1)S(1)}, u32[]{:S(2)}, u32[]{:S(2)}) collective-permute-start(bf16[8,768,128]{2,1,0:T(8,128)(2,1)S(1)} %get-tuple-element.140), channel_id=1, source_target_pairs={{0,16},{1,17},{2,18},{3,19},{4,20},{5,21},{6,22},{7,23},{8,9},{9,8... | collective-permute-start | bytes 4718600 | tf_op jit(solution)/shard_map/ppermute | solution.py:240
  125.1 9.2 %collective-permute-start.20 = (bf16[16,144,128]{2,1,0:T(8,128)(2,1)S(1)}, bf16[16,144,128]{2,1,0:T(8,128)(2,1)S(1)}, u32[]{:S(2)}, u32[]{:S(2)}) collective-permute-start(bf16[16,144,128]{2,1,0:T(8,128)(2,1)S(1)} %get-tuple-element.154), channel_id=1, source_target_pairs={{0,8},{1,9},{2,10},{3,11},{4,12},{5,13},{6,14},{7,15},{8,0},{9,1},... | collective-permute-start | bytes 1769480 | tf_op jit(solution)/shard_map/ppermute | solution.py:240
  134.5 11.8 %collective-permute-start.22 = (bf16[8,144,128]{2,1,0:T(8,128)(2,1)S(1)}, bf16[8,144,128]{2,1,0:T(8,128)(2,1)S(1)}, u32[]{:S(2)}, u32[]{:S(2)}) collective-permute-start(bf16[8,144,128]{2,1,0:T(8,128)(2,1)S(1)} %slice.364), channel_id=1, source_target_pairs={{0,16},{1,17},{2,18},{3,19},{4,20},{5,21},{6,22},{7,23},{8,9},{9,8... | collective-permute-start | bytes 884744 | tf_op jit(solution)/shard_map/ppermute | solution.py:240
  138.6 16.2 %collective-permute-start.26 = (bf16[4,768,128]{2,1,0:T(8,128)(2,1)S(1)}, bf16[4,768,128]{2,1,0:T(8,128)(2,1)S(1)}, u32[]{:S(2)}, u32[]{:S(2)}) collective-permute-start(bf16[4,768,128]{2,1,0:T(8,128)(2,1)S(1)} %get-tuple-element.200), channel_id=1, source_target_pairs={{0,1},{1,0},{2,3},{3,2},{4,5},{5,4},{6,7},{7,6},{8,24},{9,25},{10,... | collective-permute-start | bytes 2359304 | tf_op jit(solution)/shard_map/ppermute | solution.py:240
  139.8 12.4 %collective-permute-start.23 = (bf16[16,24,1536]{2,1,0:T(8,128)(2,1)S(1)}, bf16[16,24,1536]{2,1,0:T(8,128)(2,1)S(1)}, u32[]{:S(2)}, u32[]{:S(2)}) collective-permute-start(bf16[16,24,1536]{2,1,0:T(8,128)(2,1)S(1)} %bitcast.51), channel_id=1, source_target_pairs={{0,8},{1,9},{2,10},{3,11},{4,12},{5,13},{6,14},{7,15},{8,0},{9,1},... | collective-permute-start | bytes 3538952 | tf_op jit(solution)/shard_map/ppermute | solution.py:240
  145.6 7.3 %collective-permute-start.27 = (bf16[16,24,896]{2,1,0:T(8,128)(2,1)S(1)}, bf16[16,24,896]{2,1,0:T(8,128)(2,1)S(1)}, u32[]{:S(2)}, u32[]{:S(2)}) collective-permute-start(bf16[16,24,896]{2,1,0:T(8,128)(2,1)S(1)} %bitcast.56), channel_id=1, source_target_pairs={{0,8},{1,9},{2,10},{3,11},{4,12},{5,13},{6,14},{7,15},{8,0},{9,1},... | collective-permute-start | bytes 2064392 | tf_op jit(solution)/shard_map/ppermute | solution.py:240
  146.2 2.0 %copy-start.8 = (bf16[768,2304]{1,0:T(8,128)(2,1)S(1)}, bf16[768,2304]{1,0:T(8,128)(2,1)}, u32[]{:S(2)}) copy-start(bf16[768,2304]{1,0:T(8,128)(2,1)} %copy-done.7) | copy-start | bytes 10616836
  146.5 11.3 %collective-permute-start.25 = (bf16[4,528,128]{2,1,0:T(8,128)(2,1)S(1)}, bf16[4,528,128]{2,1,0:T(8,128)(2,1)S(1)}, u32[]{:S(2)}, u32[]{:S(2)}) collective-permute-start(bf16[4,528,128]{2,1,0:T(8,128)(2,1)S(1)} %pad_maximum_fusion), channel_id=1, source_target_pairs={{0,1},{1,0},{2,3},{3,2},{4,5},{5,4},{6,7},{7,6},{8,24},{9,25},{10,... | collective-permute-start | bytes 1622024 | tf_op jit(solution)/shard_map/ppermute | solution.py:240
  152.5 9.9 %collective-permute-start.24 = (bf16[8,24,1536]{2,1,0:T(8,128)(2,1)S(1)}, bf16[8,24,1536]{2,1,0:T(8,128)(2,1)S(1)}, u32[]{:S(2)}, u32[]{:S(2)}) collective-permute-start(bf16[8,24,1536]{2,1,0:T(8,128)(2,1)S(1)} %get-tuple-element.207), channel_id=1, source_target_pairs={{0,16},{1,17},{2,18},{3,19},{4,20},{5,21},{6,22},{7,23},{8,9},{9,8... | collective-permute-start | bytes 1769480 | tf_op jit(solution)/shard_map/ppermute | solution.py:240
  153.1 13.5 %collective-permute-start.31 = (bf16[8,24,896]{2,1,0:T(8,128)(2,1)S(1)}, bf16[8,24,896]{2,1,0:T(8,128)(2,1)S(1)}, u32[]{:S(2)}, u32[]{:S(2)}) collective-permute-start(bf16[8,24,896]{2,1,0:T(8,128)(2,1)S(1)} %get-tuple-element.220), channel_id=1, source_target_pairs={{0,16},{1,17},{2,18},{3,19},{4,20},{5,21},{6,22},{7,23},{8,9},{9,8... | collective-permute-start | bytes 1032200 | tf_op jit(solution)/shard_map/ppermute | solution.py:240
  155.0 12.3 %collective-permute-start.30 = (bf16[2,768,128]{2,1,0:T(8,128)(2,1)S(1)}, bf16[2,768,128]{2,1,0:T(8,128)(2,1)S(1)}, u32[]{:S(2)}, u32[]{:S(2)}) collective-permute-start(bf16[2,768,128]{2,1,0:T(8,128)(2,1)S(1)} %get-tuple-element.202), channel_id=1, source_target_pairs={{0,2},{1,3},{2,0},{3,1},{4,6},{5,7},{6,4},{7,5},{8,10},{9,11},{10,... | collective-permute-start | bytes 1179656 | tf_op jit(solution)/shard_map/ppermute | solution.py:240
  157.9 15.3 %collective-permute-start.29 = (bf16[2,528,128]{2,1,0:T(8,128)(2,1)S(1)}, bf16[2,528,128]{2,1,0:T(8,128)(2,1)S(1)}, u32[]{:S(2)}, u32[]{:S(2)}) collective-permute-start(bf16[2,528,128]{2,1,0:T(8,128)(2,1)S(1)} %get-tuple-element.212), channel_id=1, source_target_pairs={{0,2},{1,3},{2,0},{3,1},{4,6},{5,7},{6,4},{7,5},{8,10},{9,11},{10,... | collective-permute-start | bytes 811016 | tf_op jit(solution)/shard_map/ppermute | solution.py:240
  162.6 10.8 %collective-permute-start.28 = (bf16[4,24,1536]{2,1,0:T(8,128)(2,1)S(1)}, bf16[4,24,1536]{2,1,0:T(8,128)(2,1)S(1)}, u32[]{:S(2)}, u32[]{:S(2)}) collective-permute-start(bf16[4,24,1536]{2,1,0:T(8,128)(2,1)S(1)} %get-tuple-element.205), channel_id=1, source_target_pairs={{0,1},{1,0},{2,3},{3,2},{4,5},{5,4},{6,7},{7,6},{8,24},{9,25},{10,... | collective-permute-start | bytes 884744 | tf_op jit(solution)/shard_map/ppermute | solution.py:240
  166.6 8.7 %collective-permute-start.34 = (bf16[4,24,896]{2,1,0:T(8,128)(2,1)S(1)}, bf16[4,24,896]{2,1,0:T(8,128)(2,1)S(1)}, u32[]{:S(2)}, u32[]{:S(2)}) collective-permute-start(bf16[4,24,896]{2,1,0:T(8,128)(2,1)S(1)} %get-tuple-element.218), channel_id=1, source_target_pairs={{0,1},{1,0},{2,3},{3,2},{4,5},{5,4},{6,7},{7,6},{8,24},{9,25},{10,... | collective-permute-start | bytes 516104 | tf_op jit(solution)/shard_map/ppermute | solution.py:240
  167.4 15.9 %collective-permute-start.38 = (bf16[1,768,128]{2,1,0:T(8,128)(2,1)S(1)}, bf16[1,768,128]{2,1,0:T(8,128)(2,1)S(1)}, u32[]{:S(2)}, u32[]{:S(2)}) collective-permute-start(bf16[1,768,128]{2,1,0:T(8,128)(2,1)S(1)} %add_convert_fusion.12), channel_id=1, source_target_pairs={{0,4},{1,5},{2,6},{3,7},{4,0},{5,1},{6,2},{7,3},{8,12},{9,13},{10,... | collective-permute-start | bytes 589832 | tf_op jit(solution)/shard_map/ppermute | solution.py:240
  173.3 11.7 %collective-permute-start.37 = (bf16[1,528,128]{2,1,0:T(8,128)(2,1)S(1)}, bf16[1,528,128]{2,1,0:T(8,128)(2,1)S(1)}, u32[]{:S(2)}, u32[]{:S(2)}) collective-permute-start(bf16[1,528,128]{2,1,0:T(8,128)(2,1)S(1)} %add_convert_fusion.20), channel_id=1, source_target_pairs={{0,4},{1,5},{2,6},{3,7},{4,0},{5,1},{6,2},{7,3},{8,12},{9,13},{10,... | collective-permute-start | bytes 405512 | tf_op jit(solution)/shard_map/ppermute | solution.py:240
  173.5 11.6 %collective-permute-start.32 = (bf16[2,24,1536]{2,1,0:T(8,128)(2,1)S(1)}, bf16[2,24,1536]{2,1,0:T(8,128)(2,1)S(1)}, u32[]{:S(2)}, u32[]{:S(2)}) collective-permute-start(bf16[2,24,1536]{2,1,0:T(8,128)(2,1)S(1)} %get-tuple-element.226), channel_id=1, source_target_pairs={{0,2},{1,3},{2,0},{3,1},{4,6},{5,7},{6,4},{7,5},{8,10},{9,11},{10,... | collective-permute-start | bytes 442376 | tf_op jit(solution)/shard_map/ppermute | solution.py:240
  175.3 9.8 %collective-permute-start.35 = (bf16[2,24,896]{2,1,0:T(8,128)(2,1)S(1)}, bf16[2,24,896]{2,1,0:T(8,128)(2,1)S(1)}, u32[]{:S(2)}, u32[]{:S(2)}) collective-permute-start(bf16[2,24,896]{2,1,0:T(8,128)(2,1)S(1)} %get-tuple-element.238), channel_id=1, source_target_pairs={{0,2},{1,3},{2,0},{3,1},{4,6},{5,7},{6,4},{7,5},{8,10},{9,11},{10,... | collective-permute-start | bytes 258056 | tf_op jit(solution)/shard_map/ppermute | solution.py:240
  185.0 8.6 %copy-start.11 = (bf16[24,2304]{1,0:T(8,128)(2,1)S(1)}, bf16[24,2304]{1,0:T(8,128)(2,1)}, u32[]{:S(2)}) copy-start(bf16[24,2304]{1,0:T(8,128)(2,1)} %param.13) | copy-start | bytes 331780
  185.1 8.7 %copy-start.14 = (bf16[24]{0:T(256)(128)(2,1)S(1)}, bf16[24]{0:T(256)(128)(2,1)}, u32[]{:S(2)}) copy-start(bf16[24]{0:T(256)(128)(2,1)} %param.16) | copy-start | bytes 148
  185.2 5.0 %collective-permute-start.36 = (bf16[1,24,896]{2,1,0:T(8,128)(2,1)S(1)}, bf16[1,24,896]{2,1,0:T(8,128)(2,1)S(1)}, u32[]{:S(2)}, u32[]{:S(2)}) collective-permute-start(bf16[1,24,896]{2,1,0:T(8,128)(2,1)S(1)} %add_convert_fusion.25), channel_id=1, source_target_pairs={{0,4},{1,5},{2,6},{3,7},{4,0},{5,1},{6,2},{7,3},{8,12},{9,13},{10,... | collective-permute-start | bytes 129032 | tf_op jit(solution)/shard_map/ppermute | solution.py:240
  187.9 6.4 %collective-permute-start.39 = (f32[576,128]{1,0:T(8,128)S(1)}, f32[576,128]{1,0:T(8,128)S(1)}, u32[]{:S(2)}, u32[]{:S(2)}) collective-permute-start(f32[576,128]{1,0:T(8,128)S(1)} %pad_maximum_fusion.2), channel_id=1, source_target_pairs={{0,8},{1,9},{2,10},{3,11},{4,12},{5,13},{6,14},{7,15},{8,0},{9,1},... | collective-permute-start | bytes 884744 | tf_op jit(solution)/shard_map/ppermute | solution.py:240
  187.9 5.6 %collective-permute-start.33 = (bf16[1,24,1536]{2,1,0:T(8,128)(2,1)S(1)}, bf16[1,24,1536]{2,1,0:T(8,128)(2,1)S(1)}, u32[]{:S(2)}, u32[]{:S(2)}) collective-permute-start(bf16[1,24,1536]{2,1,0:T(8,128)(2,1)S(1)} %add_convert_fusion.23), channel_id=1, source_target_pairs={{0,4},{1,5},{2,6},{3,7},{4,0},{5,1},{6,2},{7,3},{8,12},{9,13},{10,... | collective-permute-start | bytes 221192 | tf_op jit(solution)/shard_map/ppermute | solution.py:240
  193.6 1.8 copy-start.12
where the time goes:
time: 197 us; the launch traced here: 196 us
  waiting for transfers between devices  72.8 us (37%)
  Pallas kernels  67.5 us (34%)
  starting transfers between devices  38 us (19%)
  local copies, waits for them, and re-layouts  10.2 us (5%)
  other arithmetic  5.78 us (3%)
  between operations  2 us (1%)
    ppermute x40, waiting for transfers between devices, send(): return lax.ppermute(array, AXES, flip_pairs(rule))  72.8 us
    ppermute x40, starting transfers between devices, send(): return lax.ppermute(array, AXES, flip_pairs(rule))  38 us
    pallas_call x1, Pallas kernels, own_sequence(): call(functools.partial(ffn_kernel, False), (4,), sequence_specs + [tile(w...  15.2 us
    pallas_call x2, Pallas kernels, attend_back(): call(attend_back_kernel, (count,), specs * 2 + tap_specs + [specs[0]] * 2...  13.5 us
    pallas_call x1, Pallas kernels, own_sequence(): call(attend_kernel, (groups,), part_specs, [lane_block, lse_spec], [shape...  9.19 us
    pallas_call x1, Pallas kernels, own_sequence(): call(functools.partial(ffn_kernel, True), (2,), sequence_specs + [tile(ha...  7.27 us
    pallas_call x1, Pallas kernels, own_sequence(): call(project_kernel, (wide // LANES,), [token, half_block, half_block, fe...  7.2 us
    unnamed x48, local copies, waits for them, and re-layouts  7.19 us
  transfers between devices with their start and end apart: 40, of which 21 were waited for; matrix products, arithmetic and copies ran while one was open for 4% of the time, Pallas kernels for 34%

commit v1 on v0

--- a/solution.py
+++ b/solution.py
@@ -821,31 +821,35 @@
     b_keep = jnp.concatenate([b_keep, out_keep], axis=1)
     b_go = jnp.concatenate([b_go, out_go], axis=1)
     b_sum = send(b_go, over_first)
+    x_keep, x_go = halved(x_keep, tie(x_sum, y_away))
+    x_sum = send(x_go, over_second)
+    a_keep, a_go = halved(a_keep, tie(a_sum, x_go))
+    a_sum = send(a_go, over_z(1))
     grad_inputs = call(
         last_kernel, (1,),
         [whole(g.shape) for g in grad_projected] + [whole((width, wide)), token, gain_spec, token],
         [token], [shape((seq, width), BF)], busy=4, name="last",
-    )(meta, *grad_projected, qkv_full, x, gains, tie(grad_residual, y_away, a_go, b_go))[0]
-    x_keep, x_go = halved(x_keep, tie(x_sum, grad_inputs))
-    x_sum = send(x_go, over_second)
-    y_keep, y_go = halved(y_keep, tie(y_sum, x_go))
+    )(meta, *grad_projected, qkv_full, x, gains, tie(grad_residual, y_away, a_go, b_go, x_go))[0]
+    y_keep, y_go = halved(y_keep, tie(y_sum, grad_inputs))
     y_sum = send(y_go, over_second)
-    a_keep, a_go = halved(a_keep, tie(a_sum, y_go))
-    a_sum = send(a_go, over_z(1))
-    b_keep, b_go = halved(b_keep, tie(b_sum, a_go))
+    b_keep, b_go = halved(b_keep, tie(b_sum, y_go))
     b_sum = send(b_go, over_z(1))
-    x_keep, x_go = halved(x_keep, tie(x_sum, b_go))
+    a_keep, a_go = halved(a_keep, tie(a_sum, b_go))
+    a_sum = send(a_go, over_z(2))
+    x_keep, x_go = halved(x_keep, tie(x_sum, a_go))
     x_sum = send(x_go, over_first)
     y_keep, y_go = halved(y_keep, tie(y_sum, x_go))
     y_sum = send(y_go, over_first)
-    a_keep, a_go = halved(a_keep, tie(a_sum, y_go))
-    a_sum = send(a_go, over_z(2))
-    b_keep, b_go = halved(b_keep, tie(b_sum, a_go))
+    b_keep, b_go = halved(b_keep, tie(b_sum, y_go))
     b_sum = send(b_go, over_z(2))
     x_keep, x_go = halved(x_keep, tie(x_sum, b_go))
     x_sum = send(x_go, over_z(1))
     y_keep, y_go = halved(y_keep, tie(y_sum, x_go))
     y_sum = send(y_go, over_z(1))
+    x_keep, x_go = halved(x_keep, tie(x_sum, y_go))
+    x_sum = send(x_go, over_z(2))
+    y_keep, y_go = halved(y_keep, tie(y_sum, x_go))
+    y_sum = send(y_go, over_z(2))
     grad_a = a_keep[0].astype(F32) + tie(a_sum, y_go)[0].astype(F32)
     grad_b = b_keep[0].astype(F32) + tie(b_sum, y_go)[0].astype(F32)
     grad_out_w = jnp.transpose(grad_b[half:].reshape(width // PART, rows, PART), (1, 0, 2)).reshape(rows, width)
@@ -871,10 +875,6 @@
         for i in range(2)
     )
 
-    x_keep, x_go = halved(x_keep, tie(x_sum, grad_a, grad_b))
-    x_sum = send(x_go, over_z(2))
-    y_keep, y_go = halved(y_keep, tie(y_sum, x_go))
-    y_sum = send(y_go, over_z(2))
     x_total = x_keep[0].astype(F32) + x_sum[0].astype(F32)
     y_total = y_keep[0].astype(F32) + y_sum[0].astype(F32)
     few = y_total[:8, 3 * LANES :]

time: 197 us -> 193 us (0.980)
  waiting for transfers between devices: 72.8 us -> 68.2 us
  starting transfers between devices: 38 us -> 40.1 us
    ppermute x40, waiting for transfers between devices: 72.8 us -> 68.2 us  [send(): return lax.ppermute(array, AXES, flip_pairs(rule))]
    ppermute x40, starting transfers between devices: 38 us -> 40.1 us  [send(): return lax.ppermute(array, AXES, flip_pairs(rule))]
  transfers between devices with their start and end apart: 40 -> 40, of which waited for: 21 -> 18; matrix products, arithmetic and copies ran while one was open for 4% -> 4% of each run, Pallas kernels for 34% -> 35%
where the time goes in v1:
time: 193 us
  waiting for transfers between devices  68.2 us (35%)
  Pallas kernels  67.5 us (35%)
  starting transfers between devices  40.1 us (21%)
  local copies, waits for them, and re-layouts  9.49 us (5%)
  other arithmetic  5.81 us (3%)
  between operations  1.98 us (1%)
    ppermute x40, waiting for transfers between devices, send(): return lax.ppermute(array, AXES, flip_pairs(rule))  68.2 us
    ppermute x40, starting transfers between devices, send(): return lax.ppermute(array, AXES, flip_pairs(rule))  40.1 us
    pallas_call x1, Pallas kernels, own_sequence(): call(functools.partial(ffn_kernel, False), (4,), sequence_specs + [tile(w...  15.2 us
    pallas_call x2, Pallas kernels, attend_back(): call(attend_back_kernel, (count,), specs * 2 + tap_specs + [specs[0]] * 2...  13.5 us
    pallas_call x1, Pallas kernels, own_sequence(): call(attend_kernel, (groups,), part_specs, [lane_block, lse_spec], [shape...  9.19 us
    pallas_call x1, Pallas kernels, own_sequence(): call(functools.partial(ffn_kernel, True), (2,), sequence_specs + [tile(ha...  7.27 us
    pallas_call x1, Pallas kernels, own_sequence(): call(project_kernel, (wide // LANES,), [token, half_block, half_block, fe...  7.2 us
    unnamed x48, local copies, waits for them, and re-layouts  6.46 us
  transfers between devices with their start and end apart: 40, of which 18 were waited for; matrix products, arithmetic and copies ran while one was open for 4% of the time, Pallas kernels for 35%

profile of v1, /device:TPU:0, one launch (start us, length us, event | category | flops | bytes accessed | tf_op | source)
XLA Modules:
  0.0 193.1 jit_solution(4930278234555140064)
XLA Ops:
  1.3 1.0 fusion.22
  2.3 4.1 %collective-permute-start = (bf16[1,24,2432]{2,1,0:T(8,128)(2,1)S(1)}, bf16[1,24,2432]{2,1,0:T(8,128)(2,1)S(1)}, u32[]{:S(2)}, u32[]{:S(2)}) collective-permute-start(bf16[1,24,2432]{2,1,0:T(8,128)(2,1)S(1)} %fusion.22), channel_id=1, source_target_pairs={{0,4},{1,5},{2,6},{3,7},{4,0},{5,1},{6,2},{7,3},{8,12},{9,13},{10,... | collective-permute-start | bytes 350216 | tf_op jit(solution)/shard_map/ppermute | solution.py:240
  6.5 1.1 copy-done.4
  7.5 1.1 copy-done.5
  8.6 0.8 copy-done.6
  9.3 0.8 pack.1
  10.2 1.9 %collective-permute-done = bf16[1,24,2432]{2,1,0:T(8,128)(2,1)S(1)} collective-permute-done((bf16[1,24,2432]{2,1,0:T(8,128)(2,1)S(1)}, bf16[1,24,2432]{2,1,0:T(8,128)(2,1)S(1)}, u32[]{:S(2)}, u32[]{:S(2)}) %collective-permute-start) | collective-permute-done | bytes 116768 | tf_op jit(solution)/shard_map/ppermute | solution.py:240
  12.1 0.8 collective-permute-start.2
  13.0 6.1 %collective-permute-done.2 = bf16[2,24,2432]{2,1,0:T(8,128)(2,1)S(1)} collective-permute-done((bf16[2,24,2432]{2,1,0:T(8,128)(2,1)S(1)}, bf16[2,24,2432]{2,1,0:T(8,128)(2,1)S(1)}, u32[]{:S(2)}, u32[]{:S(2)}) %collective-permute-start.2) | collective-permute-done | bytes 233504 | tf_op jit(solution)/shard_map/ppermute | solution.py:240
  19.1 1.3 collective-permute-start.4
  20.5 3.3 %collective-permute-start.1 = (bf16[1,528,128]{2,1,0:T(8,128)(2,1)S(1)}, bf16[1,528,128]{2,1,0:T(8,128)(2,1)S(1)}, u32[]{:S(2)}, u32[]{:S(2)}) collective-permute-start(bf16[1,528,128]{2,1,0:T(8,128)(2,1)S(1)} %get-tuple-element.109), channel_id=1, source_target_pairs={{0,4},{1,5},{2,6},{3,7},{4,0},{5,1},{6,2},{7,3},{8,12},{9,13},{10,... | collective-permute-start | bytes 405512 | tf_op jit(solution)/shard_map/ppermute | solution.py:240
  23.9 5.8 %collective-permute-done.1 = bf16[1,528,128]{2,1,0:T(8,128)(2,1)S(1)} collective-permute-done((bf16[1,528,128]{2,1,0:T(8,128)(2,1)S(1)}, bf16[1,528,128]{2,1,0:T(8,128)(2,1)S(1)}, u32[]{:S(2)}, u32[]{:S(2)}) %collective-permute-start.1) | collective-permute-done | bytes 135200 | tf_op jit(solution)/shard_map/ppermute | solution.py:240
  29.9 0.6 collective-permute-start.6
  30.5 0.7 collective-permute-start.7
  31.2 3.4 %collective-permute-start.3 = (bf16[1,768,128]{2,1,0:T(8,128)(2,1)S(1)}, bf16[1,768,128]{2,1,0:T(8,128)(2,1)S(1)}, u32[]{:S(2)}, u32[]{:S(2)}) collective-permute-start(bf16[1,768,128]{2,1,0:T(8,128)(2,1)S(1)} %get-tuple-element.112), channel_id=1, source_target_pairs={{0,4},{1,5},{2,6},{3,7},{4,0},{5,1},{6,2},{7,3},{8,12},{9,13},{10,... | collective-permute-start | bytes 589832 | tf_op jit(solution)/shard_map/ppermute | solution.py:240
  34.7 7.4 %collective-permute-done.3 = bf16[1,768,128]{2,1,0:T(8,128)(2,1)S(1)} collective-permute-done((bf16[1,768,128]{2,1,0:T(8,128)(2,1)S(1)}, bf16[1,768,128]{2,1,0:T(8,128)(2,1)S(1)}, u32[]{:S(2)}, u32[]{:S(2)}) %collective-permute-start.3) | collective-permute-done | bytes 196640 | tf_op jit(solution)/shard_map/ppermute | solution.py:240
  42.1 1.3 collective-permute-done.7
  43.9 2.9 %collective-permute-start.5 = (bf16[2,768,128]{2,1,0:T(8,128)(2,1)S(1)}, bf16[2,768,128]{2,1,0:T(8,128)(2,1)S(1)}, u32[]{:S(2)}, u32[]{:S(2)}) collective-permute-start(bf16[2,768,128]{2,1,0:T(8,128)(2,1)S(1)} %get-tuple-element.261), channel_id=1, source_target_pairs={{0,2},{1,3},{2,0},{3,1},{4,6},{5,7},{6,4},{7,5},{8,10},{9,11},{10,... | collective-permute-start | bytes 1179656 | tf_op jit(solution)/shard_map/ppermute | solution.py:240
  46.8 0.8 prepare.1
  48.6 7.9 %collective-permute-done.5 = bf16[2,768,128]{2,1,0:T(8,128)(2,1)S(1)} collective-permute-done((bf16[2,768,128]{2,1,0:T(8,128)(2,1)S(1)}, bf16[2,768,128]{2,1,0:T(8,128)(2,1)S(1)}, u32[]{:S(2)}, u32[]{:S(2)}) %collective-permute-start.5) | collective-permute-done | bytes 393248 | tf_op jit(solution)/shard_map/ppermute | solution.py:240
  57.2 7.2 %project.1 = (bf16[512,2304]{1,0:T(8,128)(2,1)S(1)}, bf16[512,2304]{1,0:T(8,128)(2,1)S(1)}, bf16[768,2304]{1,0:T(8,128)(2,1)S(1)}, bf16[32,24,512]{2,1,0:T(8,128...) custom-call(s32[64]{0:T(128)S(1)} %compare_select_fusion.1.meta, bf16[512,768]{1,0:T(8,128)(2,1)S(1)} %bitcast.53, ...), custom_call_target="tpu_custom_call" | custom-call | flops 8049999872 | tf_op jit(solution)/shard_map/project/pallas_call | solution.py:701
  64.6 0.5 collective-permute-start.13
  65.1 5.7 %collective-permute-done.10 = bf16[4,768,128]{2,1,0:T(8,128)(2,1)S(1)} collective-permute-done((bf16[4,768,128]{2,1,0:T(8,128)(2,1)S(1)}, bf16[4,768,128]{2,1,0:T(8,128)(2,1)S(1)}, u32[]{:S(2)}, u32[]{:S(2)}) %collective-permute-start.10) | collective-permute-done | bytes 786464 | tf_op jit(solution)/shard_map/ppermute | solution.py:240
  71.1 9.2 %attend.1 = (bf16[512,768]{1,0:T(8,128)(2,1)S(1)}, f32[3,8,512]{2,1,0:T(8,128)S(1)}) custom-call(s32[64]{0:T(128)S(1)} %compare_select_fusion.1.meta, bf16[512,2304]{1,0:T(8,128)(2,1)S(1)} %get-tuple-element.126.q_ref.k_ref.v_ref, bf16[512,2304]{1,0:T(8,128)(2,1)S(1)} %get-tuple-element.126.q_ref.k_ref.v_ref, ...), custom_call_target="tpu_custom_call" | custom-call | flops 10350000128 | tf_op jit(solution)/shard_map/attend/pallas_call | solution.py:717
  80.7 1.9 collective-permute-done.14.other_ref
  82.6 2.2 %mend.1 = (f32[512,768]{1,0:T(8,128)S(1)}, bf16[512,768]{1,0:T(8,128)(2,1)S(1)}, bf16[768,512]{1,0:T(8,128)(2,1)S(1)}, bf16[32,24,512]{2,1,0:T(8,128)(2,1)S(1)}, bf16[768,768]{1,0:T(8,128)(2,1)S(1)}) custom-call(s32[64]{0:T(128)S(1)} %compare_select_fusion.1.meta, bf16[512,768]{1,0:T(8,128)(2,1)S(1)} %get-tuple-element.127.att_ref.out_ref, ...), custom_call_target="tpu_custom_call" | custom-call | flops 2875000064 | tf_op jit(solution)/shard_map/mend/pallas_call | solution.py:727
  84.8 1.2 copy-done.9
  86.5 1.8 collective-permute-done.15.refs_4_
  88.3 1.1 collective-permute-done.16.refs_6_
  89.4 7.3 %ffn.2 = (f32[512,768]{1,0:T(8,128)S(1)}, f32[512,768]{1,0:T(8,128)S(1)}, f32[512,768]{1,0:T(8,128)S(1)}, f32[512,768]{1,0:T(8,128)S(1)}, bf16[8,384,128]{2,1,0:...) custom-call(s32[64]{0:T(128)S(1)} %compare_select_fusion.1.meta, bf16[512,768]{1,0:T(8,128)(2,1)S(1)} %get-tuple-element.133.refs_0_, ...), custom_call_target="tpu_custom_call" | custom-call | flops 2300000000 | tf_op jit(solution)/shard_map/ffn/pallas_call | solution.py:748
  96.9 4.2 %collective-permute-done.17 = bf16[8,768,128]{2,1,0:T(8,128)(2,1)S(1)} collective-permute-done((bf16[8,768,128]{2,1,0:T(8,128)(2,1)S(1)}, bf16[8,768,128]{2,1,0:T(8,128)(2,1)S(1)}, u32[]{:S(2)}, u32[]{:S(2)}) %collective-permute-start.17) | collective-permute-done | bytes 1572896 | tf_op jit(solution)/shard_map/ppermute | solution.py:240
  101.1 1.2 constant_dynamic-update-slice_fusion.35.refs_8_.refs_9_.refs_10_.refs_11_
  102.4 15.2 %ffn.3 = (f32[512,768]{1,0:T(8,128)S(1)}, f32[512,768]{1,0:T(8,128)S(1)}, bf16[1024,768]{1,0:T(8,128)(2,1)S(1)}, bf16[8,768,128]{2,1,0:T(8,128)(2,1)S(1)}, bf16[8,768,128]{2,1,0:T(8,128)(2,1)S(1)}) custom-call(s32[64]{0:T(128)S(1)} %compare_select_fusion.1.meta, bf16[512,768]{1,0:T(8,128)(2,1)S(1)} %get-tuple-element.133.refs_0_, ...), custom_call_target="tpu_custom_call" | custom-call | flops 17250000896 | tf_op jit(solution)/shard_map/ffn/pallas_call | solution.py:756
  118.0 3.1 %collective-permute-done.19.come_ref = bf16[1024,768]{1,0:T(8,128)(2,1)S(1)} collective-permute-done((bf16[1024,768]{1,0:T(8,128)(2,1)S(1)}, bf16[1024,768]{1,0:T(8,128)(2,1)S(1)}, u32[]{:S(2)}, u32[]{:S(2)}) %collective-permute-start.19) | collective-permute-done | bytes 1572896 | tf_op jit(solution)/shard_map/ppermute | solution.py:240
  121.1 4.0 %turn.1 = (bf16[512,768]{1,0:T(8,128)(2,1)}, f32[512,768]{1,0:T(8,128)S(1)}, bf16[512,768]{1,0:T(8,128)(2,1)S(1)}, f32[1,768]{1,0:T(1,128)S(1)}, bf16[16,144,128...) custom-call(s32[64]{0:T(128)S(1)} %compare_select_fusion.1.meta, f32[512,768]{1,0:T(8,128)S(1)} %get-tuple-element.145.grad_ref, ...), custom_call_target="tpu_custom_call" | custom-call | flops 4600000000 | tf_op jit(solution)/shard_map/turn/pallas_call | solution.py:768
  125.2 9.1 %attend_back.2 = (bf16[512,512]{1,0:T(8,128)(2,1)S(1)}, bf16[512,512]{1,0:T(8,128)(2,1)S(1)}, bf16[512,512]{1,0:T(8,128)(2,1)S(1)}, f32[8,512]{1,0:T(8,128)S(1)}...) custom-call(s32[64]{0:T(128)S(1)} %compare_select_fusion.1.meta, ...), custom_call_target="tpu_custom_call" | custom-call | flops 2300000000 | tf_op jit(solution)/shard_map/attend_back/pallas_call | solution.py:783
  134.6 1.9 weight.2
  136.5 1.7 collective-permute-done.21
  138.6 1.2 collective-permute-start.22
  139.8 4.4 %attend_back.3 = (bf16[512,256]{1,0:T(8,128)(2,1)S(1)}, bf16[512,256]{1,0:T(8,128)(2,1)S(1)}, bf16[512,256]{1,0:T(8,128)(2,1)S(1)}, f32[8,256]{1,0:T(8,128)S(1)}...) custom-call(s32[64]{0:T(128)S(1)} %compare_select_fusion.1.meta, ...), custom_call_target="tpu_custom_call" | custom-call | flops 1150000000 | tf_op jit(solution)/shard_map/attend_back/pallas_call | solution.py:783
  144.2 1.3 weight.3
  145.6 0.6 collective-permute-start.28
  146.5 1.0 collective-permute-start.27
  148.1 3.6 %collective-permute-done.22 = bf16[4,768,128]{2,1,0:T(8,128)(2,1)S(1)} collective-permute-done((bf16[4,768,128]{2,1,0:T(8,128)(2,1)S(1)}, bf16[4,768,128]{2,1,0:T(8,128)(2,1)S(1)}, u32[]{:S(2)}, u32[]{:S(2)}) %collective-permute-start.22) | collective-permute-done | bytes 786464 | tf_op jit(solution)/shard_map/ppermute | solution.py:240
  152.0 2.2 %collective-permute-start.26 = (bf16[2,768,128]{2,1,0:T(8,128)(2,1)S(1)}, bf16[2,768,128]{2,1,0:T(8,128)(2,1)S(1)}, u32[]{:S(2)}, u32[]{:S(2)}) collective-permute-start(bf16[2,768,128]{2,1,0:T(8,128)(2,1)S(1)} %get-tuple-element.206), channel_id=1, source_target_pairs={{0,2},{1,3},{2,0},{3,1},{4,6},{5,7},{6,4},{7,5},{8,10},{9,11},{10,... | collective-permute-start | bytes 1179656 | tf_op jit(solution)/shard_map/ppermute | solution.py:240
  154.2 4.0 %last.1 = bf16[512,768]{1,0:T(8,128)(2,1)} custom-call(s32[64]{0:T(128)S(1)} %compare_select_fusion.1.meta, bf16[512,512]{1,0:T(8,128)(2,1)S(1)} %get-tuple-element.158.refs_0_, bf16[512,256]{1,0:T(8,128)(2,1)S(1)} %get-tuple-element.169.refs_7_.refs_1_, bf16[512,512]{1,0:T(8,128)(2,1)S(1)} %get-tuple-element.163.refs_1_.refs_2_, ...), custom_call_target="tpu_custom_call" | custom-call | flops 4600000000 | tf_op jit(solution)/shard_map/last/pallas_call | solution.py:828
  158.5 4.9 %collective-permute-done.27 = bf16[4,528,128]{2,1,0:T(8,128)(2,1)S(1)} collective-permute-done((bf16[4,528,128]{2,1,0:T(8,128)(2,1)S(1)}, bf16[4,528,128]{2,1,0:T(8,128)(2,1)S(1)}, u32[]{:S(2)}, u32[]{:S(2)}) %collective-permute-start.27) | collective-permute-done | bytes 540704 | tf_op jit(solution)/shard_map/ppermute | solution.py:240
  163.5 2.2 %collective-permute-start.30 = (bf16[2,528,128]{2,1,0:T(8,128)(2,1)S(1)}, bf16[2,528,128]{2,1,0:T(8,128)(2,1)S(1)}, u32[]{:S(2)}, u32[]{:S(2)}) collective-permute-start(bf16[2,528,128]{2,1,0:T(8,128)(2,1)S(1)} %get-tuple-element.214), channel_id=1, source_target_pairs={{0,2},{1,3},{2,0},{3,1},{4,6},{5,7},{6,4},{7,5},{8,10},{9,11},{10,... | collective-permute-start | bytes 811016 | tf_op jit(solution)/shard_map/ppermute | solution.py:240
  165.8 1.8 collective-permute-start.38
  167.7 0.8 collective-permute-start.29
  168.6 1.4 collective-permute-start.33
  170.0 2.7 %collective-permute-done.30 = bf16[2,528,128]{2,1,0:T(8,128)(2,1)S(1)} collective-permute-done((bf16[2,528,128]{2,1,0:T(8,128)(2,1)S(1)}, bf16[2,528,128]{2,1,0:T(8,128)(2,1)S(1)}, u32[]{:S(2)}, u32[]{:S(2)}) %collective-permute-start.30) | collective-permute-done | bytes 270368 | tf_op jit(solution)/shard_map/ppermute | solution.py:240
  172.7 2.6 %collective-permute-start.37 = (bf16[1,528,128]{2,1,0:T(8,128)(2,1)S(1)}, bf16[1,528,128]{2,1,0:T(8,128)(2,1)S(1)}, u32[]{:S(2)}, u32[]{:S(2)}) collective-permute-start(bf16[1,528,128]{2,1,0:T(8,128)(2,1)S(1)} %add_convert_fusion.20), channel_id=1, source_target_pairs={{0,4},{1,5},{2,6},{3,7},{4,0},{5,1},{6,2},{7,3},{8,12},{9,13},{10,... | collective-permute-start | bytes 405512 | tf_op jit(solution)/shard_map/ppermute | solution.py:240
  175.4 2.6 %collective-permute-start.32 = (bf16[2,24,1536]{2,1,0:T(8,128)(2,1)S(1)}, bf16[2,24,1536]{2,1,0:T(8,128)(2,1)S(1)}, u32[]{:S(2)}, u32[]{:S(2)}) collective-permute-start(bf16[2,24,1536]{2,1,0:T(8,128)(2,1)S(1)} %get-tuple-element.227), channel_id=1, source_target_pairs={{0,2},{1,3},{2,0},{3,1},{4,6},{5,7},{6,4},{7,5},{8,10},{9,11},{10,... | collective-permute-start | bytes 442376 | tf_op jit(solution)/shard_map/ppermute | solution.py:240
  178.1 4.0 %collective-permute-done.32 = bf16[2,24,1536]{2,1,0:T(8,128)(2,1)S(1)} collective-permute-done((bf16[2,24,1536]{2,1,0:T(8,128)(2,1)S(1)}, bf16[2,24,1536]{2,1,0:T(8,128)(2,1)S(1)}, u32[]{:S(2)}, u32[]{:S(2)}) %collective-permute-start.32) | collective-permute-done | bytes 147488 | tf_op jit(solution)/shard_map/ppermute | solution.py:240
  182.1 1.7 collective-permute-start.34
  183.8 1.4 collective-permute-start.36
  185.5 0.6 copy.23
  186.2 3.1 %collective-permute-done.36 = bf16[1,24,896]{2,1,0:T(8,128)(2,1)S(1)} collective-permute-done((bf16[1,24,896]{2,1,0:T(8,128)(2,1)S(1)}, bf16[1,24,896]{2,1,0:T(8,128)(2,1)S(1)}, u32[]{:S(2)}, u32[]{:S(2)}) %collective-permute-start.36) | collective-permute-done | bytes 43040 | tf_op jit(solution)/shard_map/ppermute | solution.py:240
  189.3 0.6 slice_bitcast_fusion
  189.9 0.5 slice_bitcast_fusion.1
  190.7 0.5 convert_divide_fusion
  191.5 0.8 maximum_bitcast_fusion
  192.3 0.8 pad_maximum_fusion.3
  (125 shorter events, 8.3 us)
Async XLA Ops:
  2.3 9.8 %collective-permute-start = (bf16[1,24,2432]{2,1,0:T(8,128)(2,1)S(1)}, bf16[1,24,2432]{2,1,0:T(8,128)(2,1)S(1)}, u32[]{:S(2)}, u32[]{:S(2)}) collective-permute-start(bf16[1,24,2432]{2,1,0:T(8,128)(2,1)S(1)} %fusion.22), channel_id=1, source_target_pairs={{0,4},{1,5},{2,6},{3,7},{4,0},{5,1},{6,2},{7,3},{8,12},{9,13},{10,... | collective-permute-start | bytes 350216 | tf_op jit(solution)/shard_map/ppermute | solution.py:240
  6.4 1.1 copy-start.4
  7.5 1.1 copy-start.5
  8.6 0.8 copy-start.6
  12.1 6.9 %collective-permute-start.2 = (bf16[2,24,2432]{2,1,0:T(8,128)(2,1)S(1)}, bf16[2,24,2432]{2,1,0:T(8,128)(2,1)S(1)}, u32[]{:S(2)}, u32[]{:S(2)}) collective-permute-start(bf16[2,24,2432]{2,1,0:T(8,128)(2,1)S(1)} %pad_maximum_fusion.5), channel_id=1, source_target_pairs={{0,2},{1,3},{2,0},{3,1},{4,6},{5,7},{6,4},{7,5},{8,10},{9,11},{10,... | collective-permute-start | bytes 700424 | tf_op jit(solution)/shard_map/ppermute | solution.py:240
  19.1 10.6 %collective-permute-start.4 = (bf16[4,24,2432]{2,1,0:T(8,128)(2,1)S(1)}, bf16[4,24,2432]{2,1,0:T(8,128)(2,1)S(1)}, u32[]{:S(2)}, u32[]{:S(2)}) collective-permute-start(bf16[4,24,2432]{2,1,0:T(8,128)(2,1)S(1)} %get-tuple-element.257), channel_id=1, source_target_pairs={{0,1},{1,0},{2,3},{3,2},{4,5},{5,4},{6,7},{7,6},{8,24},{9,25},{10,... | collective-permute-start | bytes 1400840 | tf_op jit(solution)/shard_map/ppermute | solution.py:240
  20.5 9.2 %collective-permute-start.1 = (bf16[1,528,128]{2,1,0:T(8,128)(2,1)S(1)}, bf16[1,528,128]{2,1,0:T(8,128)(2,1)S(1)}, u32[]{:S(2)}, u32[]{:S(2)}) collective-permute-start(bf16[1,528,128]{2,1,0:T(8,128)(2,1)S(1)} %get-tuple-element.109), channel_id=1, source_target_pairs={{0,4},{1,5},{2,6},{3,7},{4,0},{5,1},{6,2},{7,3},{8,12},{9,13},{10,... | collective-permute-start | bytes 405512 | tf_op jit(solution)/shard_map/ppermute | solution.py:240
  29.9 13.8 %collective-permute-start.6 = (bf16[8,24,2432]{2,1,0:T(8,128)(2,1)S(1)}, bf16[8,24,2432]{2,1,0:T(8,128)(2,1)S(1)}, u32[]{:S(2)}, u32[]{:S(2)}) collective-permute-start(bf16[8,24,2432]{2,1,0:T(8,128)(2,1)S(1)} %get-tuple-element.232), channel_id=1, source_target_pairs={{0,16},{1,17},{2,18},{3,19},{4,20},{5,21},{6,22},{7,23},{8,9},{9,8... | collective-permute-start | bytes 2801672 | tf_op jit(solution)/shard_map/ppermute | solution.py:240
  30.5 12.9 %collective-permute-start.7 = (bf16[2,528,128]{2,1,0:T(8,128)(2,1)S(1)}, bf16[2,528,128]{2,1,0:T(8,128)(2,1)S(1)}, u32[]{:S(2)}, u32[]{:S(2)}) collective-permute-start(bf16[2,528,128]{2,1,0:T(8,128)(2,1)S(1)} %get-tuple-element.269), channel_id=1, source_target_pairs={{0,2},{1,3},{2,0},{3,1},{4,6},{5,7},{6,4},{7,5},{8,10},{9,11},{10,... | collective-permute-start | bytes 811016 | tf_op jit(solution)/shard_map/ppermute | solution.py:240
  31.2 10.9 %collective-permute-start.3 = (bf16[1,768,128]{2,1,0:T(8,128)(2,1)S(1)}, bf16[1,768,128]{2,1,0:T(8,128)(2,1)S(1)}, u32[]{:S(2)}, u32[]{:S(2)}) collective-permute-start(bf16[1,768,128]{2,1,0:T(8,128)(2,1)S(1)} %get-tuple-element.112), channel_id=1, source_target_pairs={{0,4},{1,5},{2,6},{3,7},{4,0},{5,1},{6,2},{7,3},{8,12},{9,13},{10,... | collective-permute-start | bytes 589832 | tf_op jit(solution)/shard_map/ppermute | solution.py:240
  43.5 3.3 %copy-start.2 = (bf16[1,512,768]{2,1,0:T(8,128)(2,1)S(1)}, bf16[1,512,768]{2,1,0:T(8,128)(2,1)}, u32[]{:S(2)}) copy-start(bf16[1,512,768]{2,1,0:T(8,128)(2,1)} %param.12) | copy-start | bytes 2359300
  43.8 12.7 %collective-permute-start.8 = (bf16[16,24,2432]{2,1,0:T(8,128)(2,1)S(1)}, bf16[16,24,2432]{2,1,0:T(8,128)(2,1)S(1)}, u32[]{:S(2)}, u32[]{:S(2)}) collective-permute-start(bf16[16,24,2432]{2,1,0:T(8,128)(2,1)S(1)} %constant_dynamic-update-slice_fusion.14.own_ref.few_own_ref), channel_id=1, source_target_pairs={{0,8},{1,9},{2,10},{3,11},{4,12},{5,13},{6,14},{7,15},{8,0},{9,1},... | collective-permute-start | bytes 5603336 | tf_op jit(solution)/shard_map/ppermute | solution.py:240
  43.9 12.6 %collective-permute-start.5 = (bf16[2,768,128]{2,1,0:T(8,128)(2,1)S(1)}, bf16[2,768,128]{2,1,0:T(8,128)(2,1)S(1)}, u32[]{:S(2)}, u32[]{:S(2)}) collective-permute-start(bf16[2,768,128]{2,1,0:T(8,128)(2,1)S(1)} %get-tuple-element.261), channel_id=1, source_target_pairs={{0,2},{1,3},{2,0},{3,1},{4,6},{5,7},{6,4},{7,5},{8,10},{9,11},{10,... | collective-permute-start | bytes 1179656 | tf_op jit(solution)/shard_map/ppermute | solution.py:240
  47.6 9.5 %copy-start.3 = (bf16[1,512,768]{2,1,0:T(8,128)(2,1)S(1)}, bf16[1,512,768]{2,1,0:T(8,128)(2,1)}, u32[]{:S(2)}) copy-start(bf16[1,512,768]{2,1,0:T(8,128)(2,1)} %param.10) | copy-start | bytes 2359300
  47.7 23.5 %collective-permute-start.12 = (bf16[768,512]{1,0:T(8,128)(2,1)S(1)}, bf16[768,512]{1,0:T(8,128)(2,1)S(1)}, u32[]{:S(2)}, u32[]{:S(2)}) collective-permute-start(bf16[768,512]{1,0:T(8,128)(2,1)S(1)} %get-tuple-element.125.refs_3_), channel_id=1, source_target_pairs={{0,8},{1,9},{2,10},{3,11},{4,12},{5,13},{6,14},{7,15},{8,0},{9,1},... | collective-permute-start | bytes 2359304 | tf_op jit(solution)/shard_map/ppermute | solution.py:240
  47.9 23.3 %collective-permute-start.11 = (bf16[512,768]{1,0:T(8,128)(2,1)S(1)}, bf16[512,768]{1,0:T(8,128)(2,1)S(1)}, u32[]{:S(2)}, u32[]{:S(2)}) collective-permute-start(bf16[512,768]{1,0:T(8,128)(2,1)S(1)} %get-tuple-element.124.refs_1_.go_ref), channel_id=1, source_target_pairs={{0,8},{1,9},{2,10},{3,11},{4,12},{5,13},{6,14},{7,15},{8,0},{9,1},... | collective-permute-start | bytes 2359304 | tf_op jit(solution)/shard_map/ppermute | solution.py:240
  48.2 16.1 %collective-permute-start.9 = (bf16[4,528,128]{2,1,0:T(8,128)(2,1)S(1)}, bf16[4,528,128]{2,1,0:T(8,128)(2,1)S(1)}, u32[]{:S(2)}, u32[]{:S(2)}) collective-permute-start(bf16[4,528,128]{2,1,0:T(8,128)(2,1)S(1)} %get-tuple-element.120), channel_id=1, source_target_pairs={{0,1},{1,0},{2,3},{3,2},{4,5},{5,4},{6,7},{7,6},{8,24},{9,25},{10,... | collective-permute-start | bytes 1622024 | tf_op jit(solution)/shard_map/ppermute | solution.py:240
  56.7 14.1 %collective-permute-start.10 = (bf16[4,768,128]{2,1,0:T(8,128)(2,1)S(1)}, bf16[4,768,128]{2,1,0:T(8,128)(2,1)S(1)}, u32[]{:S(2)}, u32[]{:S(2)}) collective-permute-start(bf16[4,768,128]{2,1,0:T(8,128)(2,1)S(1)} %get-tuple-element.239), channel_id=1, source_target_pairs={{0,1},{1,0},{2,3},{3,2},{4,5},{5,4},{6,7},{7,6},{8,24},{9,25},{10,... | collective-permute-start | bytes 2359304 | tf_op jit(solution)/shard_map/ppermute | solution.py:240
  64.4 6.7 %copy-start.7 = (bf16[768,2304]{1,0:T(8,128)(2,1)}, bf16[768,2304]{1,0:T(8,128)(2,1)S(1)}, u32[]{:S(2)}) copy-start(bf16[768,2304]{1,0:T(8,128)(2,1)S(1)} %get-tuple-element.172.refs_6_) | copy-start | bytes 10616836
  64.6 15.7 %collective-permute-start.13 = (bf16[8,528,128]{2,1,0:T(8,128)(2,1)S(1)}, bf16[8,528,128]{2,1,0:T(8,128)(2,1)S(1)}, u32[]{:S(2)}, u32[]{:S(2)}) collective-permute-start(bf16[8,528,128]{2,1,0:T(8,128)(2,1)S(1)} %get-tuple-element.230), channel_id=1, source_target_pairs={{0,16},{1,17},{2,18},{3,19},{4,20},{5,21},{6,22},{7,23},{8,9},{9,8... | collective-permute-start | bytes 3244040 | tf_op jit(solution)/shard_map/ppermute | solution.py:240
  71.1 9.2 %copy-start.13 = (bf16[16,768,128]{2,1,0:T(8,128)(2,1)}, bf16[16,768,128]{2,1,0:T(8,128)(2,1)S(1)}, u32[]{:S(2)}) copy-start(bf16[16,768,128]{2,1,0:T(8,128)(2,1)S(1)} %get-tuple-element.217) | copy-start | bytes 9437188
  80.5 2.1 %collective-permute-start.14 = (bf16[16,144,128]{2,1,0:T(8,128)(2,1)S(1)}, bf16[16,144,128]{2,1,0:T(8,128)(2,1)S(1)}, u32[]{:S(2)}, u32[]{:S(2)}) collective-permute-start(bf16[16,144,128]{2,1,0:T(8,128)(2,1)S(1)} %slice.363.own_ref), channel_id=1, source_target_pairs={{0,8},{1,9},{2,10},{3,11},{4,12},{5,13},{6,14},{7,15},{8,0},{9,1},... | collective-permute-start | bytes 1769480 | tf_op jit(solution)/shard_map/ppermute | solution.py:240
  80.6 20.5 %collective-permute-start.17 = (bf16[8,768,128]{2,1,0:T(8,128)(2,1)S(1)}, bf16[8,768,128]{2,1,0:T(8,128)(2,1)S(1)}, u32[]{:S(2)}, u32[]{:S(2)}) collective-permute-start(bf16[8,768,128]{2,1,0:T(8,128)(2,1)S(1)} %get-tuple-element.134), channel_id=1, source_target_pairs={{0,16},{1,17},{2,18},{3,19},{4,20},{5,21},{6,22},{7,23},{8,9},{9,8... | collective-permute-start | bytes 4718600 | tf_op jit(solution)/shard_map/ppermute | solution.py:240
  84.8 1.2 copy-start.9
  86.0 2.3 %collective-permute-start.15 = (bf16[512,768]{1,0:T(8,128)(2,1)S(1)}, bf16[512,768]{1,0:T(8,128)(2,1)S(1)}, u32[]{:S(2)}, u32[]{:S(2)}) collective-permute-start(bf16[512,768]{1,0:T(8,128)(2,1)S(1)} %get-tuple-element.133.refs_0_), channel_id=1, source_target_pairs={{0,8},{1,9},{2,10},{3,11},{4,12},{5,13},{6,14},{7,15},{8,0},{9,1},... | collective-permute-start | bytes 2359304 | tf_op jit(solution)/shard_map/ppermute | solution.py:240
  86.2 3.3 %collective-permute-start.16 = (bf16[768,512]{1,0:T(8,128)(2,1)S(1)}, bf16[768,512]{1,0:T(8,128)(2,1)S(1)}, u32[]{:S(2)}, u32[]{:S(2)}) collective-permute-start(bf16[768,512]{1,0:T(8,128)(2,1)S(1)} %get-tuple-element.131.refs_2_), channel_id=1, source_target_pairs={{0,8},{1,9},{2,10},{3,11},{4,12},{5,13},{6,14},{7,15},{8,0},{9,1},... | collective-permute-start | bytes 2359304 | tf_op jit(solution)/shard_map/ppermute | solution.py:240
  96.7 5.6 %copy-start = (f32[512,768]{1,0:T(8,128)}, f32[512,768]{1,0:T(8,128)S(1)}, u32[]{:S(2)}) copy-start(f32[512,768]{1,0:T(8,128)S(1)} %get-tuple-element.138.refs_14_) | copy-start | bytes 4718596
  96.7 5.6 %copy-start.1 = (f32[512,768]{1,0:T(8,128)}, f32[512,768]{1,0:T(8,128)S(1)}, u32[]{:S(2)}) copy-start(f32[512,768]{1,0:T(8,128)S(1)} %get-tuple-element.139.refs_15_) | copy-start | bytes 4718596
  96.7 20.9 %collective-permute-start.18 = (bf16[8,384,128]{2,1,0:T(8,128)(2,1)S(1)}, bf16[8,384,128]{2,1,0:T(8,128)(2,1)S(1)}, u32[]{:S(2)}, u32[]{:S(2)}) collective-permute-start(bf16[8,384,128]{2,1,0:T(8,128)(2,1)S(1)} %get-tuple-element.132), channel_id=1, source_target_pairs={{0,16},{1,17},{2,18},{3,19},{4,20},{5,21},{6,22},{7,23},{8,9},{9,8... | collective-permute-start | bytes 2359304 | tf_op jit(solution)/shard_map/ppermute | solution.py:240
  117.6 3.5 %copy-start.10 = (f32[512,768]{1,0:T(8,128)S(1)}, f32[512,768]{1,0:T(8,128)}, u32[]{:S(2)}) copy-start(f32[512,768]{1,0:T(8,128)} %copy-done.9) | copy-start | bytes 4718596
  117.6 3.5 %collective-permute-start.19 = (bf16[1024,768]{1,0:T(8,128)(2,1)S(1)}, bf16[1024,768]{1,0:T(8,128)(2,1)S(1)}, u32[]{:S(2)}, u32[]{:S(2)}) collective-permute-start(bf16[1024,768]{1,0:T(8,128)(2,1)S(1)} %get-tuple-element.147), channel_id=1, source_target_pairs={{0,8},{1,9},{2,10},{3,11},{4,12},{5,13},{6,14},{7,15},{8,0},{9,1},... | collective-permute-start | bytes 4718600 | tf_op jit(solution)/shard_map/ppermute | solution.py:240
  117.7 20.5 %collective-permute-start.21 = (bf16[8,768,128]{2,1,0:T(8,128)(2,1)S(1)}, bf16[8,768,128]{2,1,0:T(8,128)(2,1)S(1)}, u32[]{:S(2)}, u32[]{:S(2)}) collective-permute-start(bf16[8,768,128]{2,1,0:T(8,128)(2,1)S(1)} %get-tuple-element.141), channel_id=1, source_target_pairs={{0,16},{1,17},{2,18},{3,19},{4,20},{5,21},{6,22},{7,23},{8,9},{9,8... | collective-permute-start | bytes 4718600 | tf_op jit(solution)/shard_map/ppermute | solution.py:240
  125.1 9.2 %collective-permute-start.20 = (bf16[16,144,128]{2,1,0:T(8,128)(2,1)S(1)}, bf16[16,144,128]{2,1,0:T(8,128)(2,1)S(1)}, u32[]{:S(2)}, u32[]{:S(2)}) collective-permute-start(bf16[16,144,128]{2,1,0:T(8,128)(2,1)S(1)} %get-tuple-element.155), channel_id=1, source_target_pairs={{0,8},{1,9},{2,10},{3,11},{4,12},{5,13},{6,14},{7,15},{8,0},{9,1},... | collective-permute-start | bytes 1769480 | tf_op jit(solution)/shard_map/ppermute | solution.py:240
  134.5 11.8 %collective-permute-start.24 = (bf16[8,144,128]{2,1,0:T(8,128)(2,1)S(1)}, bf16[8,144,128]{2,1,0:T(8,128)(2,1)S(1)}, u32[]{:S(2)}, u32[]{:S(2)}) collective-permute-start(bf16[8,144,128]{2,1,0:T(8,128)(2,1)S(1)} %slice.364), channel_id=1, source_target_pairs={{0,16},{1,17},{2,18},{3,19},{4,20},{5,21},{6,22},{7,23},{8,9},{9,8... | collective-permute-start | bytes 884744 | tf_op jit(solution)/shard_map/ppermute | solution.py:240
  138.6 13.2 %collective-permute-start.22 = (bf16[4,768,128]{2,1,0:T(8,128)(2,1)S(1)}, bf16[4,768,128]{2,1,0:T(8,128)(2,1)S(1)}, u32[]{:S(2)}, u32[]{:S(2)}) collective-permute-start(bf16[4,768,128]{2,1,0:T(8,128)(2,1)S(1)} %get-tuple-element.202), channel_id=1, source_target_pairs={{0,1},{1,0},{2,3},{3,2},{4,5},{5,4},{6,7},{7,6},{8,24},{9,25},{10,... | collective-permute-start | bytes 2359304 | tf_op jit(solution)/shard_map/ppermute | solution.py:240
  139.8 7.6 %collective-permute-start.23 = (bf16[16,24,1536]{2,1,0:T(8,128)(2,1)S(1)}, bf16[16,24,1536]{2,1,0:T(8,128)(2,1)S(1)}, u32[]{:S(2)}, u32[]{:S(2)}) collective-permute-start(bf16[16,24,1536]{2,1,0:T(8,128)(2,1)S(1)} %bitcast.51), channel_id=1, source_target_pairs={{0,8},{1,9},{2,10},{3,11},{4,12},{5,13},{6,14},{7,15},{8,0},{9,1},... | collective-permute-start | bytes 3538952 | tf_op jit(solution)/shard_map/ppermute | solution.py:240
  145.6 12.6 %collective-permute-start.28 = (bf16[16,24,896]{2,1,0:T(8,128)(2,1)S(1)}, bf16[16,24,896]{2,1,0:T(8,128)(2,1)S(1)}, u32[]{:S(2)}, u32[]{:S(2)}) collective-permute-start(bf16[16,24,896]{2,1,0:T(8,128)(2,1)S(1)} %bitcast.56), channel_id=1, source_target_pairs={{0,8},{1,9},{2,10},{3,11},{4,12},{5,13},{6,14},{7,15},{8,0},{9,1},... | collective-permute-start | bytes 2064392 | tf_op jit(solution)/shard_map/ppermute | solution.py:240
  146.5 16.9 %collective-permute-start.27 = (bf16[4,528,128]{2,1,0:T(8,128)(2,1)S(1)}, bf16[4,528,128]{2,1,0:T(8,128)(2,1)S(1)}, u32[]{:S(2)}, u32[]{:S(2)}) collective-permute-start(bf16[4,528,128]{2,1,0:T(8,128)(2,1)S(1)} %pad_maximum_fusion), channel_id=1, source_target_pairs={{0,1},{1,0},{2,3},{3,2},{4,5},{5,4},{6,7},{7,6},{8,24},{9,25},{10,... | collective-permute-start | bytes 1622024 | tf_op jit(solution)/shard_map/ppermute | solution.py:240
  147.4 6.8 %copy-start.8 = (bf16[768,2304]{1,0:T(8,128)(2,1)S(1)}, bf16[768,2304]{1,0:T(8,128)(2,1)}, u32[]{:S(2)}) copy-start(bf16[768,2304]{1,0:T(8,128)(2,1)} %copy-done.7) | copy-start | bytes 10616836
  147.7 19.9 %collective-permute-start.25 = (bf16[8,24,1536]{2,1,0:T(8,128)(2,1)S(1)}, bf16[8,24,1536]{2,1,0:T(8,128)(2,1)S(1)}, u32[]{:S(2)}, u32[]{:S(2)}) collective-permute-start(bf16[8,24,1536]{2,1,0:T(8,128)(2,1)S(1)} %get-tuple-element.210), channel_id=1, source_target_pairs={{0,16},{1,17},{2,18},{3,19},{4,20},{5,21},{6,22},{7,23},{8,9},{9,8... | collective-permute-start | bytes 1769480 | tf_op jit(solution)/shard_map/ppermute | solution.py:240
  152.0 13.8 %collective-permute-start.26 = (bf16[2,768,128]{2,1,0:T(8,128)(2,1)S(1)}, bf16[2,768,128]{2,1,0:T(8,128)(2,1)S(1)}, u32[]{:S(2)}, u32[]{:S(2)}) collective-permute-start(bf16[2,768,128]{2,1,0:T(8,128)(2,1)S(1)} %get-tuple-element.206), channel_id=1, source_target_pairs={{0,2},{1,3},{2,0},{3,1},{4,6},{5,7},{6,4},{7,5},{8,10},{9,11},{10,... | collective-permute-start | bytes 1179656 | tf_op jit(solution)/shard_map/ppermute | solution.py:240
  158.4 10.1 %collective-permute-start.31 = (bf16[8,24,896]{2,1,0:T(8,128)(2,1)S(1)}, bf16[8,24,896]{2,1,0:T(8,128)(2,1)S(1)}, u32[]{:S(2)}, u32[]{:S(2)}) collective-permute-start(bf16[8,24,896]{2,1,0:T(8,128)(2,1)S(1)} %get-tuple-element.222), channel_id=1, source_target_pairs={{0,16},{1,17},{2,18},{3,19},{4,20},{5,21},{6,22},{7,23},{8,9},{9,8... | collective-permute-start | bytes 1032200 | tf_op jit(solution)/shard_map/ppermute | solution.py:240
  163.5 9.2 %collective-permute-start.30 = (bf16[2,528,128]{2,1,0:T(8,128)(2,1)S(1)}, bf16[2,528,128]{2,1,0:T(8,128)(2,1)S(1)}, u32[]{:S(2)}, u32[]{:S(2)}) collective-permute-start(bf16[2,528,128]{2,1,0:T(8,128)(2,1)S(1)} %get-tuple-element.214), channel_id=1, source_target_pairs={{0,2},{1,3},{2,0},{3,1},{4,6},{5,7},{6,4},{7,5},{8,10},{9,11},{10,... | collective-permute-start | bytes 811016 | tf_op jit(solution)/shard_map/ppermute | solution.py:240
  165.8 19.4 %collective-permute-start.38 = (bf16[1,768,128]{2,1,0:T(8,128)(2,1)S(1)}, bf16[1,768,128]{2,1,0:T(8,128)(2,1)S(1)}, u32[]{:S(2)}, u32[]{:S(2)}) collective-permute-start(bf16[1,768,128]{2,1,0:T(8,128)(2,1)S(1)} %add_convert_fusion.12), channel_id=1, source_target_pairs={{0,4},{1,5},{2,6},{3,7},{4,0},{5,1},{6,2},{7,3},{8,12},{9,13},{10,... | collective-permute-start | bytes 589832 | tf_op jit(solution)/shard_map/ppermute | solution.py:240
  167.7 7.5 %collective-permute-start.29 = (bf16[4,24,1536]{2,1,0:T(8,128)(2,1)S(1)}, bf16[4,24,1536]{2,1,0:T(8,128)(2,1)S(1)}, u32[]{:S(2)}, u32[]{:S(2)}) collective-permute-start(bf16[4,24,1536]{2,1,0:T(8,128)(2,1)S(1)} %get-tuple-element.207), channel_id=1, source_target_pairs={{0,1},{1,0},{2,3},{3,2},{4,5},{5,4},{6,7},{7,6},{8,24},{9,25},{10,... | collective-permute-start | bytes 884744 | tf_op jit(solution)/shard_map/ppermute | solution.py:240
  168.6 9.4 %collective-permute-start.33 = (bf16[4,24,896]{2,1,0:T(8,128)(2,1)S(1)}, bf16[4,24,896]{2,1,0:T(8,128)(2,1)S(1)}, u32[]{:S(2)}, u32[]{:S(2)}) collective-permute-start(bf16[4,24,896]{2,1,0:T(8,128)(2,1)S(1)} %get-tuple-element.220), channel_id=1, source_target_pairs={{0,1},{1,0},{2,3},{3,2},{4,5},{5,4},{6,7},{7,6},{8,24},{9,25},{10,... | collective-permute-start | bytes 516104 | tf_op jit(solution)/shard_map/ppermute | solution.py:240
  172.7 12.6 %collective-permute-start.37 = (bf16[1,528,128]{2,1,0:T(8,128)(2,1)S(1)}, bf16[1,528,128]{2,1,0:T(8,128)(2,1)S(1)}, u32[]{:S(2)}, u32[]{:S(2)}) collective-permute-start(bf16[1,528,128]{2,1,0:T(8,128)(2,1)S(1)} %add_convert_fusion.20), channel_id=1, source_target_pairs={{0,4},{1,5},{2,6},{3,7},{4,0},{5,1},{6,2},{7,3},{8,12},{9,13},{10,... | collective-permute-start | bytes 405512 | tf_op jit(solution)/shard_map/ppermute | solution.py:240
  175.4 6.7 %collective-permute-start.32 = (bf16[2,24,1536]{2,1,0:T(8,128)(2,1)S(1)}, bf16[2,24,1536]{2,1,0:T(8,128)(2,1)S(1)}, u32[]{:S(2)}, u32[]{:S(2)}) collective-permute-start(bf16[2,24,1536]{2,1,0:T(8,128)(2,1)S(1)} %get-tuple-element.227), channel_id=1, source_target_pairs={{0,2},{1,3},{2,0},{3,1},{4,6},{5,7},{6,4},{7,5},{8,10},{9,11},{10,... | collective-permute-start | bytes 442376 | tf_op jit(solution)/shard_map/ppermute | solution.py:240
  178.0 5.8 %collective-permute-start.35 = (bf16[2,24,896]{2,1,0:T(8,128)(2,1)S(1)}, bf16[2,24,896]{2,1,0:T(8,128)(2,1)S(1)}, u32[]{:S(2)}, u32[]{:S(2)}) collective-permute-start(bf16[2,24,896]{2,1,0:T(8,128)(2,1)S(1)} %get-tuple-element.241), channel_id=1, source_target_pairs={{0,2},{1,3},{2,0},{3,1},{4,6},{5,7},{6,4},{7,5},{8,10},{9,11},{10,... | collective-permute-start | bytes 258056 | tf_op jit(solution)/shard_map/ppermute | solution.py:240
  182.1 8.2 %collective-permute-start.34 = (bf16[1,24,1536]{2,1,0:T(8,128)(2,1)S(1)}, bf16[1,24,1536]{2,1,0:T(8,128)(2,1)S(1)}, u32[]{:S(2)}, u32[]{:S(2)}) collective-permute-start(bf16[1,24,1536]{2,1,0:T(8,128)(2,1)S(1)} %add_convert_fusion.23), channel_id=1, source_target_pairs={{0,4},{1,5},{2,6},{3,7},{4,0},{5,1},{6,2},{7,3},{8,12},{9,13},{10,... | collective-permute-start | bytes 221192 | tf_op jit(solution)/shard_map/ppermute | solution.py:240
  183.8 5.4 %collective-permute-start.36 = (bf16[1,24,896]{2,1,0:T(8,128)(2,1)S(1)}, bf16[1,24,896]{2,1,0:T(8,128)(2,1)S(1)}, u32[]{:S(2)}, u32[]{:S(2)}) collective-permute-start(bf16[1,24,896]{2,1,0:T(8,128)(2,1)S(1)} %add_convert_fusion.25), channel_id=1, source_target_pairs={{0,4},{1,5},{2,6},{3,7},{4,0},{5,1},{6,2},{7,3},{8,12},{9,13},{10,... | collective-permute-start | bytes 129032 | tf_op jit(solution)/shard_map/ppermute | solution.py:240
  185.4 5.1 %copy-start.11 = (bf16[24,2304]{1,0:T(8,128)(2,1)S(1)}, bf16[24,2304]{1,0:T(8,128)(2,1)}, u32[]{:S(2)}) copy-start(bf16[24,2304]{1,0:T(8,128)(2,1)} %param.13) | copy-start | bytes 331780
  185.4 5.3 %copy-start.14 = (bf16[24]{0:T(256)(128)(2,1)S(1)}, bf16[24]{0:T(256)(128)(2,1)}, u32[]{:S(2)}) copy-start(bf16[24]{0:T(256)(128)(2,1)} %param.16) | copy-start | bytes 148
  186.2 5.0 %collective-permute-start.39 = (f32[576,128]{1,0:T(8,128)S(1)}, f32[576,128]{1,0:T(8,128)S(1)}, u32[]{:S(2)}, u32[]{:S(2)}) collective-permute-start(f32[576,128]{1,0:T(8,128)S(1)} %pad_maximum_fusion.2), channel_id=1, source_target_pairs={{0,8},{1,9},{2,10},{3,11},{4,12},{5,13},{6,14},{7,15},{8,0},{9,1},... | collective-permute-start | bytes 884744 | tf_op jit(solution)/shard_map/ppermute | solution.py:240
  190.5 1.8 copy-start.12

commit v2 on v1

--- a/solution.py
+++ b/solution.py
@@ -207,7 +207,7 @@
 AXES = ("batch", "wide")
 LANES = 256
 PART = 128
-VMEM_MIB = {"ffn": 36}
+VMEM_MIB = {"ffn": 22}
 
 
 def fits(mesh, args):

time: 193 us -> 190 us (0.984)
  Pallas kernels: 67.5 us -> 65 us
  local copies, waits for them, and re-layouts: 9.49 us -> 7.19 us
    pallas_call x1, Pallas kernels: 15.2 us -> 12.8 us  [own_sequence(): call(functools.partial(ffn_kernel, False), (4,), sequence_specs + [tile(w...]
    unnamed x48 -> x34, local copies, waits for them, and re-layouts: 6.46 us -> 5.2 us
  transfers between devices with their start and end apart: 40 -> 40, of which waited for: 18 -> 18; matrix products, arithmetic and copies ran while one was open for 4% -> 4% of each run, Pallas kernels for 35% -> 34%
where the time goes in v2:
time: 190 us; the launch traced here: 189 us
  waiting for transfers between devices  69.3 us (36%)
  Pallas kernels  65 us (34%)
  starting transfers between devices  40.2 us (21%)
  local copies, waits for them, and re-layouts  7.19 us (4%)
  other arithmetic  5.86 us (3%)
  between operations  1.92 us (1%)
    ppermute x40, waiting for transfers between devices, send(): return lax.ppermute(array, AXES, flip_pairs(rule))  69.3 us
    ppermute x40, starting transfers between devices, send(): return lax.ppermute(array, AXES, flip_pairs(rule))  40.2 us
    pallas_call x2, Pallas kernels, attend_back(): call(attend_back_kernel, (count,), specs * 2 + tap_specs + [specs[0]] * 2...  13.5 us
    pallas_call x1, Pallas kernels, own_sequence(): call(functools.partial(ffn_kernel, False), (4,), sequence_specs + [tile(w...  12.8 us
    pallas_call x1, Pallas kernels, own_sequence(): call(attend_kernel, (groups,), part_specs, [lane_block, lse_spec], [shape...  9.19 us
    pallas_call x1, Pallas kernels, own_sequence(): call(functools.partial(ffn_kernel, True), (2,), sequence_specs + [tile(ha...  7.29 us
    pallas_call x1, Pallas kernels, own_sequence(): call(project_kernel, (wide // LANES,), [token, half_block, half_block, fe...  7.21 us
    unnamed x34, local copies, waits for them, and re-layouts  5.2 us
  transfers between devices with their start and end apart: 40, of which 18 were waited for; matrix products, arithmetic and copies ran while one was open for 4% of the time, Pallas kernels for 34%

profile of v2, /device:TPU:0, one launch (start us, length us, event | category | flops | bytes accessed | tf_op | source)
XLA Modules:
  0.0 189.5 jit_solution(1234592212330664810)
XLA Ops:
  1.3 1.0 fusion.22
  2.3 4.1 %collective-permute-start = (bf16[1,24,2432]{2,1,0:T(8,128)(2,1)S(1)}, bf16[1,24,2432]{2,1,0:T(8,128)(2,1)S(1)}, u32[]{:S(2)}, u32[]{:S(2)}) collective-permute-start(bf16[1,24,2432]{2,1,0:T(8,128)(2,1)S(1)} %fusion.22), channel_id=1, source_target_pairs={{0,4},{1,5},{2,6},{3,7},{4,0},{5,1},{6,2},{7,3},{8,12},{9,13},{10,... | collective-permute-start | bytes 350216 | tf_op jit(solution)/shard_map/ppermute | solution.py:240
  6.5 1.1 copy-done.2
  7.5 1.1 copy-done.3
  8.6 0.8 copy-done.4
  9.3 0.8 pack.1
  10.2 1.9 %collective-permute-done = bf16[1,24,2432]{2,1,0:T(8,128)(2,1)S(1)} collective-permute-done((bf16[1,24,2432]{2,1,0:T(8,128)(2,1)S(1)}, bf16[1,24,2432]{2,1,0:T(8,128)(2,1)S(1)}, u32[]{:S(2)}, u32[]{:S(2)}) %collective-permute-start) | collective-permute-done | bytes 116768 | tf_op jit(solution)/shard_map/ppermute | solution.py:240
  12.1 0.8 collective-permute-start.2
  13.0 6.1 %collective-permute-done.2 = bf16[2,24,2432]{2,1,0:T(8,128)(2,1)S(1)} collective-permute-done((bf16[2,24,2432]{2,1,0:T(8,128)(2,1)S(1)}, bf16[2,24,2432]{2,1,0:T(8,128)(2,1)S(1)}, u32[]{:S(2)}, u32[]{:S(2)}) %collective-permute-start.2) | collective-permute-done | bytes 233504 | tf_op jit(solution)/shard_map/ppermute | solution.py:240
  19.1 1.3 collective-permute-start.4
  20.5 3.3 %collective-permute-start.1 = (bf16[1,528,128]{2,1,0:T(8,128)(2,1)S(1)}, bf16[1,528,128]{2,1,0:T(8,128)(2,1)S(1)}, u32[]{:S(2)}, u32[]{:S(2)}) collective-permute-start(bf16[1,528,128]{2,1,0:T(8,128)(2,1)S(1)} %get-tuple-element.109), channel_id=1, source_target_pairs={{0,4},{1,5},{2,6},{3,7},{4,0},{5,1},{6,2},{7,3},{8,12},{9,13},{10,... | collective-permute-start | bytes 405512 | tf_op jit(solution)/shard_map/ppermute | solution.py:240
  23.9 5.8 %collective-permute-done.1 = bf16[1,528,128]{2,1,0:T(8,128)(2,1)S(1)} collective-permute-done((bf16[1,528,128]{2,1,0:T(8,128)(2,1)S(1)}, bf16[1,528,128]{2,1,0:T(8,128)(2,1)S(1)}, u32[]{:S(2)}, u32[]{:S(2)}) %collective-permute-start.1) | collective-permute-done | bytes 135200 | tf_op jit(solution)/shard_map/ppermute | solution.py:240
  29.9 0.6 collective-permute-start.6
  30.5 0.7 collective-permute-start.7
  31.2 3.4 %collective-permute-start.3 = (bf16[1,768,128]{2,1,0:T(8,128)(2,1)S(1)}, bf16[1,768,128]{2,1,0:T(8,128)(2,1)S(1)}, u32[]{:S(2)}, u32[]{:S(2)}) collective-permute-start(bf16[1,768,128]{2,1,0:T(8,128)(2,1)S(1)} %get-tuple-element.112), channel_id=1, source_target_pairs={{0,4},{1,5},{2,6},{3,7},{4,0},{5,1},{6,2},{7,3},{8,12},{9,13},{10,... | collective-permute-start | bytes 589832 | tf_op jit(solution)/shard_map/ppermute | solution.py:240
  34.7 7.4 %collective-permute-done.3 = bf16[1,768,128]{2,1,0:T(8,128)(2,1)S(1)} collective-permute-done((bf16[1,768,128]{2,1,0:T(8,128)(2,1)S(1)}, bf16[1,768,128]{2,1,0:T(8,128)(2,1)S(1)}, u32[]{:S(2)}, u32[]{:S(2)}) %collective-permute-start.3) | collective-permute-done | bytes 196640 | tf_op jit(solution)/shard_map/ppermute | solution.py:240
  42.1 1.3 collective-permute-done.7
  43.9 2.9 %collective-permute-start.5 = (bf16[2,768,128]{2,1,0:T(8,128)(2,1)S(1)}, bf16[2,768,128]{2,1,0:T(8,128)(2,1)S(1)}, u32[]{:S(2)}, u32[]{:S(2)}) collective-permute-start(bf16[2,768,128]{2,1,0:T(8,128)(2,1)S(1)} %get-tuple-element.261), channel_id=1, source_target_pairs={{0,2},{1,3},{2,0},{3,1},{4,6},{5,7},{6,4},{7,5},{8,10},{9,11},{10,... | collective-permute-start | bytes 1179656 | tf_op jit(solution)/shard_map/ppermute | solution.py:240
  46.8 0.8 prepare.1
  48.6 7.9 %collective-permute-done.5 = bf16[2,768,128]{2,1,0:T(8,128)(2,1)S(1)} collective-permute-done((bf16[2,768,128]{2,1,0:T(8,128)(2,1)S(1)}, bf16[2,768,128]{2,1,0:T(8,128)(2,1)S(1)}, u32[]{:S(2)}, u32[]{:S(2)}) %collective-permute-start.5) | collective-permute-done | bytes 393248 | tf_op jit(solution)/shard_map/ppermute | solution.py:240
  56.7 0.4 collective-permute-start.10
  57.2 7.2 %project.1 = (bf16[512,2304]{1,0:T(8,128)(2,1)S(1)}, bf16[512,2304]{1,0:T(8,128)(2,1)S(1)}, bf16[768,2304]{1,0:T(8,128)(2,1)S(1)}, bf16[32,24,512]{2,1,0:T(8,128...) custom-call(s32[64]{0:T(128)S(1)} %compare_select_fusion.1.meta, bf16[512,768]{1,0:T(8,128)(2,1)S(1)} %bitcast.53, ...), custom_call_target="tpu_custom_call" | custom-call | flops 8049999872 | tf_op jit(solution)/shard_map/project/pallas_call | solution.py:701
  64.6 0.5 collective-permute-start.13
  65.1 5.7 %collective-permute-done.10 = bf16[4,768,128]{2,1,0:T(8,128)(2,1)S(1)} collective-permute-done((bf16[4,768,128]{2,1,0:T(8,128)(2,1)S(1)}, bf16[4,768,128]{2,1,0:T(8,128)(2,1)S(1)}, u32[]{:S(2)}, u32[]{:S(2)}) %collective-permute-start.10) | collective-permute-done | bytes 786464 | tf_op jit(solution)/shard_map/ppermute | solution.py:240
  71.1 9.2 %attend.1 = (bf16[512,768]{1,0:T(8,128)(2,1)S(1)}, f32[3,8,512]{2,1,0:T(8,128)S(1)}) custom-call(s32[64]{0:T(128)S(1)} %compare_select_fusion.1.meta, bf16[512,2304]{1,0:T(8,128)(2,1)S(1)} %get-tuple-element.126.q_ref.k_ref.v_ref, bf16[512,2304]{1,0:T(8,128)(2,1)S(1)} %get-tuple-element.126.q_ref.k_ref.v_ref, ...), custom_call_target="tpu_custom_call" | custom-call | flops 10350000128 | tf_op jit(solution)/shard_map/attend/pallas_call | solution.py:717
  80.7 1.9 %collective-permute-done.14.other_ref = bf16[16,144,128]{2,1,0:T(8,128)(2,1)S(1)} collective-permute-done((bf16[16,144,128]{2,1,0:T(8,128)(2,1)S(1)}, bf16[16,144,128]{2,1,0:T(8,128)(2,1)S(1)}, u32[]{:S(2)}, u32[]{:S(2)}) %collective-permute-start.14) | collective-permute-done | bytes 589856 | tf_op jit(solution)/shard_map/ppermute | solution.py:240
  82.6 2.2 %mend.1 = (f32[512,768]{1,0:T(8,128)S(1)}, bf16[512,768]{1,0:T(8,128)(2,1)S(1)}, bf16[768,512]{1,0:T(8,128)(2,1)S(1)}, bf16[32,24,512]{2,1,0:T(8,128)(2,1)S(1)}, bf16[768,768]{1,0:T(8,128)(2,1)S(1)}) custom-call(s32[64]{0:T(128)S(1)} %compare_select_fusion.1.meta, bf16[512,768]{1,0:T(8,128)(2,1)S(1)} %get-tuple-element.127.att_ref.out_ref, ...), custom_call_target="tpu_custom_call" | custom-call | flops 2875000064 | tf_op jit(solution)/shard_map/mend/pallas_call | solution.py:727
  85.3 1.8 collective-permute-done.15.refs_4_
  87.1 1.1 collective-permute-done.16.refs_6_
  88.2 7.3 %ffn.2 = (f32[512,768]{1,0:T(8,128)S(1)}, f32[512,768]{1,0:T(8,128)S(1)}, f32[512,768]{1,0:T(8,128)S(1)}, f32[512,768]{1,0:T(8,128)S(1)}, bf16[8,384,128]{2,1,0:...) custom-call(s32[64]{0:T(128)S(1)} %compare_select_fusion.1.meta, bf16[512,768]{1,0:T(8,128)(2,1)S(1)} %get-tuple-element.133.refs_0_, ...), custom_call_target="tpu_custom_call" | custom-call | flops 2300000000 | tf_op jit(solution)/shard_map/ffn/pallas_call | solution.py:748
  95.7 5.4 %collective-permute-done.17 = bf16[8,768,128]{2,1,0:T(8,128)(2,1)S(1)} collective-permute-done((bf16[8,768,128]{2,1,0:T(8,128)(2,1)S(1)}, bf16[8,768,128]{2,1,0:T(8,128)(2,1)S(1)}, u32[]{:S(2)}, u32[]{:S(2)}) %collective-permute-start.17) | collective-permute-done | bytes 1572896 | tf_op jit(solution)/shard_map/ppermute | solution.py:240
  101.3 12.8 %ffn.3 = (f32[512,768]{1,0:T(8,128)S(1)}, f32[512,768]{1,0:T(8,128)S(1)}, bf16[1024,768]{1,0:T(8,128)(2,1)S(1)}, bf16[8,768,128]{2,1,0:T(8,128)(2,1)S(1)}, bf16[8,768,128]{2,1,0:T(8,128)(2,1)S(1)}) custom-call(s32[64]{0:T(128)S(1)} %compare_select_fusion.1.meta, bf16[512,768]{1,0:T(8,128)(2,1)S(1)} %get-tuple-element.133.refs_0_, ...), custom_call_target="tpu_custom_call" | custom-call | flops 17250000896 | tf_op jit(solution)/shard_map/ffn/pallas_call | solution.py:756
  114.5 3.1 %collective-permute-done.19.come_ref = bf16[1024,768]{1,0:T(8,128)(2,1)S(1)} collective-permute-done((bf16[1024,768]{1,0:T(8,128)(2,1)S(1)}, bf16[1024,768]{1,0:T(8,128)(2,1)S(1)}, u32[]{:S(2)}, u32[]{:S(2)}) %collective-permute-start.19) | collective-permute-done | bytes 1572896 | tf_op jit(solution)/shard_map/ppermute | solution.py:240
  117.6 4.0 %turn.1 = (bf16[512,768]{1,0:T(8,128)(2,1)}, f32[512,768]{1,0:T(8,128)S(1)}, bf16[512,768]{1,0:T(8,128)(2,1)S(1)}, f32[1,768]{1,0:T(1,128)S(1)}, bf16[16,144,128...) custom-call(s32[64]{0:T(128)S(1)} %compare_select_fusion.1.meta, f32[512,768]{1,0:T(8,128)S(1)} %get-tuple-element.145.grad_ref, ...), custom_call_target="tpu_custom_call" | custom-call | flops 4600000000 | tf_op jit(solution)/shard_map/turn/pallas_call | solution.py:768
  121.7 9.1 %attend_back.2 = (bf16[512,512]{1,0:T(8,128)(2,1)S(1)}, bf16[512,512]{1,0:T(8,128)(2,1)S(1)}, bf16[512,512]{1,0:T(8,128)(2,1)S(1)}, f32[8,512]{1,0:T(8,128)S(1)}...) custom-call(s32[64]{0:T(128)S(1)} %compare_select_fusion.1.meta, ...), custom_call_target="tpu_custom_call" | custom-call | flops 2300000000 | tf_op jit(solution)/shard_map/attend_back/pallas_call | solution.py:783
  131.0 1.9 %weight.2 = (bf16[384,1536]{1,0:T(8,128)(2,1)S(1)}, bf16[384,1536]{1,0:T(8,128)(2,1)S(1)}) custom-call(s32[64]{0:T(128)S(1)} %compare_select_fusion.1.meta, bf16[768,512]{1,0:T(8,128)(2,1)S(1)} %bitcast.57, bf16[512,512]{1,0:T(8,128)(2,1)S(1)} %get-tuple-element.158.refs_0_, bf16[512,512]{1,0:T(8,128)(2,1)S(1)} %get-tuple-element.163.refs_1_.refs_2_, ...), custom_call_target="tpu_custom_call" | custom-call | flops 1150000000 | tf_op jit(solution)/shard_map/weight/pallas_call | solution.py:795
  133.0 1.7 collective-permute-done.21
  134.6 0.4 add_convert_fusion
  135.1 1.2 collective-permute-start.22
  136.3 4.4 %attend_back.3 = (bf16[512,256]{1,0:T(8,128)(2,1)S(1)}, bf16[512,256]{1,0:T(8,128)(2,1)S(1)}, bf16[512,256]{1,0:T(8,128)(2,1)S(1)}, f32[8,256]{1,0:T(8,128)S(1)}...) custom-call(s32[64]{0:T(128)S(1)} %compare_select_fusion.1.meta, ...), custom_call_target="tpu_custom_call" | custom-call | flops 1150000000 | tf_op jit(solution)/shard_map/attend_back/pallas_call | solution.py:783
  140.7 1.3 weight.3
  142.0 0.6 collective-permute-start.28
  142.9 1.0 collective-permute-start.27
  144.6 3.6 %collective-permute-done.22 = bf16[4,768,128]{2,1,0:T(8,128)(2,1)S(1)} collective-permute-done((bf16[4,768,128]{2,1,0:T(8,128)(2,1)S(1)}, bf16[4,768,128]{2,1,0:T(8,128)(2,1)S(1)}, u32[]{:S(2)}, u32[]{:S(2)}) %collective-permute-start.22) | collective-permute-done | bytes 786464 | tf_op jit(solution)/shard_map/ppermute | solution.py:240
  148.4 2.3 %collective-permute-start.26 = (bf16[2,768,128]{2,1,0:T(8,128)(2,1)S(1)}, bf16[2,768,128]{2,1,0:T(8,128)(2,1)S(1)}, u32[]{:S(2)}, u32[]{:S(2)}) collective-permute-start(bf16[2,768,128]{2,1,0:T(8,128)(2,1)S(1)} %get-tuple-element.206), channel_id=1, source_target_pairs={{0,2},{1,3},{2,0},{3,1},{4,6},{5,7},{6,4},{7,5},{8,10},{9,11},{10,... | collective-permute-start | bytes 1179656 | tf_op jit(solution)/shard_map/ppermute | solution.py:240
  150.7 4.0 %last.1 = bf16[512,768]{1,0:T(8,128)(2,1)} custom-call(s32[64]{0:T(128)S(1)} %compare_select_fusion.1.meta, bf16[512,512]{1,0:T(8,128)(2,1)S(1)} %get-tuple-element.158.refs_0_, bf16[512,256]{1,0:T(8,128)(2,1)S(1)} %get-tuple-element.169.refs_7_.refs_1_, bf16[512,512]{1,0:T(8,128)(2,1)S(1)} %get-tuple-element.163.refs_1_.refs_2_, ...), custom_call_target="tpu_custom_call" | custom-call | flops 4600000000 | tf_op jit(solution)/shard_map/last/pallas_call | solution.py:828
  154.9 4.9 %collective-permute-done.27 = bf16[4,528,128]{2,1,0:T(8,128)(2,1)S(1)} collective-permute-done((bf16[4,528,128]{2,1,0:T(8,128)(2,1)S(1)}, bf16[4,528,128]{2,1,0:T(8,128)(2,1)S(1)}, u32[]{:S(2)}, u32[]{:S(2)}) %collective-permute-start.27) | collective-permute-done | bytes 540704 | tf_op jit(solution)/shard_map/ppermute | solution.py:240
  159.9 2.3 %collective-permute-start.30 = (bf16[2,528,128]{2,1,0:T(8,128)(2,1)S(1)}, bf16[2,528,128]{2,1,0:T(8,128)(2,1)S(1)}, u32[]{:S(2)}, u32[]{:S(2)}) collective-permute-start(bf16[2,528,128]{2,1,0:T(8,128)(2,1)S(1)} %get-tuple-element.214), channel_id=1, source_target_pairs={{0,2},{1,3},{2,0},{3,1},{4,6},{5,7},{6,4},{7,5},{8,10},{9,11},{10,... | collective-permute-start | bytes 811016 | tf_op jit(solution)/shard_map/ppermute | solution.py:240
  162.2 1.8 collective-permute-start.38
  164.2 0.8 collective-permute-start.29
  165.1 1.4 collective-permute-start.33
  166.4 2.6 %collective-permute-done.30 = bf16[2,528,128]{2,1,0:T(8,128)(2,1)S(1)} collective-permute-done((bf16[2,528,128]{2,1,0:T(8,128)(2,1)S(1)}, bf16[2,528,128]{2,1,0:T(8,128)(2,1)S(1)}, u32[]{:S(2)}, u32[]{:S(2)}) %collective-permute-start.30) | collective-permute-done | bytes 270368 | tf_op jit(solution)/shard_map/ppermute | solution.py:240
  169.1 2.6 %collective-permute-start.37 = (bf16[1,528,128]{2,1,0:T(8,128)(2,1)S(1)}, bf16[1,528,128]{2,1,0:T(8,128)(2,1)S(1)}, u32[]{:S(2)}, u32[]{:S(2)}) collective-permute-start(bf16[1,528,128]{2,1,0:T(8,128)(2,1)S(1)} %add_convert_fusion.20), channel_id=1, source_target_pairs={{0,4},{1,5},{2,6},{3,7},{4,0},{5,1},{6,2},{7,3},{8,12},{9,13},{10,... | collective-permute-start | bytes 405512 | tf_op jit(solution)/shard_map/ppermute | solution.py:240
  171.8 2.6 %collective-permute-start.32 = (bf16[2,24,1536]{2,1,0:T(8,128)(2,1)S(1)}, bf16[2,24,1536]{2,1,0:T(8,128)(2,1)S(1)}, u32[]{:S(2)}, u32[]{:S(2)}) collective-permute-start(bf16[2,24,1536]{2,1,0:T(8,128)(2,1)S(1)} %get-tuple-element.227), channel_id=1, source_target_pairs={{0,2},{1,3},{2,0},{3,1},{4,6},{5,7},{6,4},{7,5},{8,10},{9,11},{10,... | collective-permute-start | bytes 442376 | tf_op jit(solution)/shard_map/ppermute | solution.py:240
  174.5 4.0 %collective-permute-done.32 = bf16[2,24,1536]{2,1,0:T(8,128)(2,1)S(1)} collective-permute-done((bf16[2,24,1536]{2,1,0:T(8,128)(2,1)S(1)}, bf16[2,24,1536]{2,1,0:T(8,128)(2,1)S(1)}, u32[]{:S(2)}, u32[]{:S(2)}) %collective-permute-start.32) | collective-permute-done | bytes 147488 | tf_op jit(solution)/shard_map/ppermute | solution.py:240
  178.6 1.6 collective-permute-start.34
  180.2 1.5 collective-permute-start.36
  181.9 0.6 copy.23
  182.6 3.0 %collective-permute-done.36 = bf16[1,24,896]{2,1,0:T(8,128)(2,1)S(1)} collective-permute-done((bf16[1,24,896]{2,1,0:T(8,128)(2,1)S(1)}, bf16[1,24,896]{2,1,0:T(8,128)(2,1)S(1)}, u32[]{:S(2)}, u32[]{:S(2)}) %collective-permute-start.36) | collective-permute-done | bytes 43040 | tf_op jit(solution)/shard_map/ppermute | solution.py:240
  185.7 0.6 slice_bitcast_fusion
  186.2 0.5 slice_bitcast_fusion.1
  187.0 0.5 convert_divide_fusion
  187.9 0.8 maximum_bitcast_fusion
  188.7 0.8 pad_maximum_fusion.3
  (111 shorter events, 7.7 us)
Async XLA Ops:
  2.3 9.8 %collective-permute-start = (bf16[1,24,2432]{2,1,0:T(8,128)(2,1)S(1)}, bf16[1,24,2432]{2,1,0:T(8,128)(2,1)S(1)}, u32[]{:S(2)}, u32[]{:S(2)}) collective-permute-start(bf16[1,24,2432]{2,1,0:T(8,128)(2,1)S(1)} %fusion.22), channel_id=1, source_target_pairs={{0,4},{1,5},{2,6},{3,7},{4,0},{5,1},{6,2},{7,3},{8,12},{9,13},{10,... | collective-permute-start | bytes 350216 | tf_op jit(solution)/shard_map/ppermute | solution.py:240
  6.4 1.1 copy-start.2
  7.5 1.1 copy-start.3
  8.6 0.8 copy-start.4
  12.1 6.9 %collective-permute-start.2 = (bf16[2,24,2432]{2,1,0:T(8,128)(2,1)S(1)}, bf16[2,24,2432]{2,1,0:T(8,128)(2,1)S(1)}, u32[]{:S(2)}, u32[]{:S(2)}) collective-permute-start(bf16[2,24,2432]{2,1,0:T(8,128)(2,1)S(1)} %pad_maximum_fusion.5), channel_id=1, source_target_pairs={{0,2},{1,3},{2,0},{3,1},{4,6},{5,7},{6,4},{7,5},{8,10},{9,11},{10,... | collective-permute-start | bytes 700424 | tf_op jit(solution)/shard_map/ppermute | solution.py:240
  19.1 10.6 %collective-permute-start.4 = (bf16[4,24,2432]{2,1,0:T(8,128)(2,1)S(1)}, bf16[4,24,2432]{2,1,0:T(8,128)(2,1)S(1)}, u32[]{:S(2)}, u32[]{:S(2)}) collective-permute-start(bf16[4,24,2432]{2,1,0:T(8,128)(2,1)S(1)} %get-tuple-element.257), channel_id=1, source_target_pairs={{0,1},{1,0},{2,3},{3,2},{4,5},{5,4},{6,7},{7,6},{8,24},{9,25},{10,... | collective-permute-start | bytes 1400840 | tf_op jit(solution)/shard_map/ppermute | solution.py:240
  20.5 9.2 %collective-permute-start.1 = (bf16[1,528,128]{2,1,0:T(8,128)(2,1)S(1)}, bf16[1,528,128]{2,1,0:T(8,128)(2,1)S(1)}, u32[]{:S(2)}, u32[]{:S(2)}) collective-permute-start(bf16[1,528,128]{2,1,0:T(8,128)(2,1)S(1)} %get-tuple-element.109), channel_id=1, source_target_pairs={{0,4},{1,5},{2,6},{3,7},{4,0},{5,1},{6,2},{7,3},{8,12},{9,13},{10,... | collective-permute-start | bytes 405512 | tf_op jit(solution)/shard_map/ppermute | solution.py:240
  29.9 13.8 %collective-permute-start.6 = (bf16[8,24,2432]{2,1,0:T(8,128)(2,1)S(1)}, bf16[8,24,2432]{2,1,0:T(8,128)(2,1)S(1)}, u32[]{:S(2)}, u32[]{:S(2)}) collective-permute-start(bf16[8,24,2432]{2,1,0:T(8,128)(2,1)S(1)} %get-tuple-element.232), channel_id=1, source_target_pairs={{0,16},{1,17},{2,18},{3,19},{4,20},{5,21},{6,22},{7,23},{8,9},{9,8... | collective-permute-start | bytes 2801672 | tf_op jit(solution)/shard_map/ppermute | solution.py:240
  30.5 12.9 %collective-permute-start.7 = (bf16[2,528,128]{2,1,0:T(8,128)(2,1)S(1)}, bf16[2,528,128]{2,1,0:T(8,128)(2,1)S(1)}, u32[]{:S(2)}, u32[]{:S(2)}) collective-permute-start(bf16[2,528,128]{2,1,0:T(8,128)(2,1)S(1)} %get-tuple-element.269), channel_id=1, source_target_pairs={{0,2},{1,3},{2,0},{3,1},{4,6},{5,7},{6,4},{7,5},{8,10},{9,11},{10,... | collective-permute-start | bytes 811016 | tf_op jit(solution)/shard_map/ppermute | solution.py:240
  31.2 10.9 %collective-permute-start.3 = (bf16[1,768,128]{2,1,0:T(8,128)(2,1)S(1)}, bf16[1,768,128]{2,1,0:T(8,128)(2,1)S(1)}, u32[]{:S(2)}, u32[]{:S(2)}) collective-permute-start(bf16[1,768,128]{2,1,0:T(8,128)(2,1)S(1)} %get-tuple-element.112), channel_id=1, source_target_pairs={{0,4},{1,5},{2,6},{3,7},{4,0},{5,1},{6,2},{7,3},{8,12},{9,13},{10,... | collective-permute-start | bytes 589832 | tf_op jit(solution)/shard_map/ppermute | solution.py:240
  43.5 3.3 %copy-start = (bf16[1,512,768]{2,1,0:T(8,128)(2,1)S(1)}, bf16[1,512,768]{2,1,0:T(8,128)(2,1)}, u32[]{:S(2)}) copy-start(bf16[1,512,768]{2,1,0:T(8,128)(2,1)} %param.12) | copy-start | bytes 2359300
  43.8 12.7 %collective-permute-start.8 = (bf16[16,24,2432]{2,1,0:T(8,128)(2,1)S(1)}, bf16[16,24,2432]{2,1,0:T(8,128)(2,1)S(1)}, u32[]{:S(2)}, u32[]{:S(2)}) collective-permute-start(bf16[16,24,2432]{2,1,0:T(8,128)(2,1)S(1)} %constant_dynamic-update-slice_fusion.14.own_ref.few_own_ref), channel_id=1, source_target_pairs={{0,8},{1,9},{2,10},{3,11},{4,12},{5,13},{6,14},{7,15},{8,0},{9,1},... | collective-permute-start | bytes 5603336 | tf_op jit(solution)/shard_map/ppermute | solution.py:240
  43.9 12.6 %collective-permute-start.5 = (bf16[2,768,128]{2,1,0:T(8,128)(2,1)S(1)}, bf16[2,768,128]{2,1,0:T(8,128)(2,1)S(1)}, u32[]{:S(2)}, u32[]{:S(2)}) collective-permute-start(bf16[2,768,128]{2,1,0:T(8,128)(2,1)S(1)} %get-tuple-element.261), channel_id=1, source_target_pairs={{0,2},{1,3},{2,0},{3,1},{4,6},{5,7},{6,4},{7,5},{8,10},{9,11},{10,... | collective-permute-start | bytes 1179656 | tf_op jit(solution)/shard_map/ppermute | solution.py:240
  47.6 9.5 %copy-start.1 = (bf16[1,512,768]{2,1,0:T(8,128)(2,1)S(1)}, bf16[1,512,768]{2,1,0:T(8,128)(2,1)}, u32[]{:S(2)}) copy-start(bf16[1,512,768]{2,1,0:T(8,128)(2,1)} %param.10) | copy-start | bytes 2359300
  47.7 23.5 %collective-permute-start.12 = (bf16[768,512]{1,0:T(8,128)(2,1)S(1)}, bf16[768,512]{1,0:T(8,128)(2,1)S(1)}, u32[]{:S(2)}, u32[]{:S(2)}) collective-permute-start(bf16[768,512]{1,0:T(8,128)(2,1)S(1)} %get-tuple-element.125.refs_3_), channel_id=1, source_target_pairs={{0,8},{1,9},{2,10},{3,11},{4,12},{5,13},{6,14},{7,15},{8,0},{9,1},... | collective-permute-start | bytes 2359304 | tf_op jit(solution)/shard_map/ppermute | solution.py:240
  47.9 23.3 %collective-permute-start.11 = (bf16[512,768]{1,0:T(8,128)(2,1)S(1)}, bf16[512,768]{1,0:T(8,128)(2,1)S(1)}, u32[]{:S(2)}, u32[]{:S(2)}) collective-permute-start(bf16[512,768]{1,0:T(8,128)(2,1)S(1)} %get-tuple-element.124.refs_1_.go_ref), channel_id=1, source_target_pairs={{0,8},{1,9},{2,10},{3,11},{4,12},{5,13},{6,14},{7,15},{8,0},{9,1},... | collective-permute-start | bytes 2359304 | tf_op jit(solution)/shard_map/ppermute | solution.py:240
  48.2 16.1 %collective-permute-start.9 = (bf16[4,528,128]{2,1,0:T(8,128)(2,1)S(1)}, bf16[4,528,128]{2,1,0:T(8,128)(2,1)S(1)}, u32[]{:S(2)}, u32[]{:S(2)}) collective-permute-start(bf16[4,528,128]{2,1,0:T(8,128)(2,1)S(1)} %get-tuple-element.120), channel_id=1, source_target_pairs={{0,1},{1,0},{2,3},{3,2},{4,5},{5,4},{6,7},{7,6},{8,24},{9,25},{10,... | collective-permute-start | bytes 1622024 | tf_op jit(solution)/shard_map/ppermute | solution.py:240
  56.7 14.1 %collective-permute-start.10 = (bf16[4,768,128]{2,1,0:T(8,128)(2,1)S(1)}, bf16[4,768,128]{2,1,0:T(8,128)(2,1)S(1)}, u32[]{:S(2)}, u32[]{:S(2)}) collective-permute-start(bf16[4,768,128]{2,1,0:T(8,128)(2,1)S(1)} %get-tuple-element.239), channel_id=1, source_target_pairs={{0,1},{1,0},{2,3},{3,2},{4,5},{5,4},{6,7},{7,6},{8,24},{9,25},{10,... | collective-permute-start | bytes 2359304 | tf_op jit(solution)/shard_map/ppermute | solution.py:240
  64.6 15.7 %collective-permute-start.13 = (bf16[8,528,128]{2,1,0:T(8,128)(2,1)S(1)}, bf16[8,528,128]{2,1,0:T(8,128)(2,1)S(1)}, u32[]{:S(2)}, u32[]{:S(2)}) collective-permute-start(bf16[8,528,128]{2,1,0:T(8,128)(2,1)S(1)} %get-tuple-element.230), channel_id=1, source_target_pairs={{0,16},{1,17},{2,18},{3,19},{4,20},{5,21},{6,22},{7,23},{8,9},{9,8... | collective-permute-start | bytes 3244040 | tf_op jit(solution)/shard_map/ppermute | solution.py:240
  80.5 2.1 %collective-permute-start.14 = (bf16[16,144,128]{2,1,0:T(8,128)(2,1)S(1)}, bf16[16,144,128]{2,1,0:T(8,128)(2,1)S(1)}, u32[]{:S(2)}, u32[]{:S(2)}) collective-permute-start(bf16[16,144,128]{2,1,0:T(8,128)(2,1)S(1)} %slice.363.own_ref), channel_id=1, source_target_pairs={{0,8},{1,9},{2,10},{3,11},{4,12},{5,13},{6,14},{7,15},{8,0},{9,1},... | collective-permute-start | bytes 1769480 | tf_op jit(solution)/shard_map/ppermute | solution.py:240
  80.6 20.5 %collective-permute-start.17 = (bf16[8,768,128]{2,1,0:T(8,128)(2,1)S(1)}, bf16[8,768,128]{2,1,0:T(8,128)(2,1)S(1)}, u32[]{:S(2)}, u32[]{:S(2)}) collective-permute-start(bf16[8,768,128]{2,1,0:T(8,128)(2,1)S(1)} %get-tuple-element.134), channel_id=1, source_target_pairs={{0,16},{1,17},{2,18},{3,19},{4,20},{5,21},{6,22},{7,23},{8,9},{9,8... | collective-permute-start | bytes 4718600 | tf_op jit(solution)/shard_map/ppermute | solution.py:240
  84.8 2.4 %collective-permute-start.15 = (bf16[512,768]{1,0:T(8,128)(2,1)S(1)}, bf16[512,768]{1,0:T(8,128)(2,1)S(1)}, u32[]{:S(2)}, u32[]{:S(2)}) collective-permute-start(bf16[512,768]{1,0:T(8,128)(2,1)S(1)} %get-tuple-element.133.refs_0_), channel_id=1, source_target_pairs={{0,8},{1,9},{2,10},{3,11},{4,12},{5,13},{6,14},{7,15},{8,0},{9,1},... | collective-permute-start | bytes 2359304 | tf_op jit(solution)/shard_map/ppermute | solution.py:240
  85.0 3.3 %collective-permute-start.16 = (bf16[768,512]{1,0:T(8,128)(2,1)S(1)}, bf16[768,512]{1,0:T(8,128)(2,1)S(1)}, u32[]{:S(2)}, u32[]{:S(2)}) collective-permute-start(bf16[768,512]{1,0:T(8,128)(2,1)S(1)} %get-tuple-element.131.refs_2_), channel_id=1, source_target_pairs={{0,8},{1,9},{2,10},{3,11},{4,12},{5,13},{6,14},{7,15},{8,0},{9,1},... | collective-permute-start | bytes 2359304 | tf_op jit(solution)/shard_map/ppermute | solution.py:240
  95.5 18.5 %collective-permute-start.18 = (bf16[8,384,128]{2,1,0:T(8,128)(2,1)S(1)}, bf16[8,384,128]{2,1,0:T(8,128)(2,1)S(1)}, u32[]{:S(2)}, u32[]{:S(2)}) collective-permute-start(bf16[8,384,128]{2,1,0:T(8,128)(2,1)S(1)} %get-tuple-element.132), channel_id=1, source_target_pairs={{0,16},{1,17},{2,18},{3,19},{4,20},{5,21},{6,22},{7,23},{8,9},{9,8... | collective-permute-start | bytes 2359304 | tf_op jit(solution)/shard_map/ppermute | solution.py:240
  114.1 3.5 %collective-permute-start.19 = (bf16[1024,768]{1,0:T(8,128)(2,1)S(1)}, bf16[1024,768]{1,0:T(8,128)(2,1)S(1)}, u32[]{:S(2)}, u32[]{:S(2)}) collective-permute-start(bf16[1024,768]{1,0:T(8,128)(2,1)S(1)} %get-tuple-element.147), channel_id=1, source_target_pairs={{0,8},{1,9},{2,10},{3,11},{4,12},{5,13},{6,14},{7,15},{8,0},{9,1},... | collective-permute-start | bytes 4718600 | tf_op jit(solution)/shard_map/ppermute | solution.py:240
  114.2 20.5 %collective-permute-start.21 = (bf16[8,768,128]{2,1,0:T(8,128)(2,1)S(1)}, bf16[8,768,128]{2,1,0:T(8,128)(2,1)S(1)}, u32[]{:S(2)}, u32[]{:S(2)}) collective-permute-start(bf16[8,768,128]{2,1,0:T(8,128)(2,1)S(1)} %get-tuple-element.141), channel_id=1, source_target_pairs={{0,16},{1,17},{2,18},{3,19},{4,20},{5,21},{6,22},{7,23},{8,9},{9,8... | collective-permute-start | bytes 4718600 | tf_op jit(solution)/shard_map/ppermute | solution.py:240
  121.5 9.2 %collective-permute-start.20 = (bf16[16,144,128]{2,1,0:T(8,128)(2,1)S(1)}, bf16[16,144,128]{2,1,0:T(8,128)(2,1)S(1)}, u32[]{:S(2)}, u32[]{:S(2)}) collective-permute-start(bf16[16,144,128]{2,1,0:T(8,128)(2,1)S(1)} %get-tuple-element.155), channel_id=1, source_target_pairs={{0,8},{1,9},{2,10},{3,11},{4,12},{5,13},{6,14},{7,15},{8,0},{9,1},... | collective-permute-start | bytes 1769480 | tf_op jit(solution)/shard_map/ppermute | solution.py:240
  130.9 11.8 %collective-permute-start.24 = (bf16[8,144,128]{2,1,0:T(8,128)(2,1)S(1)}, bf16[8,144,128]{2,1,0:T(8,128)(2,1)S(1)}, u32[]{:S(2)}, u32[]{:S(2)}) collective-permute-start(bf16[8,144,128]{2,1,0:T(8,128)(2,1)S(1)} %slice.364), channel_id=1, source_target_pairs={{0,16},{1,17},{2,18},{3,19},{4,20},{5,21},{6,22},{7,23},{8,9},{9,8... | collective-permute-start | bytes 884744 | tf_op jit(solution)/shard_map/ppermute | solution.py:240
  135.1 13.1 %collective-permute-start.22 = (bf16[4,768,128]{2,1,0:T(8,128)(2,1)S(1)}, bf16[4,768,128]{2,1,0:T(8,128)(2,1)S(1)}, u32[]{:S(2)}, u32[]{:S(2)}) collective-permute-start(bf16[4,768,128]{2,1,0:T(8,128)(2,1)S(1)} %get-tuple-element.202), channel_id=1, source_target_pairs={{0,1},{1,0},{2,3},{3,2},{4,5},{5,4},{6,7},{7,6},{8,24},{9,25},{10,... | collective-permute-start | bytes 2359304 | tf_op jit(solution)/shard_map/ppermute | solution.py:240
  136.3 7.6 %collective-permute-start.23 = (bf16[16,24,1536]{2,1,0:T(8,128)(2,1)S(1)}, bf16[16,24,1536]{2,1,0:T(8,128)(2,1)S(1)}, u32[]{:S(2)}, u32[]{:S(2)}) collective-permute-start(bf16[16,24,1536]{2,1,0:T(8,128)(2,1)S(1)} %bitcast.51), channel_id=1, source_target_pairs={{0,8},{1,9},{2,10},{3,11},{4,12},{5,13},{6,14},{7,15},{8,0},{9,1},... | collective-permute-start | bytes 3538952 | tf_op jit(solution)/shard_map/ppermute | solution.py:240
  142.0 12.6 %collective-permute-start.28 = (bf16[16,24,896]{2,1,0:T(8,128)(2,1)S(1)}, bf16[16,24,896]{2,1,0:T(8,128)(2,1)S(1)}, u32[]{:S(2)}, u32[]{:S(2)}) collective-permute-start(bf16[16,24,896]{2,1,0:T(8,128)(2,1)S(1)} %bitcast.56), channel_id=1, source_target_pairs={{0,8},{1,9},{2,10},{3,11},{4,12},{5,13},{6,14},{7,15},{8,0},{9,1},... | collective-permute-start | bytes 2064392 | tf_op jit(solution)/shard_map/ppermute | solution.py:240
  142.9 16.9 %collective-permute-start.27 = (bf16[4,528,128]{2,1,0:T(8,128)(2,1)S(1)}, bf16[4,528,128]{2,1,0:T(8,128)(2,1)S(1)}, u32[]{:S(2)}, u32[]{:S(2)}) collective-permute-start(bf16[4,528,128]{2,1,0:T(8,128)(2,1)S(1)} %pad_maximum_fusion), channel_id=1, source_target_pairs={{0,1},{1,0},{2,3},{3,2},{4,5},{5,4},{6,7},{7,6},{8,24},{9,25},{10,... | collective-permute-start | bytes 1622024 | tf_op jit(solution)/shard_map/ppermute | solution.py:240
  144.2 19.8 %collective-permute-start.25 = (bf16[8,24,1536]{2,1,0:T(8,128)(2,1)S(1)}, bf16[8,24,1536]{2,1,0:T(8,128)(2,1)S(1)}, u32[]{:S(2)}, u32[]{:S(2)}) collective-permute-start(bf16[8,24,1536]{2,1,0:T(8,128)(2,1)S(1)} %get-tuple-element.210), channel_id=1, source_target_pairs={{0,16},{1,17},{2,18},{3,19},{4,20},{5,21},{6,22},{7,23},{8,9},{9,8... | collective-permute-start | bytes 1769480 | tf_op jit(solution)/shard_map/ppermute | solution.py:240
  148.4 13.8 %collective-permute-start.26 = (bf16[2,768,128]{2,1,0:T(8,128)(2,1)S(1)}, bf16[2,768,128]{2,1,0:T(8,128)(2,1)S(1)}, u32[]{:S(2)}, u32[]{:S(2)}) collective-permute-start(bf16[2,768,128]{2,1,0:T(8,128)(2,1)S(1)} %get-tuple-element.206), channel_id=1, source_target_pairs={{0,2},{1,3},{2,0},{3,1},{4,6},{5,7},{6,4},{7,5},{8,10},{9,11},{10,... | collective-permute-start | bytes 1179656 | tf_op jit(solution)/shard_map/ppermute | solution.py:240
  154.8 10.2 %collective-permute-start.31 = (bf16[8,24,896]{2,1,0:T(8,128)(2,1)S(1)}, bf16[8,24,896]{2,1,0:T(8,128)(2,1)S(1)}, u32[]{:S(2)}, u32[]{:S(2)}) collective-permute-start(bf16[8,24,896]{2,1,0:T(8,128)(2,1)S(1)} %get-tuple-element.222), channel_id=1, source_target_pairs={{0,16},{1,17},{2,18},{3,19},{4,20},{5,21},{6,22},{7,23},{8,9},{9,8... | collective-permute-start | bytes 1032200 | tf_op jit(solution)/shard_map/ppermute | solution.py:240
  159.9 9.2 %collective-permute-start.30 = (bf16[2,528,128]{2,1,0:T(8,128)(2,1)S(1)}, bf16[2,528,128]{2,1,0:T(8,128)(2,1)S(1)}, u32[]{:S(2)}, u32[]{:S(2)}) collective-permute-start(bf16[2,528,128]{2,1,0:T(8,128)(2,1)S(1)} %get-tuple-element.214), channel_id=1, source_target_pairs={{0,2},{1,3},{2,0},{3,1},{4,6},{5,7},{6,4},{7,5},{8,10},{9,11},{10,... | collective-permute-start | bytes 811016 | tf_op jit(solution)/shard_map/ppermute | solution.py:240
  162.2 19.4 %collective-permute-start.38 = (bf16[1,768,128]{2,1,0:T(8,128)(2,1)S(1)}, bf16[1,768,128]{2,1,0:T(8,128)(2,1)S(1)}, u32[]{:S(2)}, u32[]{:S(2)}) collective-permute-start(bf16[1,768,128]{2,1,0:T(8,128)(2,1)S(1)} %add_convert_fusion.12), channel_id=1, source_target_pairs={{0,4},{1,5},{2,6},{3,7},{4,0},{5,1},{6,2},{7,3},{8,12},{9,13},{10,... | collective-permute-start | bytes 589832 | tf_op jit(solution)/shard_map/ppermute | solution.py:240
  164.2 7.5 %collective-permute-start.29 = (bf16[4,24,1536]{2,1,0:T(8,128)(2,1)S(1)}, bf16[4,24,1536]{2,1,0:T(8,128)(2,1)S(1)}, u32[]{:S(2)}, u32[]{:S(2)}) collective-permute-start(bf16[4,24,1536]{2,1,0:T(8,128)(2,1)S(1)} %get-tuple-element.207), channel_id=1, source_target_pairs={{0,1},{1,0},{2,3},{3,2},{4,5},{5,4},{6,7},{7,6},{8,24},{9,25},{10,... | collective-permute-start | bytes 884744 | tf_op jit(solution)/shard_map/ppermute | solution.py:240
  165.1 9.3 %collective-permute-start.33 = (bf16[4,24,896]{2,1,0:T(8,128)(2,1)S(1)}, bf16[4,24,896]{2,1,0:T(8,128)(2,1)S(1)}, u32[]{:S(2)}, u32[]{:S(2)}) collective-permute-start(bf16[4,24,896]{2,1,0:T(8,128)(2,1)S(1)} %get-tuple-element.220), channel_id=1, source_target_pairs={{0,1},{1,0},{2,3},{3,2},{4,5},{5,4},{6,7},{7,6},{8,24},{9,25},{10,... | collective-permute-start | bytes 516104 | tf_op jit(solution)/shard_map/ppermute | solution.py:240
  169.1 12.6 %collective-permute-start.37 = (bf16[1,528,128]{2,1,0:T(8,128)(2,1)S(1)}, bf16[1,528,128]{2,1,0:T(8,128)(2,1)S(1)}, u32[]{:S(2)}, u32[]{:S(2)}) collective-permute-start(bf16[1,528,128]{2,1,0:T(8,128)(2,1)S(1)} %add_convert_fusion.20), channel_id=1, source_target_pairs={{0,4},{1,5},{2,6},{3,7},{4,0},{5,1},{6,2},{7,3},{8,12},{9,13},{10,... | collective-permute-start | bytes 405512 | tf_op jit(solution)/shard_map/ppermute | solution.py:240
  171.8 6.8 %collective-permute-start.32 = (bf16[2,24,1536]{2,1,0:T(8,128)(2,1)S(1)}, bf16[2,24,1536]{2,1,0:T(8,128)(2,1)S(1)}, u32[]{:S(2)}, u32[]{:S(2)}) collective-permute-start(bf16[2,24,1536]{2,1,0:T(8,128)(2,1)S(1)} %get-tuple-element.227), channel_id=1, source_target_pairs={{0,2},{1,3},{2,0},{3,1},{4,6},{5,7},{6,4},{7,5},{8,10},{9,11},{10,... | collective-permute-start | bytes 442376 | tf_op jit(solution)/shard_map/ppermute | solution.py:240
  174.4 5.7 %collective-permute-start.35 = (bf16[2,24,896]{2,1,0:T(8,128)(2,1)S(1)}, bf16[2,24,896]{2,1,0:T(8,128)(2,1)S(1)}, u32[]{:S(2)}, u32[]{:S(2)}) collective-permute-start(bf16[2,24,896]{2,1,0:T(8,128)(2,1)S(1)} %get-tuple-element.241), channel_id=1, source_target_pairs={{0,2},{1,3},{2,0},{3,1},{4,6},{5,7},{6,4},{7,5},{8,10},{9,11},{10,... | collective-permute-start | bytes 258056 | tf_op jit(solution)/shard_map/ppermute | solution.py:240
  178.6 8.2 %collective-permute-start.34 = (bf16[1,24,1536]{2,1,0:T(8,128)(2,1)S(1)}, bf16[1,24,1536]{2,1,0:T(8,128)(2,1)S(1)}, u32[]{:S(2)}, u32[]{:S(2)}) collective-permute-start(bf16[1,24,1536]{2,1,0:T(8,128)(2,1)S(1)} %add_convert_fusion.23), channel_id=1, source_target_pairs={{0,4},{1,5},{2,6},{3,7},{4,0},{5,1},{6,2},{7,3},{8,12},{9,13},{10,... | collective-permute-start | bytes 221192 | tf_op jit(solution)/shard_map/ppermute | solution.py:240
  180.2 5.4 %collective-permute-start.36 = (bf16[1,24,896]{2,1,0:T(8,128)(2,1)S(1)}, bf16[1,24,896]{2,1,0:T(8,128)(2,1)S(1)}, u32[]{:S(2)}, u32[]{:S(2)}) collective-permute-start(bf16[1,24,896]{2,1,0:T(8,128)(2,1)S(1)} %add_convert_fusion.25), channel_id=1, source_target_pairs={{0,4},{1,5},{2,6},{3,7},{4,0},{5,1},{6,2},{7,3},{8,12},{9,13},{10,... | collective-permute-start | bytes 129032 | tf_op jit(solution)/shard_map/ppermute | solution.py:240
  181.8 5.1 %copy-start.5 = (bf16[24,2304]{1,0:T(8,128)(2,1)S(1)}, bf16[24,2304]{1,0:T(8,128)(2,1)}, u32[]{:S(2)}) copy-start(bf16[24,2304]{1,0:T(8,128)(2,1)} %param.13) | copy-start | bytes 331780
  181.8 5.2 %copy-start.7 = (bf16[24]{0:T(256)(128)(2,1)S(1)}, bf16[24]{0:T(256)(128)(2,1)}, u32[]{:S(2)}) copy-start(bf16[24]{0:T(256)(128)(2,1)} %param.16) | copy-start | bytes 148
  182.6 5.0 %collective-permute-start.39 = (f32[576,128]{1,0:T(8,128)S(1)}, f32[576,128]{1,0:T(8,128)S(1)}, u32[]{:S(2)}, u32[]{:S(2)}) collective-permute-start(f32[576,128]{1,0:T(8,128)S(1)} %pad_maximum_fusion.2), channel_id=1, source_target_pairs={{0,8},{1,9},{2,10},{3,11},{4,12},{5,13},{6,14},{7,15},{8,0},{9,1},... | collective-permute-start | bytes 884744 | tf_op jit(solution)/shard_map/ppermute | solution.py:240
  186.9 1.8 copy-start.6

commit v3 on v2

--- a/solution.py
+++ b/solution.py
@@ -691,8 +691,6 @@
     qkv16 = join([qkv8, tie(qkv_second, a2, b4)])
     qkv_core = send(qkv16, over_core)
     b_first = send(tie(b4, qkv16), over_first)
-    a4 = join([a2, tie(a_near, qkv_core)])
-    a_first = send(a4, over_first)
 
     lane_block = pl.BlockSpec((seq, LANES), lambda j, m: (0, j))
     half_block = pl.BlockSpec((16, rows, LANES), lambda j, m: (0, 0, j))
@@ -706,14 +704,15 @@
         [shape((seq, wide), BF), shape((seq, wide), BF), shape((width, wide), BF), shape((32, rows, seq), BF),
          shape((8, wide), F32), shape((8, width), F32)],
         [pltpu.VMEM((seq, width), BF)], busy=7, name="project",
-    )(meta, tie(x, a4), qkv16, qkv_core, qkv16, qkv_core)
-
+    )(meta, tie(x, a2, b4), qkv16, qkv_core, qkv16, qkv_core)
+
+    a4 = join([a2, tie(a_near, mixed)])
+    a_first = send(a4, over_first)
     b8 = join([b4, tie(b_first, mixed)])
     b_second = send(b8, over_second)
     part_specs = [pl.BlockSpec((seq, LANES), lambda j, m, p=p: (0, p * groups + j)) for p in range(3)]
     lse_spec = pl.BlockSpec((1, 8, seq), lambda j, m: (j, 0, 0))
-    a8 = join([a4, tie(a_first, mixed)])
-    ready = tie(mixed, b8, a8, go_other, got_other)
+    ready = tie(mixed, b8, a4, go_other, got_other)
     attended, lse = call(
         attend_kernel, (groups,), part_specs, [lane_block, lse_spec],
         [shape((seq, width), BF), shape((groups, 8, seq), F32)], [pltpu.VMEM((LANES, seq), F32)],
@@ -723,6 +722,7 @@
     b16 = join([b8, tie(b_second, attended)])
     out16 = b16[:, half:, :]
     out_core = send(out16, over_core)
+    a8 = join([a4, tie(a_first, attended)])
     a_second = send(tie(a8, b16), over_second)
     residual, normed_two, normed_two_t, attended_t, out_full = call(
         mend_kernel, (1,),

time: 190 us -> 191 us (level)
  waiting for transfers between devices: 69.3 us -> 71.4 us
    ppermute x40, waiting for transfers between devices: 69.3 us -> 71.4 us  [send(): return lax.ppermute(array, AXES, flip_pairs(rule))]
  transfers between devices with their start and end apart: 40 -> 40, of which waited for: 18 -> 19; matrix products, arithmetic and copies ran while one was open for 4% -> 4% of each run, Pallas kernels for 34% -> 34%
where the time goes in v3:
time: 191 us; the launch traced here: 190 us
  waiting for transfers between devices  71.4 us (37%)
  Pallas kernels  65 us (34%)
  starting transfers between devices  38.4 us (20%)
  local copies, waits for them, and re-layouts  7.49 us (4%)
  other arithmetic  6.01 us (3%)
    ppermute x40, waiting for transfers between devices, send(): return lax.ppermute(array, AXES, flip_pairs(rule))  71.4 us
    ppermute x40, starting transfers between devices, send(): return lax.ppermute(array, AXES, flip_pairs(rule))  38.4 us
    pallas_call x2, Pallas kernels, attend_back(): call(attend_back_kernel, (count,), specs * 2 + tap_specs + [specs[0]] * 2...  13.5 us
    pallas_call x1, Pallas kernels, own_sequence(): call(functools.partial(ffn_kernel, False), (4,), sequence_specs + [tile(w...  12.8 us
    pallas_call x1, Pallas kernels, own_sequence(): call(attend_kernel, (groups,), part_specs, [lane_block, lse_spec], [shape...  9.19 us
    pallas_call x1, Pallas kernels, own_sequence(): call(functools.partial(ffn_kernel, True), (2,), sequence_specs + [tile(ha...  7.29 us
    pallas_call x1, Pallas kernels, own_sequence(): call(project_kernel, (wide // LANES,), [token, half_block, half_block, fe...  7.21 us
    unnamed x34, local copies, waits for them, and re-layouts  5.51 us
  transfers between devices with their start and end apart: 40, of which 19 were waited for; matrix products, arithmetic and copies ran while one was open for 4% of the time, Pallas kernels for 34%

profile of v3, /device:TPU:0, one launch (start us, length us, event | category | flops | bytes accessed | tf_op | source)
XLA Modules:
  0.0 190.2 jit_solution(18025004383057148694)
XLA Ops:
  1.3 1.0 fusion.22
  2.3 4.1 %collective-permute-start = (bf16[1,24,2432]{2,1,0:T(8,128)(2,1)S(1)}, bf16[1,24,2432]{2,1,0:T(8,128)(2,1)S(1)}, u32[]{:S(2)}, u32[]{:S(2)}) collective-permute-start(bf16[1,24,2432]{2,1,0:T(8,128)(2,1)S(1)} %fusion.22), channel_id=1, source_target_pairs={{0,4},{1,5},{2,6},{3,7},{4,0},{5,1},{6,2},{7,3},{8,12},{9,13},{10,... | collective-permute-start | bytes 350216 | tf_op jit(solution)/shard_map/ppermute | solution.py:240
  6.5 1.1 copy-done.2
  7.5 1.1 copy-done.3
  8.6 0.8 copy-done.4
  9.3 0.8 pack.1
  10.2 1.9 %collective-permute-done = bf16[1,24,2432]{2,1,0:T(8,128)(2,1)S(1)} collective-permute-done((bf16[1,24,2432]{2,1,0:T(8,128)(2,1)S(1)}, bf16[1,24,2432]{2,1,0:T(8,128)(2,1)S(1)}, u32[]{:S(2)}, u32[]{:S(2)}) %collective-permute-start) | collective-permute-done | bytes 116768 | tf_op jit(solution)/shard_map/ppermute | solution.py:240
  12.1 0.8 collective-permute-start.2
  13.0 6.1 %collective-permute-done.2 = bf16[2,24,2432]{2,1,0:T(8,128)(2,1)S(1)} collective-permute-done((bf16[2,24,2432]{2,1,0:T(8,128)(2,1)S(1)}, bf16[2,24,2432]{2,1,0:T(8,128)(2,1)S(1)}, u32[]{:S(2)}, u32[]{:S(2)}) %collective-permute-start.2) | collective-permute-done | bytes 233504 | tf_op jit(solution)/shard_map/ppermute | solution.py:240
  19.1 1.3 collective-permute-start.4
  20.5 3.3 %collective-permute-start.1 = (bf16[1,528,128]{2,1,0:T(8,128)(2,1)S(1)}, bf16[1,528,128]{2,1,0:T(8,128)(2,1)S(1)}, u32[]{:S(2)}, u32[]{:S(2)}) collective-permute-start(bf16[1,528,128]{2,1,0:T(8,128)(2,1)S(1)} %get-tuple-element.109), channel_id=1, source_target_pairs={{0,4},{1,5},{2,6},{3,7},{4,0},{5,1},{6,2},{7,3},{8,12},{9,13},{10,... | collective-permute-start | bytes 405512 | tf_op jit(solution)/shard_map/ppermute | solution.py:240
  23.9 5.8 %collective-permute-done.1 = bf16[1,528,128]{2,1,0:T(8,128)(2,1)S(1)} collective-permute-done((bf16[1,528,128]{2,1,0:T(8,128)(2,1)S(1)}, bf16[1,528,128]{2,1,0:T(8,128)(2,1)S(1)}, u32[]{:S(2)}, u32[]{:S(2)}) %collective-permute-start.1) | collective-permute-done | bytes 135200 | tf_op jit(solution)/shard_map/ppermute | solution.py:240
  29.9 0.6 collective-permute-start.6
  30.5 0.7 collective-permute-start.5
  31.2 3.4 %collective-permute-start.3 = (bf16[1,768,128]{2,1,0:T(8,128)(2,1)S(1)}, bf16[1,768,128]{2,1,0:T(8,128)(2,1)S(1)}, u32[]{:S(2)}, u32[]{:S(2)}) collective-permute-start(bf16[1,768,128]{2,1,0:T(8,128)(2,1)S(1)} %get-tuple-element.112), channel_id=1, source_target_pairs={{0,4},{1,5},{2,6},{3,7},{4,0},{5,1},{6,2},{7,3},{8,12},{9,13},{10,... | collective-permute-start | bytes 589832 | tf_op jit(solution)/shard_map/ppermute | solution.py:240
  34.6 7.5 %collective-permute-done.3 = bf16[1,768,128]{2,1,0:T(8,128)(2,1)S(1)} collective-permute-done((bf16[1,768,128]{2,1,0:T(8,128)(2,1)S(1)}, bf16[1,768,128]{2,1,0:T(8,128)(2,1)S(1)}, u32[]{:S(2)}, u32[]{:S(2)}) %collective-permute-start.3) | collective-permute-done | bytes 196640 | tf_op jit(solution)/shard_map/ppermute | solution.py:240
  42.1 1.3 collective-permute-done.5
  43.8 0.7 copy-done
  44.6 0.8 prepare.1
  45.5 0.5 collective-permute-start.10
  46.0 2.8 %collective-permute-start.9 = (bf16[2,768,128]{2,1,0:T(8,128)(2,1)S(1)}, bf16[2,768,128]{2,1,0:T(8,128)(2,1)S(1)}, u32[]{:S(2)}, u32[]{:S(2)}) collective-permute-start(bf16[2,768,128]{2,1,0:T(8,128)(2,1)S(1)} %get-tuple-element.257), channel_id=1, source_target_pairs={{0,2},{1,3},{2,0},{3,1},{4,6},{5,7},{6,4},{7,5},{8,10},{9,11},{10,... | collective-permute-start | bytes 1179656 | tf_op jit(solution)/shard_map/ppermute | solution.py:240
  49.2 7.2 %project.1 = (bf16[512,2304]{1,0:T(8,128)(2,1)S(1)}, bf16[512,2304]{1,0:T(8,128)(2,1)S(1)}, bf16[768,2304]{1,0:T(8,128)(2,1)S(1)}, bf16[32,24,512]{2,1,0:T(8,128...) custom-call(s32[64]{0:T(128)S(1)} %compare_select_fusion.1.meta, bf16[512,768]{1,0:T(8,128)(2,1)S(1)} %bitcast.53, ...), custom_call_target="tpu_custom_call" | custom-call | flops 8049999872 | tf_op jit(solution)/shard_map/project/pallas_call | solution.py:699
  56.4 1.8 collective-permute-done.9
  58.8 0.4 collective-permute-start.16
  59.2 9.2 %attend.1 = (bf16[512,768]{1,0:T(8,128)(2,1)S(1)}, f32[3,8,512]{2,1,0:T(8,128)S(1)}) custom-call(s32[64]{0:T(128)S(1)} %compare_select_fusion.1.meta, bf16[512,2304]{1,0:T(8,128)(2,1)S(1)} %get-tuple-element.125.q_ref.k_ref.v_ref, bf16[512,2304]{1,0:T(8,128)(2,1)S(1)} %get-tuple-element.125.q_ref.k_ref.v_ref, ...), custom_call_target="tpu_custom_call" | custom-call | flops 10350000128 | tf_op jit(solution)/shard_map/attend/pallas_call | solution.py:716
  68.4 12.4 %collective-permute-done.12 = bf16[8,528,128]{2,1,0:T(8,128)(2,1)S(1)} collective-permute-done((bf16[8,528,128]{2,1,0:T(8,128)(2,1)S(1)}, bf16[8,528,128]{2,1,0:T(8,128)(2,1)S(1)}, u32[]{:S(2)}, u32[]{:S(2)}) %collective-permute-start.12) | collective-permute-done | bytes 1081376 | tf_op jit(solution)/shard_map/ppermute | solution.py:240
  81.6 1.5 collective-permute-done.13.other_ref
  83.1 2.2 %mend.1 = (f32[512,768]{1,0:T(8,128)S(1)}, bf16[512,768]{1,0:T(8,128)(2,1)S(1)}, bf16[768,512]{1,0:T(8,128)(2,1)S(1)}, bf16[32,24,512]{2,1,0:T(8,128)(2,1)S(1)}, bf16[768,768]{1,0:T(8,128)(2,1)S(1)}) custom-call(s32[64]{0:T(128)S(1)} %compare_select_fusion.1.meta, bf16[512,768]{1,0:T(8,128)(2,1)S(1)} %get-tuple-element.126.att_ref.out_ref, ...), custom_call_target="tpu_custom_call" | custom-call | flops 2875000064 | tf_op jit(solution)/shard_map/mend/pallas_call | solution.py:727
  86.0 1.7 collective-permute-done.14.refs_4_
  87.6 1.1 collective-permute-done.15.refs_6_
  88.8 7.3 %ffn.2 = (f32[512,768]{1,0:T(8,128)S(1)}, f32[512,768]{1,0:T(8,128)S(1)}, f32[512,768]{1,0:T(8,128)S(1)}, f32[512,768]{1,0:T(8,128)S(1)}, bf16[8,384,128]{2,1,0:...) custom-call(s32[64]{0:T(128)S(1)} %compare_select_fusion.1.meta, bf16[512,768]{1,0:T(8,128)(2,1)S(1)} %get-tuple-element.132.refs_0_, ...), custom_call_target="tpu_custom_call" | custom-call | flops 2300000000 | tf_op jit(solution)/shard_map/ffn/pallas_call | solution.py:748
  96.4 5.4 %collective-permute-done.17 = bf16[8,768,128]{2,1,0:T(8,128)(2,1)S(1)} collective-permute-done((bf16[8,768,128]{2,1,0:T(8,128)(2,1)S(1)}, bf16[8,768,128]{2,1,0:T(8,128)(2,1)S(1)}, u32[]{:S(2)}, u32[]{:S(2)}) %collective-permute-start.17) | collective-permute-done | bytes 1572896 | tf_op jit(solution)/shard_map/ppermute | solution.py:240
  102.0 12.8 %ffn.3 = (f32[512,768]{1,0:T(8,128)S(1)}, f32[512,768]{1,0:T(8,128)S(1)}, bf16[1024,768]{1,0:T(8,128)(2,1)S(1)}, bf16[8,768,128]{2,1,0:T(8,128)(2,1)S(1)}, bf16[8,768,128]{2,1,0:T(8,128)(2,1)S(1)}) custom-call(s32[64]{0:T(128)S(1)} %compare_select_fusion.1.meta, bf16[512,768]{1,0:T(8,128)(2,1)S(1)} %get-tuple-element.132.refs_0_, ...), custom_call_target="tpu_custom_call" | custom-call | flops 17250000896 | tf_op jit(solution)/shard_map/ffn/pallas_call | solution.py:756
  115.4 2.8 %collective-permute-done.19.come_ref = bf16[1024,768]{1,0:T(8,128)(2,1)S(1)} collective-permute-done((bf16[1024,768]{1,0:T(8,128)(2,1)S(1)}, bf16[1024,768]{1,0:T(8,128)(2,1)S(1)}, u32[]{:S(2)}, u32[]{:S(2)}) %collective-permute-start.19) | collective-permute-done | bytes 1572896 | tf_op jit(solution)/shard_map/ppermute | solution.py:240
  118.2 4.0 %turn.1 = (bf16[512,768]{1,0:T(8,128)(2,1)}, f32[512,768]{1,0:T(8,128)S(1)}, bf16[512,768]{1,0:T(8,128)(2,1)S(1)}, f32[1,768]{1,0:T(1,128)S(1)}, bf16[16,144,128...) custom-call(s32[64]{0:T(128)S(1)} %compare_select_fusion.1.meta, f32[512,768]{1,0:T(8,128)S(1)} %get-tuple-element.145.grad_ref, ...), custom_call_target="tpu_custom_call" | custom-call | flops 4600000000 | tf_op jit(solution)/shard_map/turn/pallas_call | solution.py:768
  122.3 9.1 %attend_back.2 = (bf16[512,512]{1,0:T(8,128)(2,1)S(1)}, bf16[512,512]{1,0:T(8,128)(2,1)S(1)}, bf16[512,512]{1,0:T(8,128)(2,1)S(1)}, f32[8,512]{1,0:T(8,128)S(1)}...) custom-call(s32[64]{0:T(128)S(1)} %compare_select_fusion.1.meta, ...), custom_call_target="tpu_custom_call" | custom-call | flops 2300000000 | tf_op jit(solution)/shard_map/attend_back/pallas_call | solution.py:783
  132.0 1.9 %weight.2 = (bf16[384,1536]{1,0:T(8,128)(2,1)S(1)}, bf16[384,1536]{1,0:T(8,128)(2,1)S(1)}) custom-call(s32[64]{0:T(128)S(1)} %compare_select_fusion.1.meta, bf16[768,512]{1,0:T(8,128)(2,1)S(1)} %bitcast.57, bf16[512,512]{1,0:T(8,128)(2,1)S(1)} %get-tuple-element.158.refs_0_, bf16[512,512]{1,0:T(8,128)(2,1)S(1)} %get-tuple-element.163.refs_1_.refs_2_, ...), custom_call_target="tpu_custom_call" | custom-call | flops 1150000000 | tf_op jit(solution)/shard_map/weight/pallas_call | solution.py:795
  133.9 1.4 collective-permute-done.21
  135.7 1.6 collective-permute-start.22
  137.3 4.4 %attend_back.3 = (bf16[512,256]{1,0:T(8,128)(2,1)S(1)}, bf16[512,256]{1,0:T(8,128)(2,1)S(1)}, bf16[512,256]{1,0:T(8,128)(2,1)S(1)}, f32[8,256]{1,0:T(8,128)S(1)}...) custom-call(s32[64]{0:T(128)S(1)} %compare_select_fusion.1.meta, ...), custom_call_target="tpu_custom_call" | custom-call | flops 1150000000 | tf_op jit(solution)/shard_map/attend_back/pallas_call | solution.py:783
  141.8 1.3 weight.3
  143.1 0.6 collective-permute-start.28
  144.0 0.6 collective-permute-start.27
  145.3 3.2 %collective-permute-done.22 = bf16[4,768,128]{2,1,0:T(8,128)(2,1)S(1)} collective-permute-done((bf16[4,768,128]{2,1,0:T(8,128)(2,1)S(1)}, bf16[4,768,128]{2,1,0:T(8,128)(2,1)S(1)}, u32[]{:S(2)}, u32[]{:S(2)}) %collective-permute-start.22) | collective-permute-done | bytes 786464 | tf_op jit(solution)/shard_map/ppermute | solution.py:240
  148.7 1.4 collective-permute-start.26
  150.0 4.0 %last.1 = bf16[512,768]{1,0:T(8,128)(2,1)} custom-call(s32[64]{0:T(128)S(1)} %compare_select_fusion.1.meta, bf16[512,512]{1,0:T(8,128)(2,1)S(1)} %get-tuple-element.158.refs_0_, bf16[512,256]{1,0:T(8,128)(2,1)S(1)} %get-tuple-element.169.refs_7_.refs_1_, bf16[512,512]{1,0:T(8,128)(2,1)S(1)} %get-tuple-element.163.refs_1_.refs_2_, ...), custom_call_target="tpu_custom_call" | custom-call | flops 4600000000 | tf_op jit(solution)/shard_map/last/pallas_call | solution.py:828
  154.3 5.8 %collective-permute-done.27 = bf16[4,528,128]{2,1,0:T(8,128)(2,1)S(1)} collective-permute-done((bf16[4,528,128]{2,1,0:T(8,128)(2,1)S(1)}, bf16[4,528,128]{2,1,0:T(8,128)(2,1)S(1)}, u32[]{:S(2)}, u32[]{:S(2)}) %collective-permute-start.27) | collective-permute-done | bytes 540704 | tf_op jit(solution)/shard_map/ppermute | solution.py:240
  160.2 1.4 collective-permute-start.30
  161.6 2.9 %collective-permute-start.38 = (bf16[1,768,128]{2,1,0:T(8,128)(2,1)S(1)}, bf16[1,768,128]{2,1,0:T(8,128)(2,1)S(1)}, u32[]{:S(2)}, u32[]{:S(2)}) collective-permute-start(bf16[1,768,128]{2,1,0:T(8,128)(2,1)S(1)} %add_convert_fusion.12), channel_id=1, source_target_pairs={{0,4},{1,5},{2,6},{3,7},{4,0},{5,1},{6,2},{7,3},{8,12},{9,13},{10,... | collective-permute-start | bytes 589832 | tf_op jit(solution)/shard_map/ppermute | solution.py:240
  164.7 1.2 collective-permute-start.29
  166.0 1.0 collective-permute-start.33
  167.0 3.7 %collective-permute-done.30 = bf16[2,528,128]{2,1,0:T(8,128)(2,1)S(1)} collective-permute-done((bf16[2,528,128]{2,1,0:T(8,128)(2,1)S(1)}, bf16[2,528,128]{2,1,0:T(8,128)(2,1)S(1)}, u32[]{:S(2)}, u32[]{:S(2)}) %collective-permute-start.30) | collective-permute-done | bytes 270368 | tf_op jit(solution)/shard_map/ppermute | solution.py:240
  170.7 1.1 collective-permute-start.37
  172.0 2.5 %collective-permute-start.32 = (bf16[2,24,1536]{2,1,0:T(8,128)(2,1)S(1)}, bf16[2,24,1536]{2,1,0:T(8,128)(2,1)S(1)}, u32[]{:S(2)}, u32[]{:S(2)}) collective-permute-start(bf16[2,24,1536]{2,1,0:T(8,128)(2,1)S(1)} %get-tuple-element.225), channel_id=1, source_target_pairs={{0,2},{1,3},{2,0},{3,1},{4,6},{5,7},{6,4},{7,5},{8,10},{9,11},{10,... | collective-permute-start | bytes 442376 | tf_op jit(solution)/shard_map/ppermute | solution.py:240
  174.7 3.8 %collective-permute-done.32 = bf16[2,24,1536]{2,1,0:T(8,128)(2,1)S(1)} collective-permute-done((bf16[2,24,1536]{2,1,0:T(8,128)(2,1)S(1)}, bf16[2,24,1536]{2,1,0:T(8,128)(2,1)S(1)}, u32[]{:S(2)}, u32[]{:S(2)}) %collective-permute-start.32) | collective-permute-done | bytes 147488 | tf_op jit(solution)/shard_map/ppermute | solution.py:240
  178.4 2.1 %collective-permute-start.34 = (bf16[1,24,1536]{2,1,0:T(8,128)(2,1)S(1)}, bf16[1,24,1536]{2,1,0:T(8,128)(2,1)S(1)}, u32[]{:S(2)}, u32[]{:S(2)}) collective-permute-start(bf16[1,24,1536]{2,1,0:T(8,128)(2,1)S(1)} %add_convert_fusion.23), channel_id=1, source_target_pairs={{0,4},{1,5},{2,6},{3,7},{4,0},{5,1},{6,2},{7,3},{8,12},{9,13},{10,... | collective-permute-start | bytes 221192 | tf_op jit(solution)/shard_map/ppermute | solution.py:240
  180.9 0.6 collective-permute-start.36
  181.8 0.6 copy.23
  182.5 3.9 %collective-permute-done.36 = bf16[1,24,896]{2,1,0:T(8,128)(2,1)S(1)} collective-permute-done((bf16[1,24,896]{2,1,0:T(8,128)(2,1)S(1)}, bf16[1,24,896]{2,1,0:T(8,128)(2,1)S(1)}, u32[]{:S(2)}, u32[]{:S(2)}) %collective-permute-start.36) | collective-permute-done | bytes 43040 | tf_op jit(solution)/shard_map/ppermute | solution.py:240
  186.3 0.6 slice_bitcast_fusion
  186.9 0.5 slice_bitcast_fusion.1
  187.7 0.5 convert_divide_fusion
  188.6 0.8 maximum_bitcast_fusion
  189.4 0.8 pad_maximum_fusion.4
  (112 shorter events, 9.0 us)
Async XLA Ops:
  2.3 9.8 %collective-permute-start = (bf16[1,24,2432]{2,1,0:T(8,128)(2,1)S(1)}, bf16[1,24,2432]{2,1,0:T(8,128)(2,1)S(1)}, u32[]{:S(2)}, u32[]{:S(2)}) collective-permute-start(bf16[1,24,2432]{2,1,0:T(8,128)(2,1)S(1)} %fusion.22), channel_id=1, source_target_pairs={{0,4},{1,5},{2,6},{3,7},{4,0},{5,1},{6,2},{7,3},{8,12},{9,13},{10,... | collective-permute-start | bytes 350216 | tf_op jit(solution)/shard_map/ppermute | solution.py:240
  6.4 1.1 copy-start.2
  7.5 1.1 copy-start.3
  8.6 0.8 copy-start.4
  12.1 6.9 %collective-permute-start.2 = (bf16[2,24,2432]{2,1,0:T(8,128)(2,1)S(1)}, bf16[2,24,2432]{2,1,0:T(8,128)(2,1)S(1)}, u32[]{:S(2)}, u32[]{:S(2)}) collective-permute-start(bf16[2,24,2432]{2,1,0:T(8,128)(2,1)S(1)} %pad_maximum_fusion.6), channel_id=1, source_target_pairs={{0,2},{1,3},{2,0},{3,1},{4,6},{5,7},{6,4},{7,5},{8,10},{9,11},{10,... | collective-permute-start | bytes 700424 | tf_op jit(solution)/shard_map/ppermute | solution.py:240
  19.1 10.6 %collective-permute-start.4 = (bf16[4,24,2432]{2,1,0:T(8,128)(2,1)S(1)}, bf16[4,24,2432]{2,1,0:T(8,128)(2,1)S(1)}, u32[]{:S(2)}, u32[]{:S(2)}) collective-permute-start(bf16[4,24,2432]{2,1,0:T(8,128)(2,1)S(1)} %get-tuple-element.254), channel_id=1, source_target_pairs={{0,1},{1,0},{2,3},{3,2},{4,5},{5,4},{6,7},{7,6},{8,24},{9,25},{10,... | collective-permute-start | bytes 1400840 | tf_op jit(solution)/shard_map/ppermute | solution.py:240
  20.5 9.2 %collective-permute-start.1 = (bf16[1,528,128]{2,1,0:T(8,128)(2,1)S(1)}, bf16[1,528,128]{2,1,0:T(8,128)(2,1)S(1)}, u32[]{:S(2)}, u32[]{:S(2)}) collective-permute-start(bf16[1,528,128]{2,1,0:T(8,128)(2,1)S(1)} %get-tuple-element.109), channel_id=1, source_target_pairs={{0,4},{1,5},{2,6},{3,7},{4,0},{5,1},{6,2},{7,3},{8,12},{9,13},{10,... | collective-permute-start | bytes 405512 | tf_op jit(solution)/shard_map/ppermute | solution.py:240
  29.9 13.7 %collective-permute-start.6 = (bf16[8,24,2432]{2,1,0:T(8,128)(2,1)S(1)}, bf16[8,24,2432]{2,1,0:T(8,128)(2,1)S(1)}, u32[]{:S(2)}, u32[]{:S(2)}) collective-permute-start(bf16[8,24,2432]{2,1,0:T(8,128)(2,1)S(1)} %get-tuple-element.230), channel_id=1, source_target_pairs={{0,16},{1,17},{2,18},{3,19},{4,20},{5,21},{6,22},{7,23},{8,9},{9,8... | collective-permute-start | bytes 2801672 | tf_op jit(solution)/shard_map/ppermute | solution.py:240
  30.5 12.9 %collective-permute-start.5 = (bf16[2,528,128]{2,1,0:T(8,128)(2,1)S(1)}, bf16[2,528,128]{2,1,0:T(8,128)(2,1)S(1)}, u32[]{:S(2)}, u32[]{:S(2)}) collective-permute-start(bf16[2,528,128]{2,1,0:T(8,128)(2,1)S(1)} %get-tuple-element.264), channel_id=1, source_target_pairs={{0,2},{1,3},{2,0},{3,1},{4,6},{5,7},{6,4},{7,5},{8,10},{9,11},{10,... | collective-permute-start | bytes 811016 | tf_op jit(solution)/shard_map/ppermute | solution.py:240
  31.2 10.9 %collective-permute-start.3 = (bf16[1,768,128]{2,1,0:T(8,128)(2,1)S(1)}, bf16[1,768,128]{2,1,0:T(8,128)(2,1)S(1)}, u32[]{:S(2)}, u32[]{:S(2)}) collective-permute-start(bf16[1,768,128]{2,1,0:T(8,128)(2,1)S(1)} %get-tuple-element.112), channel_id=1, source_target_pairs={{0,4},{1,5},{2,6},{3,7},{4,0},{5,1},{6,2},{7,3},{8,12},{9,13},{10,... | collective-permute-start | bytes 589832 | tf_op jit(solution)/shard_map/ppermute | solution.py:240
  43.4 1.1 copy-start
  43.7 5.4 %collective-permute-start.7 = (bf16[16,24,2432]{2,1,0:T(8,128)(2,1)S(1)}, bf16[16,24,2432]{2,1,0:T(8,128)(2,1)S(1)}, u32[]{:S(2)}, u32[]{:S(2)}) collective-permute-start(bf16[16,24,2432]{2,1,0:T(8,128)(2,1)S(1)} %constant_dynamic-update-slice_fusion.14.own_ref.few_own_ref), channel_id=1, source_target_pairs={{0,8},{1,9},{2,10},{3,11},{4,12},{5,13},{6,14},{7,15},{8,0},{9,1},... | collective-permute-start | bytes 5603336 | tf_op jit(solution)/shard_map/ppermute | solution.py:240
  44.6 4.6 %copy-start.1 = (bf16[1,512,768]{2,1,0:T(8,128)(2,1)S(1)}, bf16[1,512,768]{2,1,0:T(8,128)(2,1)}, u32[]{:S(2)}) copy-start(bf16[1,512,768]{2,1,0:T(8,128)(2,1)} %param.10) | copy-start | bytes 2359300
  45.4 13.8 %collective-permute-start.11 = (bf16[768,512]{1,0:T(8,128)(2,1)S(1)}, bf16[768,512]{1,0:T(8,128)(2,1)S(1)}, u32[]{:S(2)}, u32[]{:S(2)}) collective-permute-start(bf16[768,512]{1,0:T(8,128)(2,1)S(1)} %get-tuple-element.124.refs_3_), channel_id=1, source_target_pairs={{0,8},{1,9},{2,10},{3,11},{4,12},{5,13},{6,14},{7,15},{8,0},{9,1},... | collective-permute-start | bytes 2359304 | tf_op jit(solution)/shard_map/ppermute | solution.py:240
  45.5 13.7 %collective-permute-start.10 = (bf16[512,768]{1,0:T(8,128)(2,1)S(1)}, bf16[512,768]{1,0:T(8,128)(2,1)S(1)}, u32[]{:S(2)}, u32[]{:S(2)}) collective-permute-start(bf16[512,768]{1,0:T(8,128)(2,1)S(1)} %get-tuple-element.123.refs_1_.go_ref), channel_id=1, source_target_pairs={{0,8},{1,9},{2,10},{3,11},{4,12},{5,13},{6,14},{7,15},{8,0},{9,1},... | collective-permute-start | bytes 2359304 | tf_op jit(solution)/shard_map/ppermute | solution.py:240
  46.0 12.2 %collective-permute-start.9 = (bf16[2,768,128]{2,1,0:T(8,128)(2,1)S(1)}, bf16[2,768,128]{2,1,0:T(8,128)(2,1)S(1)}, u32[]{:S(2)}, u32[]{:S(2)}) collective-permute-start(bf16[2,768,128]{2,1,0:T(8,128)(2,1)S(1)} %get-tuple-element.257), channel_id=1, source_target_pairs={{0,2},{1,3},{2,0},{3,1},{4,6},{5,7},{6,4},{7,5},{8,10},{9,11},{10,... | collective-permute-start | bytes 1179656 | tf_op jit(solution)/shard_map/ppermute | solution.py:240
  48.8 9.4 %collective-permute-start.8 = (bf16[4,528,128]{2,1,0:T(8,128)(2,1)S(1)}, bf16[4,528,128]{2,1,0:T(8,128)(2,1)S(1)}, u32[]{:S(2)}, u32[]{:S(2)}) collective-permute-start(bf16[4,528,128]{2,1,0:T(8,128)(2,1)S(1)} %get-tuple-element.119), channel_id=1, source_target_pairs={{0,1},{1,0},{2,3},{3,2},{4,5},{5,4},{6,7},{7,6},{8,24},{9,25},{10,... | collective-permute-start | bytes 1622024 | tf_op jit(solution)/shard_map/ppermute | solution.py:240
  58.4 22.5 %collective-permute-start.12 = (bf16[8,528,128]{2,1,0:T(8,128)(2,1)S(1)}, bf16[8,528,128]{2,1,0:T(8,128)(2,1)S(1)}, u32[]{:S(2)}, u32[]{:S(2)}) collective-permute-start(bf16[8,528,128]{2,1,0:T(8,128)(2,1)S(1)} %get-tuple-element.228), channel_id=1, source_target_pairs={{0,16},{1,17},{2,18},{3,19},{4,20},{5,21},{6,22},{7,23},{8,9},{9,8... | collective-permute-start | bytes 3244040 | tf_op jit(solution)/shard_map/ppermute | solution.py:240
  58.8 22.3 %collective-permute-start.16 = (bf16[4,768,128]{2,1,0:T(8,128)(2,1)S(1)}, bf16[4,768,128]{2,1,0:T(8,128)(2,1)S(1)}, u32[]{:S(2)}, u32[]{:S(2)}) collective-permute-start(bf16[4,768,128]{2,1,0:T(8,128)(2,1)S(1)} %get-tuple-element.236), channel_id=1, source_target_pairs={{0,1},{1,0},{2,3},{3,2},{4,5},{5,4},{6,7},{7,6},{8,24},{9,25},{10,... | collective-permute-start | bytes 2359304 | tf_op jit(solution)/shard_map/ppermute | solution.py:240
  81.0 2.1 %collective-permute-start.13 = (bf16[16,144,128]{2,1,0:T(8,128)(2,1)S(1)}, bf16[16,144,128]{2,1,0:T(8,128)(2,1)S(1)}, u32[]{:S(2)}, u32[]{:S(2)}) collective-permute-start(bf16[16,144,128]{2,1,0:T(8,128)(2,1)S(1)} %slice.363.own_ref), channel_id=1, source_target_pairs={{0,8},{1,9},{2,10},{3,11},{4,12},{5,13},{6,14},{7,15},{8,0},{9,1},... | collective-permute-start | bytes 1769480 | tf_op jit(solution)/shard_map/ppermute | solution.py:240
  81.3 20.5 %collective-permute-start.17 = (bf16[8,768,128]{2,1,0:T(8,128)(2,1)S(1)}, bf16[8,768,128]{2,1,0:T(8,128)(2,1)S(1)}, u32[]{:S(2)}, u32[]{:S(2)}) collective-permute-start(bf16[8,768,128]{2,1,0:T(8,128)(2,1)S(1)} %pad_maximum_fusion), channel_id=1, source_target_pairs={{0,16},{1,17},{2,18},{3,19},{4,20},{5,21},{6,22},{7,23},{8,9},{9,8... | collective-permute-start | bytes 4718600 | tf_op jit(solution)/shard_map/ppermute | solution.py:240
  85.3 2.4 %collective-permute-start.14 = (bf16[512,768]{1,0:T(8,128)(2,1)S(1)}, bf16[512,768]{1,0:T(8,128)(2,1)S(1)}, u32[]{:S(2)}, u32[]{:S(2)}) collective-permute-start(bf16[512,768]{1,0:T(8,128)(2,1)S(1)} %get-tuple-element.132.refs_0_), channel_id=1, source_target_pairs={{0,8},{1,9},{2,10},{3,11},{4,12},{5,13},{6,14},{7,15},{8,0},{9,1},... | collective-permute-start | bytes 2359304 | tf_op jit(solution)/shard_map/ppermute | solution.py:240
  85.5 3.3 %collective-permute-start.15 = (bf16[768,512]{1,0:T(8,128)(2,1)S(1)}, bf16[768,512]{1,0:T(8,128)(2,1)S(1)}, u32[]{:S(2)}, u32[]{:S(2)}) collective-permute-start(bf16[768,512]{1,0:T(8,128)(2,1)S(1)} %get-tuple-element.130.refs_2_), channel_id=1, source_target_pairs={{0,8},{1,9},{2,10},{3,11},{4,12},{5,13},{6,14},{7,15},{8,0},{9,1},... | collective-permute-start | bytes 2359304 | tf_op jit(solution)/shard_map/ppermute | solution.py:240
  96.1 18.7 %collective-permute-start.18 = (bf16[8,384,128]{2,1,0:T(8,128)(2,1)S(1)}, bf16[8,384,128]{2,1,0:T(8,128)(2,1)S(1)}, u32[]{:S(2)}, u32[]{:S(2)}) collective-permute-start(bf16[8,384,128]{2,1,0:T(8,128)(2,1)S(1)} %get-tuple-element.131), channel_id=1, source_target_pairs={{0,16},{1,17},{2,18},{3,19},{4,20},{5,21},{6,22},{7,23},{8,9},{9,8... | collective-permute-start | bytes 2359304 | tf_op jit(solution)/shard_map/ppermute | solution.py:240
  114.8 3.5 %collective-permute-start.19 = (bf16[1024,768]{1,0:T(8,128)(2,1)S(1)}, bf16[1024,768]{1,0:T(8,128)(2,1)S(1)}, u32[]{:S(2)}, u32[]{:S(2)}) collective-permute-start(bf16[1024,768]{1,0:T(8,128)(2,1)S(1)} %get-tuple-element.147), channel_id=1, source_target_pairs={{0,8},{1,9},{2,10},{3,11},{4,12},{5,13},{6,14},{7,15},{8,0},{9,1},... | collective-permute-start | bytes 4718600 | tf_op jit(solution)/shard_map/ppermute | solution.py:240
  114.8 20.5 %collective-permute-start.21 = (bf16[8,768,128]{2,1,0:T(8,128)(2,1)S(1)}, bf16[8,768,128]{2,1,0:T(8,128)(2,1)S(1)}, u32[]{:S(2)}, u32[]{:S(2)}) collective-permute-start(bf16[8,768,128]{2,1,0:T(8,128)(2,1)S(1)} %get-tuple-element.141), channel_id=1, source_target_pairs={{0,16},{1,17},{2,18},{3,19},{4,20},{5,21},{6,22},{7,23},{8,9},{9,8... | collective-permute-start | bytes 4718600 | tf_op jit(solution)/shard_map/ppermute | solution.py:240
  122.2 9.2 %collective-permute-start.20 = (bf16[16,144,128]{2,1,0:T(8,128)(2,1)S(1)}, bf16[16,144,128]{2,1,0:T(8,128)(2,1)S(1)}, u32[]{:S(2)}, u32[]{:S(2)}) collective-permute-start(bf16[16,144,128]{2,1,0:T(8,128)(2,1)S(1)} %get-tuple-element.155), channel_id=1, source_target_pairs={{0,8},{1,9},{2,10},{3,11},{4,12},{5,13},{6,14},{7,15},{8,0},{9,1},... | collective-permute-start | bytes 1769480 | tf_op jit(solution)/shard_map/ppermute | solution.py:240
  131.6 12.2 %collective-permute-start.24 = (bf16[8,144,128]{2,1,0:T(8,128)(2,1)S(1)}, bf16[8,144,128]{2,1,0:T(8,128)(2,1)S(1)}, u32[]{:S(2)}, u32[]{:S(2)}) collective-permute-start(bf16[8,144,128]{2,1,0:T(8,128)(2,1)S(1)} %slice.364), channel_id=1, source_target_pairs={{0,16},{1,17},{2,18},{3,19},{4,20},{5,21},{6,22},{7,23},{8,9},{9,8... | collective-permute-start | bytes 884744 | tf_op jit(solution)/shard_map/ppermute | solution.py:240
  135.7 12.7 %collective-permute-start.22 = (bf16[4,768,128]{2,1,0:T(8,128)(2,1)S(1)}, bf16[4,768,128]{2,1,0:T(8,128)(2,1)S(1)}, u32[]{:S(2)}, u32[]{:S(2)}) collective-permute-start(bf16[4,768,128]{2,1,0:T(8,128)(2,1)S(1)} %get-tuple-element.202), channel_id=1, source_target_pairs={{0,1},{1,0},{2,3},{3,2},{4,5},{5,4},{6,7},{7,6},{8,24},{9,25},{10,... | collective-permute-start | bytes 2359304 | tf_op jit(solution)/shard_map/ppermute | solution.py:240
  137.3 7.2 %collective-permute-start.23 = (bf16[16,24,1536]{2,1,0:T(8,128)(2,1)S(1)}, bf16[16,24,1536]{2,1,0:T(8,128)(2,1)S(1)}, u32[]{:S(2)}, u32[]{:S(2)}) collective-permute-start(bf16[16,24,1536]{2,1,0:T(8,128)(2,1)S(1)} %bitcast.51), channel_id=1, source_target_pairs={{0,8},{1,9},{2,10},{3,11},{4,12},{5,13},{6,14},{7,15},{8,0},{9,1},... | collective-permute-start | bytes 3538952 | tf_op jit(solution)/shard_map/ppermute | solution.py:240
  143.1 10.9 %collective-permute-start.28 = (bf16[16,24,896]{2,1,0:T(8,128)(2,1)S(1)}, bf16[16,24,896]{2,1,0:T(8,128)(2,1)S(1)}, u32[]{:S(2)}, u32[]{:S(2)}) collective-permute-start(bf16[16,24,896]{2,1,0:T(8,128)(2,1)S(1)} %bitcast.56), channel_id=1, source_target_pairs={{0,8},{1,9},{2,10},{3,11},{4,12},{5,13},{6,14},{7,15},{8,0},{9,1},... | collective-permute-start | bytes 2064392 | tf_op jit(solution)/shard_map/ppermute | solution.py:240
  144.0 16.1 %collective-permute-start.27 = (bf16[4,528,128]{2,1,0:T(8,128)(2,1)S(1)}, bf16[4,528,128]{2,1,0:T(8,128)(2,1)S(1)}, u32[]{:S(2)}, u32[]{:S(2)}) collective-permute-start(bf16[4,528,128]{2,1,0:T(8,128)(2,1)S(1)} %pad_maximum_fusion.1), channel_id=1, source_target_pairs={{0,1},{1,0},{2,3},{3,2},{4,5},{5,4},{6,7},{7,6},{8,24},{9,25},{10,... | collective-permute-start | bytes 1622024 | tf_op jit(solution)/shard_map/ppermute | solution.py:240
  144.9 19.7 %collective-permute-start.25 = (bf16[8,24,1536]{2,1,0:T(8,128)(2,1)S(1)}, bf16[8,24,1536]{2,1,0:T(8,128)(2,1)S(1)}, u32[]{:S(2)}, u32[]{:S(2)}) collective-permute-start(bf16[8,24,1536]{2,1,0:T(8,128)(2,1)S(1)} %get-tuple-element.210), channel_id=1, source_target_pairs={{0,16},{1,17},{2,18},{3,19},{4,20},{5,21},{6,22},{7,23},{8,9},{9,8... | collective-permute-start | bytes 1769480 | tf_op jit(solution)/shard_map/ppermute | solution.py:240
  148.7 12.9 %collective-permute-start.26 = (bf16[2,768,128]{2,1,0:T(8,128)(2,1)S(1)}, bf16[2,768,128]{2,1,0:T(8,128)(2,1)S(1)}, u32[]{:S(2)}, u32[]{:S(2)}) collective-permute-start(bf16[2,768,128]{2,1,0:T(8,128)(2,1)S(1)} %get-tuple-element.206), channel_id=1, source_target_pairs={{0,2},{1,3},{2,0},{3,1},{4,6},{5,7},{6,4},{7,5},{8,10},{9,11},{10,... | collective-permute-start | bytes 1179656 | tf_op jit(solution)/shard_map/ppermute | solution.py:240
  154.2 11.7 %collective-permute-start.31 = (bf16[8,24,896]{2,1,0:T(8,128)(2,1)S(1)}, bf16[8,24,896]{2,1,0:T(8,128)(2,1)S(1)}, u32[]{:S(2)}, u32[]{:S(2)}) collective-permute-start(bf16[8,24,896]{2,1,0:T(8,128)(2,1)S(1)} %get-tuple-element.220), channel_id=1, source_target_pairs={{0,16},{1,17},{2,18},{3,19},{4,20},{5,21},{6,22},{7,23},{8,9},{9,8... | collective-permute-start | bytes 1032200 | tf_op jit(solution)/shard_map/ppermute | solution.py:240
  160.2 10.5 %collective-permute-start.30 = (bf16[2,528,128]{2,1,0:T(8,128)(2,1)S(1)}, bf16[2,528,128]{2,1,0:T(8,128)(2,1)S(1)}, u32[]{:S(2)}, u32[]{:S(2)}) collective-permute-start(bf16[2,528,128]{2,1,0:T(8,128)(2,1)S(1)} %get-tuple-element.214), channel_id=1, source_target_pairs={{0,2},{1,3},{2,0},{3,1},{4,6},{5,7},{6,4},{7,5},{8,10},{9,11},{10,... | collective-permute-start | bytes 811016 | tf_op jit(solution)/shard_map/ppermute | solution.py:240
  161.6 19.9 %collective-permute-start.38 = (bf16[1,768,128]{2,1,0:T(8,128)(2,1)S(1)}, bf16[1,768,128]{2,1,0:T(8,128)(2,1)S(1)}, u32[]{:S(2)}, u32[]{:S(2)}) collective-permute-start(bf16[1,768,128]{2,1,0:T(8,128)(2,1)S(1)} %add_convert_fusion.12), channel_id=1, source_target_pairs={{0,4},{1,5},{2,6},{3,7},{4,0},{5,1},{6,2},{7,3},{8,12},{9,13},{10,... | collective-permute-start | bytes 589832 | tf_op jit(solution)/shard_map/ppermute | solution.py:240
  164.7 7.2 %collective-permute-start.29 = (bf16[4,24,1536]{2,1,0:T(8,128)(2,1)S(1)}, bf16[4,24,1536]{2,1,0:T(8,128)(2,1)S(1)}, u32[]{:S(2)}, u32[]{:S(2)}) collective-permute-start(bf16[4,24,1536]{2,1,0:T(8,128)(2,1)S(1)} %get-tuple-element.207), channel_id=1, source_target_pairs={{0,1},{1,0},{2,3},{3,2},{4,5},{5,4},{6,7},{7,6},{8,24},{9,25},{10,... | collective-permute-start | bytes 884744 | tf_op jit(solution)/shard_map/ppermute | solution.py:240
  166.0 8.5 %collective-permute-start.33 = (bf16[4,24,896]{2,1,0:T(8,128)(2,1)S(1)}, bf16[4,24,896]{2,1,0:T(8,128)(2,1)S(1)}, u32[]{:S(2)}, u32[]{:S(2)}) collective-permute-start(bf16[4,24,896]{2,1,0:T(8,128)(2,1)S(1)} %get-tuple-element.218), channel_id=1, source_target_pairs={{0,1},{1,0},{2,3},{3,2},{4,5},{5,4},{6,7},{7,6},{8,24},{9,25},{10,... | collective-permute-start | bytes 516104 | tf_op jit(solution)/shard_map/ppermute | solution.py:240
  170.7 10.9 %collective-permute-start.37 = (bf16[1,528,128]{2,1,0:T(8,128)(2,1)S(1)}, bf16[1,528,128]{2,1,0:T(8,128)(2,1)S(1)}, u32[]{:S(2)}, u32[]{:S(2)}) collective-permute-start(bf16[1,528,128]{2,1,0:T(8,128)(2,1)S(1)} %add_convert_fusion.20), channel_id=1, source_target_pairs={{0,4},{1,5},{2,6},{3,7},{4,0},{5,1},{6,2},{7,3},{8,12},{9,13},{10,... | collective-permute-start | bytes 405512 | tf_op jit(solution)/shard_map/ppermute | solution.py:240
  172.0 6.5 %collective-permute-start.32 = (bf16[2,24,1536]{2,1,0:T(8,128)(2,1)S(1)}, bf16[2,24,1536]{2,1,0:T(8,128)(2,1)S(1)}, u32[]{:S(2)}, u32[]{:S(2)}) collective-permute-start(bf16[2,24,1536]{2,1,0:T(8,128)(2,1)S(1)} %get-tuple-element.225), channel_id=1, source_target_pairs={{0,2},{1,3},{2,0},{3,1},{4,6},{5,7},{6,4},{7,5},{8,10},{9,11},{10,... | collective-permute-start | bytes 442376 | tf_op jit(solution)/shard_map/ppermute | solution.py:240
  174.6 6.3 %collective-permute-start.35 = (bf16[2,24,896]{2,1,0:T(8,128)(2,1)S(1)}, bf16[2,24,896]{2,1,0:T(8,128)(2,1)S(1)}, u32[]{:S(2)}, u32[]{:S(2)}) collective-permute-start(bf16[2,24,896]{2,1,0:T(8,128)(2,1)S(1)} %get-tuple-element.238), channel_id=1, source_target_pairs={{0,2},{1,3},{2,0},{3,1},{4,6},{5,7},{6,4},{7,5},{8,10},{9,11},{10,... | collective-permute-start | bytes 258056 | tf_op jit(solution)/shard_map/ppermute | solution.py:240
  178.4 9.0 %collective-permute-start.34 = (bf16[1,24,1536]{2,1,0:T(8,128)(2,1)S(1)}, bf16[1,24,1536]{2,1,0:T(8,128)(2,1)S(1)}, u32[]{:S(2)}, u32[]{:S(2)}) collective-permute-start(bf16[1,24,1536]{2,1,0:T(8,128)(2,1)S(1)} %add_convert_fusion.23), channel_id=1, source_target_pairs={{0,4},{1,5},{2,6},{3,7},{4,0},{5,1},{6,2},{7,3},{8,12},{9,13},{10,... | collective-permute-start | bytes 221192 | tf_op jit(solution)/shard_map/ppermute | solution.py:240
  180.9 5.4 %collective-permute-start.36 = (bf16[1,24,896]{2,1,0:T(8,128)(2,1)S(1)}, bf16[1,24,896]{2,1,0:T(8,128)(2,1)S(1)}, u32[]{:S(2)}, u32[]{:S(2)}) collective-permute-start(bf16[1,24,896]{2,1,0:T(8,128)(2,1)S(1)} %add_convert_fusion.25), channel_id=1, source_target_pairs={{0,4},{1,5},{2,6},{3,7},{4,0},{5,1},{6,2},{7,3},{8,12},{9,13},{10,... | collective-permute-start | bytes 129032 | tf_op jit(solution)/shard_map/ppermute | solution.py:240
  181.7 5.9 %copy-start.5 = (bf16[24,2304]{1,0:T(8,128)(2,1)S(1)}, bf16[24,2304]{1,0:T(8,128)(2,1)}, u32[]{:S(2)}) copy-start(bf16[24,2304]{1,0:T(8,128)(2,1)} %param.13) | copy-start | bytes 331780
  181.7 6.0 %copy-start.7 = (bf16[24]{0:T(256)(128)(2,1)S(1)}, bf16[24]{0:T(256)(128)(2,1)}, u32[]{:S(2)}) copy-start(bf16[24]{0:T(256)(128)(2,1)} %param.16) | copy-start | bytes 148
  182.5 5.8 %collective-permute-start.39 = (f32[576,128]{1,0:T(8,128)S(1)}, f32[576,128]{1,0:T(8,128)S(1)}, u32[]{:S(2)}, u32[]{:S(2)}) collective-permute-start(f32[576,128]{1,0:T(8,128)S(1)} %pad_maximum_fusion.3), channel_id=1, source_target_pairs={{0,8},{1,9},{2,10},{3,11},{4,12},{5,13},{6,14},{7,15},{8,0},{9,1},... | collective-permute-start | bytes 884744 | tf_op jit(solution)/shard_map/ppermute | solution.py:240
  187.6 1.8 copy-start.6
